TPU v7x, 32 devices: a whole 2x2x4 slice. The times are simulated.
32 devices in a mesh: dp: 8 (over y, x, core), seq: 4 (over z).
Axes of the slice: x: 2, y: 2, z: 4, core: 2. Of those that a mesh axis runs over, the one named last changes fastest.
Arguments:
- hidden_in: bfloat16 [8, 1024, 768], P('dp', 'seq'), may hold values from -8 to 8, as said below
- encoder_in: bfloat16 [8, 1024, 768], P('dp', 'seq'), may hold values from -6 to 6
- prefix_len: int32 [8], P('dp'), may hold values from 102 to 512, as said below
- exit_flags: int32 [8, 1024], P('dp', 'seq'), may hold values 0 or 1
- target_ids: int32 [8, 1024], P('dp', 'seq'), may hold values from 0 to 32127
- out_cotangent: float32 [8, 1024, 768], P('dp', 'seq'), may hold values from -6 to 6
- self_gain: bfloat16 [768], P('dp'), may hold values from 0.5 to 1.5
- self_query: bfloat16 [768, 768], P('dp', 'seq'), may hold values from -0.4375 to 0.4375
- self_key: bfloat16 [768, 768], P('dp', 'seq'), may hold values from -0.21875 to 0.21875
- self_value: bfloat16 [768, 768], P('dp', 'seq'), may hold values from -0.21875 to 0.21875
- self_output: bfloat16 [768, 768], P('dp', 'seq'), may hold values from -0.875 to 0.875
- cross_gain: bfloat16 [768], P('dp'), may hold values from 0.5 to 1.5
- cross_query: bfloat16 [768, 768], P('dp', 'seq'), may hold values from -0.4375 to 0.4375
- cross_key: bfloat16 [768, 768], P('dp', 'seq'), may hold values from -0.21875 to 0.21875
- cross_value: bfloat16 [768, 768], P('dp', 'seq'), may hold values from -0.21875 to 0.21875
- cross_output: bfloat16 [768, 768], P('dp', 'seq'), may hold values from -0.875 to 0.875
- feed_gain: bfloat16 [768], P('dp'), may hold values from 0.5 to 1.5
- feed_gate: bfloat16 [768, 2048], P('dp', 'seq'), may hold values from -0.21875 to 0.21875
- feed_up: bfloat16 [768, 2048], P('dp', 'seq'), may hold values from -0.21875 to 0.21875
- feed_down: bfloat16 [2048, 768], P('dp', 'seq'), may hold values from -0.25 to 0.25
- exit_gain: bfloat16 [768], P('dp'), may hold values from 0.5 to 1.5
- embedding: bfloat16 [32128, 768], P('dp', 'seq'), may hold values from -0.21875 to 0.21875
Outputs:
- block_output: bfloat16 [8, 1024, 768], P('dp', 'seq')
- token_losses: float32 [8, 1024], P('dp', 'seq')
- hidden_grad: float32 [8, 1024, 768], P('dp', 'seq')
- encoder_grad: float32 [8, 1024, 768], P('dp', 'seq')
- self_gain_grad: float32 [768], P('dp')
- self_query_grad: float32 [768, 768], P('dp', 'seq')
- self_key_grad: float32 [768, 768], P('dp', 'seq')
- self_value_grad: float32 [768, 768], P('dp', 'seq')
- self_output_grad: float32 [768, 768], P('dp', 'seq')
- cross_gain_grad: float32 [768], P('dp')
- cross_query_grad: float32 [768, 768], P('dp', 'seq')
- cross_key_grad: float32 [768, 768], P('dp', 'seq')
- cross_value_grad: float32 [768, 768], P('dp', 'seq')
- cross_output_grad: float32 [768, 768], P('dp', 'seq')
- feed_gain_grad: float32 [768], P('dp')
- feed_gate_grad: float32 [768, 2048], P('dp', 'seq')
- feed_up_grad: float32 [768, 2048], P('dp', 'seq')
- feed_down_grad: float32 [2048, 768], P('dp', 'seq')
- exit_gain_grad: float32 [768], P('dp')
- embedding_grad: float32 [32128, 768], P('dp', 'seq')
Inputs may be any that keep to these rules, and one draw needn't show every extreme that they name: `prefix_len`: each sequence's prefix length; both the shortest and the longest allowed value occur in every draw. `hidden_in`: the layer's input.
All inputs are finite; a program needn't handle non-finite values. No bound on the sum of `exit_flags` on one device may be relied on, other than what follows from the above.
Results may differ from a plain program's by a relative error of at most 0.033.
Values may be sent and summed in bfloat16 or wider, within the bound.
No kernel may reach another device: no remote copies, remote signals or barrier semaphores. Data moves between devices by JAX's collectives and lax.ppermute only.
A program may use at most 320 MiB of HBM per device.

v0:
```python
import functools

import jax
import jax.numpy as jnp
from jax import lax
from jax.experimental import pallas as pl
from jax.experimental.layout import Layout, with_layout_constraint
from jax.experimental.pallas import tpu as pltpu
from jax.sharding import Mesh
from jax.sharding import PartitionSpec as P

HD = 64
GAIN_LANES = 128
TOKEN_ROWS = 256
LANES = 128

norm_eps = 1e-06
masked_score = -1000000000.0
dp = ("group", "part")


def contract(first_op, second_op, first_dim, second_dim):
    return lax.dot_general(
        first_op,
        second_op,
        (((first_dim,), (second_dim,)), ((), ())),
        preferred_element_type=jnp.float32,
    )


def rows_first(array):
    return with_layout_constraint(array, Layout(major_to_minor=tuple(range(array.ndim))))


def norm_columns(inputs, scaling):
    return (
        inputs
        * lax.rsqrt(jnp.mean(inputs * inputs, axis=0, keepdims=True) + norm_eps)
        * scaling[:, None]
    )


def norm_back(inputs, scaling, upstream):
    unused, pullback = jax.vjp(norm_columns, inputs, scaling)
    return pullback(upstream)


def gated_unit(gate_in, upward):
    return jax.nn.gelu(gate_in, approximate=True) * upward


def swap(pieces, axis):
    return lax.all_to_all(pieces, axis, 0, 0, tiled=True)


def relocate(block):
    size = lax.axis_size("seq")
    pairs = [
        ((group * size + part) * size + at, (group * size + at) * size + part)
        for group in range(lax.axis_size("group"))
        for part in range(size)
        for at in range(size)
    ]
    return lax.ppermute(block, ("group", "part", "seq"), pairs)


def move_kernel(*refs, moves, count):
    for source, taken, target, put in moves:
        refs[count + target][put] = refs[source][taken]


def move(arrays, shapes, moves):
    return pl.pallas_call(
        functools.partial(move_kernel, moves=moves, count=len(arrays)),
        out_shape=[jax.ShapeDtypeStruct(shape, jnp.bfloat16) for shape in shapes],
    )(*arrays)


def sum_kernel(terms_ref, *refs, pieces):
    for ref, low, high in zip(refs, pieces[:-1], pieces[1:]):
        total = terms_ref[0, :, low:high].astype(jnp.float32)
        for block in range(1, terms_ref.shape[0]):
            total += terms_ref[block, :, low:high].astype(jnp.float32)
        ref[...] = total


def edges(sizes):
    return [sum(sizes[:at]) for at in range(len(sizes) + 1)]


every = slice(None)


def exchange(shards, after):
    n_seq = lax.axis_size("seq")
    rows = shards[0].shape[0]
    sizes = [shard.shape[1] for shard in shards]
    starts = edges(sizes)
    moves = [
        (at, (every, every), 0, (block, every, slice(starts[at], starts[at + 1])))
        for at in range(len(shards))
        for block in range(n_seq)
    ]
    (copies,) = move(shards, [(n_seq, rows, starts[-1])], moves)
    copies, after = lax.optimization_barrier((copies, after))
    return swap(copies, "seq"), after


def fetch(parts, sizes, extra):
    n_seq, rows, unused = parts.shape
    starts = edges(sizes)
    moves = [
        (
            0,
            (block, every, slice(starts[at], starts[at + 1])),
            0,
            (every, slice(low, low + sizes[at])),
        )
        for at in range(len(sizes))
        for block in range(n_seq)
        for low in [n_seq * starts[at] + block * sizes[at]]
    ]
    width = n_seq * starts[-1]
    if extra is not None:
        moves.append((1, (every, every), 0, (every, slice(width, width + extra.shape[1]))))
        width += extra.shape[1]
    (full,) = move([parts] if extra is None else [parts, extra], [(rows, width)], moves)
    return lax.all_gather(full, dp, axis=0, tiled=True)


def deliver(terms, sizes, extra, out_sizes):
    n_seq = lax.axis_size("seq")
    rows = terms.shape[0]
    starts = edges(sizes)
    moves = [
        (
            0,
            (every, slice(low, low + sizes[at])),
            0,
            (block, every, slice(starts[at], starts[at + 1])),
        )
        for at in range(len(sizes))
        for block in range(n_seq)
        for low in [n_seq * starts[at] + block * sizes[at]]
    ]
    width = starts[-1]
    if extra:
        low = n_seq * width
        moves += [
            (0, (every, slice(low, low + extra)), 0, (block, every, slice(width, width + extra)))
            for block in range(n_seq)
        ]
    (parts,) = move([terms], [(n_seq, rows, width + extra)], moves)
    return pl.pallas_call(
        functools.partial(sum_kernel, pieces=edges(out_sizes)),
        out_shape=[jax.ShapeDtypeStruct((rows, size), jnp.float32) for size in out_sizes],
    )(swap(parts, "seq"))


def cut(array, sizes):
    return jnp.split(array, edges(sizes)[1:-1], axis=1)


def head_rows(row, head):
    return slice(row + head * HD, row + (head + 1) * HD)


def score_columns(key_ref, key_row, queries, head, allowed):
    scores = jnp.concatenate(
        [
            contract(key_ref[block, head_rows(key_row, head), :], queries, 0, 0)
            for block in range(key_ref.shape[0])
        ],
        axis=0,
    )
    if allowed is not None:
        scores = jnp.where(allowed, scores, masked_score)
    exponent = jnp.exp(scores - jnp.max(scores, axis=0, keepdims=True))
    return exponent * (1.0 / jnp.sum(exponent, axis=0, keepdims=True))


def allowed_columns(prefix_ref, step, blocks, rows):
    key_pos = lax.broadcasted_iota(jnp.int32, (blocks * rows, rows), 0)
    query_pos = step * rows + lax.broadcasted_iota(jnp.int32, (blocks * rows, rows), 1)
    return (key_pos <= query_pos) | (key_pos < prefix_ref[0])


def attend_kernel(prefix_ref, *refs, places, causal):
    out_ref = refs[-1]
    step = pl.program_id(0)
    (q_at, q_row), (k_at, k_row), (v_at, v_row) = places
    blocks, unused, rows = refs[k_at].shape
    allowed = allowed_columns(prefix_ref, step, blocks, rows) if causal else None
    for head in range(out_ref.shape[1] // HD):
        queries = refs[q_at][step, head_rows(q_row, head), :]
        queries = queries * jnp.asarray(HD**-0.5, queries.dtype)
        shares = score_columns(refs[k_at], k_row, queries, head, allowed).astype(queries.dtype)
        total = jnp.zeros(queries.shape, jnp.float32)
        for block in range(blocks):
            values = refs[v_at][block, head_rows(v_row, head), :]
            total += contract(values, shares[block * rows : (block + 1) * rows], 1, 0)
        out_ref[0, head_rows(0, head), :] = total.astype(out_ref.dtype)


def attend_back_kernel(prefix_ref, *refs, places, spots, count, causal):
    upstream_ref = refs[count]
    out_ref, key_sum, value_sum = refs[count + 1 :]
    step = pl.program_id(0)
    (q_at, q_row), (k_at, k_row), (v_at, v_row) = places
    blocks, unused, rows = refs[k_at].shape
    allowed = allowed_columns(prefix_ref, step, blocks, rows) if causal else None

    @pl.when(step == 0)
    def _():
        key_sum[...] = jnp.zeros_like(key_sum)
        value_sum[...] = jnp.zeros_like(value_sum)

    for head in range(upstream_ref.shape[1] // HD):
        mine = head_rows(0, head)
        queries = refs[q_at][step, head_rows(q_row, head), :]
        queries = queries * jnp.asarray(HD**-0.5, queries.dtype)
        upstream = upstream_ref[0, mine, :]
        shares = score_columns(refs[k_at], k_row, queries, head, allowed)
        share_grads = jnp.concatenate(
            [
                contract(refs[v_at][block, head_rows(v_row, head), :], upstream, 0, 0)
                for block in range(blocks)
            ],
            axis=0,
        )
        centre = jnp.sum(shares * share_grads, axis=0, keepdims=True)
        score_grads = (shares * (share_grads - centre)).astype(queries.dtype)
        shares = shares.astype(queries.dtype)
        total = jnp.zeros(queries.shape, jnp.float32)
        for block in range(blocks):
            part = slice(block * rows, (block + 1) * rows)
            key_rows = refs[k_at][block, head_rows(k_row, head), :]
            total += contract(key_rows, score_grads[part], 1, 0)
            key_sum[block, mine, :] += contract(queries, score_grads[part], 1, 1)
            value_sum[block, mine, :] += contract(upstream, shares[part], 1, 1)
        out_ref[step, head_rows(spots[0], head), :] = (total * HD**-0.5).astype(out_ref.dtype)

    @pl.when(step == pl.num_programs(0) - 1)
    def _():
        width = key_sum.shape[1]
        out_ref[:, spots[1] : spots[1] + width, :] = key_sum[...].astype(out_ref.dtype)
        out_ref[:, spots[2] : spots[2] + width, :] = value_sum[...].astype(out_ref.dtype)


def exit_kernel(token_ref, table_ref, shifted_ref, product_ref, part_ref, logit_ref, *, rows):
    lanes = table_ref.shape[1]
    chunk = next(size for size in (1024, 512, 256, 128) if lanes % size == 0)
    tokens = token_ref[...]
    row_max = jnp.full((tokens.shape[0], 1), -jnp.inf, jnp.float32)
    for low in range(0, lanes, chunk):
        logits = contract(tokens, table_ref[:, low : low + chunk], 1, 0)
        if low + chunk > rows:
            lane = low + lax.broadcasted_iota(jnp.int32, (1, chunk), 1)
            logits = jnp.where(lane < rows, logits, -jnp.inf)
        logit_ref[:, low : low + chunk] = logits
        row_max = jnp.maximum(row_max, jnp.max(logits, axis=1, keepdims=True))
    row_sum = jnp.zeros_like(row_max)
    product = jnp.zeros(product_ref.shape, jnp.float32)
    for low in range(0, lanes, chunk):
        shifted = jnp.exp(logit_ref[:, low : low + chunk] - row_max)
        row_sum += jnp.sum(shifted, axis=1, keepdims=True)
        shifted = shifted.astype(shifted_ref.dtype)
        shifted_ref[:, low : low + chunk] = shifted
        product += contract(shifted, table_ref[:, low : low + chunk], 1, 1)
    product_ref[...] = product
    lane = lax.broadcasted_iota(jnp.int32, part_ref.shape, 1)
    part_ref[...] = jnp.where(lane == 0, row_max, row_sum)


def exit_rows(tokens, table, rows):
    count, width = tokens.shape
    lanes = table.shape[1]
    step_rows = min(TOKEN_ROWS, count)
    return pl.pallas_call(
        functools.partial(exit_kernel, rows=rows),
        grid=(count // step_rows,),
        in_specs=[pl.BlockSpec((step_rows, width), lambda step: (step, 0)), whole(table)],
        out_specs=[
            pl.BlockSpec((step_rows, lanes), lambda step: (step, 0)),
            pl.BlockSpec((step_rows, width), lambda step: (step, 0)),
            pl.BlockSpec((step_rows, LANES), lambda step: (step, 0)),
        ],
        out_shape=[
            jax.ShapeDtypeStruct((count, lanes), jnp.bfloat16),
            jax.ShapeDtypeStruct((count, width), jnp.float32),
            jax.ShapeDtypeStruct((count, LANES), jnp.float32),
        ],
        scratch_shapes=[pltpu.VMEM((step_rows, lanes), jnp.float32)],
    )(tokens, table)


def whole(array):
    return pl.BlockSpec(array.shape, lambda step: (0,) * len(array.shape))


def attend(prefix, arrays, places, width, causal):
    blocks, unused, rows = arrays[0].shape
    return pl.pallas_call(
        functools.partial(attend_kernel, places=places, causal=causal),
        grid=(blocks,),
        in_specs=[pl.BlockSpec(memory_space=pltpu.SMEM)] + [whole(array) for array in arrays],
        out_specs=pl.BlockSpec((1, width, rows), lambda step: (step, 0, 0)),
        out_shape=jax.ShapeDtypeStruct((blocks, width, rows), jnp.bfloat16),
    )(prefix, *arrays)


def attend_back(prefix, arrays, upstream, places, causal):
    blocks, width, rows = upstream.shape
    shape = jax.ShapeDtypeStruct((blocks, 3 * width, rows), jnp.bfloat16)
    return pl.pallas_call(
        functools.partial(
            attend_back_kernel,
            places=places,
            spots=(0, width, 2 * width),
            count=len(arrays),
            causal=causal,
        ),
        grid=(blocks,),
        in_specs=[pl.BlockSpec(memory_space=pltpu.SMEM)]
        + [whole(array) for array in arrays]
        + [pl.BlockSpec((1, width, rows), lambda step: (step, 0, 0))],
        out_specs=whole(shape),
        out_shape=shape,
        scratch_shapes=[pltpu.VMEM((blocks, width, rows), jnp.float32)] * 2,
    )(prefix, *arrays, upstream)


def per_device(
    hidden_in,
    encoder_in,
    prefix_len,
    exit_flags,
    target_ids,
    out_cotangent,
    self_gain,
    self_query,
    self_key,
    self_value,
    self_output,
    cross_gain,
    cross_query,
    cross_key,
    cross_value,
    cross_output,
    feed_gain,
    feed_gate,
    feed_up,
    feed_down,
    exit_gain,
    embedding,
):
    width = hidden_in.shape[2]
    n_seq = lax.axis_size("seq")
    n_dp = lax.axis_size(dp)
    own_rows, own = self_query.shape
    own_feed = feed_gate.shape[1]
    fold_rows = feed_down.shape[0]
    folds = -(-fold_rows // own_rows)
    vocab_rows = embedding.shape[0]
    vocab_lanes = -(-vocab_rows // LANES) * LANES
    low = jnp.bfloat16

    gains = jnp.stack([self_gain, cross_gain, feed_gain, exit_gain], axis=1)
    gains = jnp.pad(gains, ((0, 0), (0, GAIN_LANES - gains.shape[1])))
    near_parts, moved = exchange(
        [
            jnp.concatenate([self_query, self_key, self_value], axis=1),
            self_output,
            cross_query,
            jnp.concatenate([cross_key, cross_value], axis=1),
            cross_output,
        ],
        (),
    )
    near_sizes = (3 * own, own, own, 2 * own, own)

    marks = jnp.concatenate(
        [exit_flags, target_ids, jnp.broadcast_to(prefix_len[:, None], exit_flags.shape)], axis=0
    )
    near_parts, marks, hidden_in, encoder_in = lax.optimization_barrier(
        (near_parts, marks, hidden_in, encoder_in)
    )
    near = fetch(near_parts, near_sizes, gains)
    self_qkv, self_out, cross_q, cross_kv, cross_out, gain_columns = cut(
        near, tuple(n_seq * size for size in near_sizes) + (GAIN_LANES,)
    )
    moved = (
        relocate(marks),
        relocate(hidden_in.reshape(-1, width)),
        relocate(encoder_in.reshape(-1, width)),
    )
    folded = jnp.pad(feed_down, ((0, folds * own_rows - fold_rows), (0, 0)))
    feed_parts, (marks, hidden, states) = exchange(
        [feed_gate, feed_up]
        + [folded[fold * own_rows : (fold + 1) * own_rows] for fold in range(folds)],
        moved,
    )
    feed_sizes = (own_feed, own_feed) + (own,) * folds
    prefix_len = marks[2, :1]
    marks = lax.all_gather(marks[:2], dp, axis=0)
    shard = jnp.pad(embedding.T, ((0, 0), (0, vocab_lanes - vocab_rows)))
    feed_parts, shard, marks = lax.optimization_barrier((feed_parts, shard, marks))
    feed = fetch(feed_parts, feed_sizes, None)
    gate_full, up_full, *downs = cut(feed, tuple(n_seq * size for size in feed_sizes))
    table = lax.all_gather(shard, "seq", axis=0, tiled=True)
    cotangent = relocate(out_cotangent.reshape(-1, width))
    gain_one, gain_two, gain_three, gain_exit = gain_columns[:, :4].astype(jnp.float32).T

    def blocks(rows):
        return rows.astype(low).reshape(n_seq, -1, rows.shape[1])

    def fold_up(rows):
        rows = rows.reshape(n_dp, fold_rows, -1)
        rows = jnp.pad(rows, ((0, 0), (0, folds * own_rows - fold_rows), (0, 0)))
        return [
            rows[:, fold * own_rows : (fold + 1) * own_rows].reshape(width, -1)
            for fold in range(folds)
        ]

    def unfold(parts):
        parts = [part.reshape(n_dp, own_rows, -1) for part in parts]
        rows = jnp.concatenate(parts, axis=1)[:, :fold_rows]
        return rows.reshape(n_dp * fold_rows, -1)

    residual_in = hidden.T.astype(jnp.float32)
    token_count = residual_in.shape[1]
    residual_in, states, marks = lax.optimization_barrier((residual_in, states.T, marks))
    residual_in, states = rows_first(residual_in), rows_first(states)
    cotangent = rows_first(cotangent.T)
    normed_one = norm_columns(residual_in, gain_one).astype(low)
    attended = swap(
        jnp.concatenate(
            [
                blocks(contract(self_qkv, normed_one, 0, 0)),
                blocks(contract(cross_kv, states, 0, 0)),
            ],
            axis=1,
        ),
        "part",
    )
    self_places = ((0, 0), (0, own), (0, 2 * own))
    mixture_one = swap(attend(prefix_len, [attended], self_places, own, True), "part")
    mixture_one = mixture_one.reshape(width, token_count)
    after_self = residual_in + contract(self_out, mixture_one, 0, 0)
    normed_two = norm_columns(after_self, gain_two).astype(low)
    q_two = swap(blocks(contract(cross_q, normed_two, 0, 0)), "part")
    cross_places = ((0, 0), (1, 3 * own), (1, 4 * own))
    mixture_two = swap(attend(prefix_len, [q_two, attended], cross_places, own, False), "part")
    mixture_two = mixture_two.reshape(width, token_count)
    after_cross = after_self + contract(cross_out, mixture_two, 0, 0)
    normed_three = norm_columns(after_cross, gain_three).astype(low)
    gate_pre = contract(gate_full, normed_three, 0, 0)
    up_pre = contract(up_full, normed_three, 0, 0)
    hidden_mid = gated_unit(gate_pre, up_pre).astype(low)
    hidden_folds = fold_up(hidden_mid)
    after_feed = after_cross
    for down, hidden in zip(downs, hidden_folds):
        after_feed = after_feed + contract(down, hidden, 0, 0)
    block_output = relocate(after_feed.T.astype(low)).reshape(hidden_in.shape)
    normed_exit = rows_first(norm_columns(after_feed, gain_exit).astype(low).T)
    normed_exit, table, cotangent = lax.optimization_barrier((normed_exit, table, cotangent))

    tokens = lax.all_gather(normed_exit, dp, axis=0, tiled=True)
    flag_rows = marks[:, 0].reshape(-1, 1).astype(jnp.float32)
    target_rows = marks[:, 1].reshape(-1, 1) - lax.axis_index(dp) * vocab_rows
    hits = jnp.arange(vocab_lanes)[None, :] == target_rows
    hits = hits & (target_rows < vocab_rows)
    target_terms = contract(hits.astype(low), table, 1, 1).astype(low)
    tokens, target_terms = lax.optimization_barrier((tokens, target_terms))
    shifted, products, parts = exit_rows(tokens, table, vocab_rows)
    picked = jnp.sum(tokens.astype(jnp.float32) * target_terms.astype(jnp.float32), axis=1)
    row_max = parts[:, 0]
    parts = lax.all_gather(jnp.stack([row_max, parts[:, 1], picked]), dp, axis=0)
    top = jnp.max(parts[:, 0], axis=0)
    log_total = top + jnp.log(jnp.sum(parts[:, 1] * jnp.exp(parts[:, 0] - top), axis=0))
    all_losses = flag_rows[:, 0] * (log_total - jnp.sum(parts[:, 2], axis=0))
    token_losses = lax.dynamic_slice(
        all_losses, (lax.axis_index(dp) * token_count,), (token_count,)
    )
    token_losses = relocate(token_losses.reshape(exit_flags.shape))
    factor = flag_rows * jnp.exp(row_max - log_total)[:, None]
    exit_in_grad = lax.psum_scatter(
        rows_first((factor * products - flag_rows * target_terms.astype(jnp.float32)).astype(low)),
        dp,
        scatter_dimension=0,
        tiled=True,
    )
    logit_grads = jnp.where(hits, factor * shifted - flag_rows, factor * shifted).astype(low)
    table_terms = contract(tokens, logit_grads, 0, 0).astype(low)
    exit_in_grad, table_terms, block_output, token_losses = lax.optimization_barrier(
        (rows_first(exit_in_grad), table_terms, block_output, token_losses)
    )
    exit_in_grad = rows_first(exit_in_grad.T).astype(jnp.float32)
    table_sums = lax.psum_scatter(table_terms, "seq", scatter_dimension=0, tiled=True)

    feed_grad, full_exit_gain = norm_back(after_feed, gain_exit, exit_in_grad)
    feed_grad = feed_grad + cotangent
    branch_three = feed_grad.astype(low)
    hidden_mid_grad = unfold([contract(down, branch_three, 1, 0) for down in downs])
    unused, gated_pull = jax.vjp(gated_unit, gate_pre, up_pre)
    gate_grad, up_grad = gated_pull(hidden_mid_grad)
    gate_grad, up_grad = gate_grad.astype(low), up_grad.astype(low)
    normed_three_grad = contract(gate_full, gate_grad, 1, 0) + contract(up_full, up_grad, 1, 0)
    cross_grad, full_feed_gain = norm_back(after_cross, gain_three, normed_three_grad)
    cross_grad = cross_grad + feed_grad
    branch_two = cross_grad.astype(low)
    mixture_two_grad = blocks(contract(cross_out, branch_two, 1, 0))
    cross_grads = attend_back(
        prefix_len, [q_two, attended], swap(mixture_two_grad, "part"), cross_places, False
    )
    cross_grads = swap(cross_grads, "part")
    q_grad = cross_grads[:, :own].reshape(-1, token_count)
    kv_grad = cross_grads[:, own:].reshape(-1, token_count)
    encoder_grad = relocate(contract(kv_grad, cross_kv, 0, 1)).reshape(encoder_in.shape)
    rest_terms = jnp.concatenate(
        [
            contract(normed_two, q_grad, 1, 1).astype(low),
            contract(states, kv_grad, 1, 1).astype(low),
            contract(mixture_two, branch_two, 1, 1).astype(low),
            contract(normed_three, gate_grad, 1, 1).astype(low),
            contract(normed_three, up_grad, 1, 1).astype(low),
        ]
        + [contract(hidden, branch_three, 1, 1).astype(low) for hidden in hidden_folds],
        axis=1,
    )
    self_grad, full_cross_gain = norm_back(after_self, gain_two, contract(cross_q, q_grad, 1, 0))
    self_grad = self_grad + cross_grad
    branch_one = self_grad.astype(low)
    mixture_one_grad = blocks(contract(self_out, branch_one, 1, 0))
    mixture_one_grad, rest_terms = lax.optimization_barrier((mixture_one_grad, rest_terms))
    rest_terms, table_sums = lax.optimization_barrier((rest_terms, table_sums))
    rest_terms = lax.psum_scatter(rest_terms, dp, scatter_dimension=0, tiled=True)
    qkv_grad = attend_back(
        prefix_len, [attended], swap(mixture_one_grad, "part"), self_places, True
    )
    qkv_grad, encoder_grad = lax.optimization_barrier((qkv_grad, encoder_grad))
    qkv_grad = swap(qkv_grad, "part").reshape(-1, token_count)
    normed_one_grad = contract(self_qkv, qkv_grad, 1, 0)
    input_grad, full_self_gain = norm_back(residual_in, gain_one, normed_one_grad)
    hidden_grad = relocate((input_grad + self_grad).T).reshape(hidden_in.shape)
    gain_terms = jnp.stack(
        [full_self_gain, full_cross_gain, full_feed_gain, full_exit_gain], axis=1
    ).astype(low)
    gain_terms = jnp.pad(gain_terms, ((0, 0), (0, GAIN_LANES - gain_terms.shape[1])))
    self_terms = jnp.concatenate(
        [
            contract(normed_one, qkv_grad, 1, 1).astype(low),
            contract(mixture_one, branch_one, 1, 1).astype(low),
            gain_terms,
        ],
        axis=1,
    )
    self_terms, rest_terms = lax.optimization_barrier((self_terms, rest_terms))
    self_terms = lax.psum_scatter(self_terms, dp, scatter_dimension=0, tiled=True)
    embedding_grad = table_sums[:, :vocab_rows].astype(jnp.float32).T
    (
        cross_query_grad,
        cross_key_grad,
        cross_value_grad,
        cross_output_grad,
        feed_gate_grad,
        feed_up_grad,
        *down_sums,
    ) = deliver(rest_terms, near_sizes[2:] + feed_sizes, 0, (own,) * 4 + feed_sizes)
    down_grad = jnp.concatenate(down_sums, axis=0)[:fold_rows]
    self_query_grad, self_key_grad, self_value_grad, self_output_grad, gain_sums = deliver(
        self_terms, near_sizes[:2], GAIN_LANES, (own,) * 4 + (GAIN_LANES,)
    )
    gain_sums = gain_sums[:, :4].T
    return (
        block_output,
        token_losses,
        hidden_grad,
        encoder_grad,
        gain_sums[0],
        self_query_grad,
        self_key_grad,
        self_value_grad,
        self_output_grad,
        gain_sums[1],
        cross_query_grad,
        cross_key_grad,
        cross_value_grad,
        cross_output_grad,
        gain_sums[2],
        feed_gate_grad,
        feed_up_grad,
        down_grad,
        gain_sums[3],
        embedding_grad,
    )


def solution(mesh):
    size = mesh.shape["seq"]
    planes = Mesh(mesh.devices.reshape(-1, size, size), dp + ("seq",))
    tokens = P(dp, "seq")
    rows = P(dp)
    matrix = P(dp, "seq")
    block = P(dp, "seq", None)
    attention = (rows,) + (matrix,) * 4
    return jax.shard_map(
        per_device,
        mesh=planes,
        in_specs=(block, block, rows, tokens, tokens, block)
        + attention * 2
        + (rows, matrix, matrix, matrix, rows, matrix),
        out_specs=(block, tokens, block, block)
        + attention * 2
        + (rows, matrix, matrix, matrix, rows, matrix),
        check_vma=False,
    )
```

profile of v0, /device:TPU:8, one launch (start us, length us, event | category | flops | bytes accessed | tf_op | source)
XLA Modules:
  0.0 862.8 jit_solution(9488831423563927993)
XLA Ops:
  12.7 5.4 all-to-all-start
  19.8 23.6 %all-to-all-done.refs_0_ = bf16[4,96,1536]{2,1,0:T(8,128)(2,1)S(1)} async-done(((bf16[4,96,1536]{2,1,0:T(8,128)(2,1)}), bf16[4,96,1536]{2,1,0:T(8,128)(2,1)S(1)}, u32[]{:S(2)}, u32[]{:S(2)}) %all-to-all-start) | async-done | bytes 1179680 | tf_op jit(solution)/shard_map/all_to_all | solution.py:53
  47.3 3.9 collective-permute-start.1
  53.4 3.6 collective-permute-start
  59.9 10.0 %collective-permute-done = s32[3,256]{1,0:T(4,128)S(1)} collective-permute-done((s32[3,256]{1,0:T(4,128)S(1)}, s32[3,256]{1,0:T(4,128)S(1)}, u32[]{:S(2)}, u32[]{:S(2)}) %collective-permute-start) | collective-permute-done | bytes 3104 | tf_op jit(solution)/shard_map/ppermute | solution.py:64
  69.9 18.6 %all-to-all-start.1 = ((bf16[4,96,1600]{2,1,0:T(8,128)(2,1)}), bf16[4,96,1600]{2,1,0:T(8,128)(2,1)S(1)}, u32[]{:S(2)}, u32[]{:S(2)}) async-start(bf16[4,96,1600]{2,1,0:T(8,128)(2,1)} %shard_map.365), calls=%async_computation.1 | async-start | bytes 2555904 | tf_op jit(solution)/shard_map/all_to_all | solution.py:53
  91.2 12.8 %all-gather.2 = s32[8,2,256]{2,1,0:T(2,128)} all-gather(s32[1,2,256]{2,1,0:T(2,128)S(1)} %slice_bitcast_fusion.1), channel_id=2, replica_groups=mesh['group'=2,'part'=4,'seq'=4] {'group','part'}, dimensions={0}, use_global_device_ids=true | all-gather | bytes 18432 | tf_op jit(solution)/shard_map/all_gather | solution.py:405
  104.0 11.8 %all-to-all-done.1.refs_0_ = bf16[4,96,1600]{2,1,0:T(8,128)(2,1)S(1)} async-done(((bf16[4,96,1600]{2,1,0:T(8,128)(2,1)}), bf16[4,96,1600]{2,1,0:T(8,128)(2,1)S(1)}, u32[]{:S(2)}, u32[]{:S(2)}) %all-to-all-start.1) | async-done | bytes 1228832 | tf_op jit(solution)/shard_map/all_to_all | solution.py:53
  131.2 3.6 all-to-all-start.2
  135.3 36.8 %all-to-all-done.2.refs_0_.refs_1_ = bf16[4,960,256]{2,1,0:T(8,128)(2,1)S(1)} async-done(((bf16[4,960,256]{2,1,0:T(8,128)(2,1)}), bf16[4,960,256]{2,1,0:T(8,128)(2,1)S(1)}, u32[]{:S(2)}, u32[]{:S(2)}) %all-to-all-start.2) | async-done | bytes 1966112 | tf_op jit(solution)/shard_map/all_to_all | solution.py:53
  173.4 11.5 %shard_map.368 = bf16[4,192,256]{2,1,0:T(8,128)(2,1)} custom-call(s32[1]{0:T(128)} %bitcast.12.prefix_ref, bf16[4,960,256]{2,1,0:T(8,128)(2,1)} %copy-done), custom_call_target="tpu_custom_call" | custom-call | tf_op jit(solution)/shard_map/pallas_call | solution.py:303
  184.9 14.7 %all_to_all.60 = bf16[4,192,256]{2,1,0:T(8,128)(2,1)S(1)} all-to-all(bf16[4,192,256]{2,1,0:T(8,128)(2,1)} %shard_map.368), channel_id=1, replica_groups=mesh['group'=2,'part'=4,'seq'=4] {'part'}, dimensions={0} | all-to-all | bytes 786432 | tf_op jit(solution)/shard_map/all_to_all | solution.py:53
  204.4 10.5 %all_to_all.61.refs_0_ = bf16[4,192,256]{2,1,0:T(8,128)(2,1)} all-to-all(bf16[4,192,256]{2,1,0:T(8,128)(2,1)S(1)} %bitcast.152), channel_id=1, replica_groups=mesh['group'=2,'part'=4,'seq'=4] {'part'}, dimensions={0} | all-to-all | bytes 786432 | tf_op jit(solution)/shard_map/all_to_all | solution.py:53
  214.9 11.2 %shard_map.369 = bf16[4,192,256]{2,1,0:T(8,128)(2,1)} custom-call(s32[1]{0:T(128)} %bitcast.12.prefix_ref, bf16[4,192,256]{2,1,0:T(8,128)(2,1)} %all_to_all.61.refs_0_, bf16[4,960,256]{2,1,0:T(8,128)(2,1)} %copy-done), custom_call_target="tpu_custom_call" | custom-call | tf_op jit(solution)/shard_map/pallas_call | solution.py:303
  226.1 3.5 all-to-all-start.5
  233.5 3.4 all-to-all-done.5
  239.7 3.1 fusion.35
  250.8 27.3 %collective-permute-done.3 = f32[256,768]{0,1:T(8,128)S(1)} collective-permute-done((f32[256,768]{0,1:T(8,128)}, f32[256,768]{0,1:T(8,128)S(1)}, u32[]{:S(2)}, u32[]{:S(2)}) %collective-permute-start.3) | collective-permute-done | bytes 786464 | tf_op jit(solution)/shard_map/ppermute | solution.py:64
  278.1 62.3 %all-gather.13.cloned.1.call-done.table_ref = bf16[768,4096]{1,0:T(8,128)(2,1)} async-done(((bf16[192,4096]{1,0:T(8,128)(2,1)}), bf16[768,4096]{1,0:T(8,128)(2,1)}) %all-gather.13.cloned.1.call-update) | async-done | bytes 6291472 | tf_op jit(solution)/shard_map/all_gather | solution.py:410
  341.8 19.6 %fusion.23 = bf16[2048,768]{1,0:T(8,128)(2,1)} fusion(bf16[768,4096]{1,0:T(8,128)(2,1)} %all-gather.13.cloned.1.call-done.table_ref, s32[2048]{0:T(1024)S(1)} %bitcast.163, pred[2048]{0:T(1024)(128)(4,1)S(1)} %broadcast_compare_fusion), kind=kOutput, calls=%fused_computation.29 | convolution fusion | flops 12903251968 | bytes 9447424 | tf_op jit(solution)/shard_map/dot_general | solution.py:23
  361.5 21.8 %all-gather.15.cloned.1.call-done.token_ref = bf16[2048,768]{1,0:T(8,128)(2,1)} async-done(((bf16[256,768]{1,0:T(8,128)(2,1)}), bf16[2048,768]{1,0:T(8,128)(2,1)}) %all-gather.15.cloned.1.call-update) | async-done | bytes 3145744 | tf_op jit(solution)/shard_map/all_gather | solution.py:468
  383.3 57.3 %shard_map.371 = (bf16[2048,4096]{1,0:T(8,128)(2,1)}, f32[2048,768]{1,0:T(8,128)}, f32[2048,128]{1,0:T(8,128)}) custom-call(bf16[2048,768]{1,0:T(8,128)(2,1)} %all-gather.15.cloned.1.call-done.token_ref, bf16[768,4096]{1,0:T(8,128)(2,1)} %all-gather.13.cloned.1.call-done.table_ref), custom_call_target="tpu_custom_call" | custom-call | tf_op jit(solution)/shard_map/pallas_call | solution.py:279
  440.6 3.8 fusion.16
  445.3 9.3 %all-gather.3 = f32[8,3,2048]{2,1,0:T(4,128)S(1)} all-gather(f32[1,3,2048]{2,1,0:T(4,128)S(1)} %maximum_bitcast_fusion), channel_id=3, replica_groups=mesh['group'=2,'part'=4,'seq'=4] {'group','part'}, dimensions={0}, use_global_device_ids=true | all-gather | bytes 221184 | tf_op jit(solution)/shard_map/all_gather | solution.py:478
  458.8 4.5 fusion.18
  466.8 3.1 collective-permute-start.5
  469.9 28.5 %fusion.13 = bf16[768,4096]{1,0:T(8,128)(2,1)} fusion(bf16[2048,768]{1,0:T(8,128)(2,1)} %all-gather.15.cloned.1.call-done.token_ref, bf16[2048,4096]{1,0:T(8,128)(2,1)} %get-tuple-element.88, f32[2048]{0:T(1024)S(1)} %bitcast.157, f32[2048]{0:T(1024)S(1)} %multiply_reduce_fusion, s32[2048]{0:T(1024)S(1)} %bitcast.164, ...), kind=kOutput, calls=%fused_computation.16 | convolution fusion | flops 12946767872 | bytes 26241024 | tf_op jit(solution)/shard_map/dot_general | solution.py:23
  498.4 11.1 %reduce-scatter.5.cloned.1.call-done = bf16[256,768]{1,0:T(8,128)(2,1)} async-done(((bf16[2048,768]{1,0:T(8,128)(2,1)}), bf16[256,768]{1,0:T(8,128)(2,1)}) %reduce-scatter.5.cloned.1.call-update) | async-done | bytes 393232 | tf_op jit(solution)/shard_map/reduce_scatter | solution.py:487
  521.2 3.8 fusion.29
  529.0 10.6 %all_to_all.62.refs_2_ = bf16[4,192,256]{2,1,0:T(8,128)(2,1)} all-to-all(bf16[4,192,256]{2,1,0:T(8,128)(2,1)S(1)} %bitcast.153), channel_id=1, replica_groups=mesh['group'=2,'part'=4,'seq'=4] {'part'}, dimensions={0} | all-to-all | bytes 786432 | tf_op jit(solution)/shard_map/all_to_all | solution.py:53
  539.7 18.6 %shard_map.372 = bf16[4,576,256]{2,1,0:T(8,128)(2,1)} custom-call(s32[1]{0:T(128)} %bitcast.12.prefix_ref, bf16[4,192,256]{2,1,0:T(8,128)(2,1)} %all_to_all.61.refs_0_, bf16[4,960,256]{2,1,0:T(8,128)(2,1)} %copy-done, bf16[4,192,256]{2,1,0:T(8,128)(2,1)} %all_to_all.62.refs_2_), custom_call_target="tpu_custom_call" | custom-call | tf_op jit(solution)/shard_map/pallas_call | solution.py:315
  558.3 19.5 %all_to_all.63 = bf16[4,576,256]{2,1,0:T(8,128)(2,1)S(1)} all-to-all(bf16[4,576,256]{2,1,0:T(8,128)(2,1)} %shard_map.372), channel_id=1, replica_groups=mesh['group'=2,'part'=4,'seq'=4] {'part'}, dimensions={0} | all-to-all | bytes 2359296 | tf_op jit(solution)/shard_map/all_to_all | solution.py:53
  577.9 3.3 multiply_reduce_fusion.2
  600.4 22.1 %reduce-scatter.7.cloned.1.call-done = bf16[192,4096]{1,0:T(8,128)(2,1)} async-done(((bf16[768,4096]{1,0:T(8,128)(2,1)}), bf16[192,4096]{1,0:T(8,128)(2,1)}) %reduce-scatter.7.cloned.1.call-update) | async-done | bytes 1572880 | tf_op jit(solution)/shard_map/reduce_scatter | solution.py:499
  622.5 3.4 fusion.45
  627.8 13.5 %all_to_all.64.refs_1_ = bf16[4,192,256]{2,1,0:T(8,128)(2,1)} all-to-all(bf16[4,192,256]{2,1,0:T(8,128)(2,1)S(1)} %bitcast.149), channel_id=1, replica_groups=mesh['group'=2,'part'=4,'seq'=4] {'part'}, dimensions={0} | all-to-all | bytes 786432 | tf_op jit(solution)/shard_map/all_to_all | solution.py:53
  641.3 19.9 %shard_map.373 = bf16[4,576,256]{2,1,0:T(8,128)(2,1)} custom-call(s32[1]{0:T(128)} %bitcast.12.prefix_ref, bf16[4,960,256]{2,1,0:T(8,128)(2,1)} %copy-done, bf16[4,192,256]{2,1,0:T(8,128)(2,1)} %all_to_all.64.refs_1_), custom_call_target="tpu_custom_call" | custom-call | tf_op jit(solution)/shard_map/pallas_call | solution.py:315
  662.2 6.7 all-to-all-start.9
  670.4 27.4 %all-to-all-done.9 = bf16[4,576,256]{2,1,0:T(8,128)(2,1)S(1)} async-done(((bf16[4,576,256]{2,1,0:T(8,128)(2,1)}), bf16[4,576,256]{2,1,0:T(8,128)(2,1)S(1)}, u32[]{:S(2)}, u32[]{:S(2)}) %all-to-all-start.9) | async-done | bytes 1179680 | tf_op jit(solution)/shard_map/all_to_all | solution.py:53
  697.9 4.0 multiply_reduce_fusion.3
  705.9 39.2 %reduce-scatter.9.cloned.1.call-done.refs_0_ = bf16[96,9472]{1,0:T(8,128)(2,1)} async-done(((bf16[768,9472]{1,0:T(8,128)(2,1)}), bf16[96,9472]{1,0:T(8,128)(2,1)}) %reduce-scatter.9.cloned.1.call-update) | async-done | bytes 1818640 | tf_op jit(solution)/shard_map/reduce_scatter | solution.py:537
  745.1 3.0 shard_map.376
  748.1 5.1 all-to-all-start.11
  759.5 32.8 %collective-permute-done.7 = f32[256,768]{0,1:T(8,128)S(1)} collective-permute-done((f32[256,768]{0,1:T(8,128)}, f32[256,768]{0,1:T(8,128)S(1)}, u32[]{:S(2)}, u32[]{:S(2)}) %collective-permute-start.7) | collective-permute-done | bytes 786464 | tf_op jit(solution)/shard_map/ppermute | solution.py:64
  793.4 14.0 %reduce-scatter.11.cloned.1.call-done.refs_0_ = bf16[96,3200]{1,0:T(8,128)(2,1)} async-done(((bf16[768,3200]{1,0:T(8,128)(2,1)}), bf16[96,3200]{1,0:T(8,128)(2,1)}) %reduce-scatter.11.cloned.1.call-update) | async-done | bytes 614416 | tf_op jit(solution)/shard_map/reduce_scatter | solution.py:559
  809.5 24.8 %all-to-all-start.10 = ((bf16[4,96,896]{2,1,0:T(8,128)(2,1)}), bf16[4,96,896]{2,1,0:T(8,128)(2,1)S(1)}, u32[]{:S(2)}, u32[]{:S(2)}) async-start(bf16[4,96,896]{2,1,0:T(8,128)(2,1)} %shard_map.374), calls=%async_computation.14 | async-start | bytes 1376256 | tf_op jit(solution)/shard_map/all_to_all | solution.py:53
  834.3 3.5 convert_bitcast_fusion
  842.2 7.8 all-to-all-done.10.terms_ref
  (280 shorter events, 127.1 us)
Async XLA Ops:
  7.2 12.5 %copy-start.65 = (s32[1,256]{1,0:T(1,128)S(1)}, s32[1,256]{1,0:T(1,128)}, u32[]{:S(2)}) copy-start(s32[1,256]{1,0:T(1,128)} %param.26) | copy-start | bytes 3076
  7.2 12.5 %copy-start.66 = (s32[1,256]{1,0:T(1,128)S(1)}, s32[1,256]{1,0:T(1,128)}, u32[]{:S(2)}) copy-start(s32[1,256]{1,0:T(1,128)} %param.25) | copy-start | bytes 3076
  12.7 34.4 %copy-start.37 = (bf16[1,256,768]{2,1,0:T(8,128)(2,1)S(1)}, bf16[1,256,768]{2,1,0:T(8,128)(2,1)}, u32[]{:S(2)}) copy-start(bf16[1,256,768]{2,1,0:T(8,128)(2,1)} %param.22) | copy-start | bytes 1179652
  12.7 38.5 %copy-start.38 = (bf16[1,256,768]{2,1,0:T(8,128)(2,1)S(1)}, bf16[1,256,768]{2,1,0:T(8,128)(2,1)}, u32[]{:S(2)}) copy-start(bf16[1,256,768]{2,1,0:T(8,128)(2,1)} %param.23) | copy-start | bytes 1179652
  12.7 30.7 %all-to-all-start = ((bf16[4,96,1536]{2,1,0:T(8,128)(2,1)}), bf16[4,96,1536]{2,1,0:T(8,128)(2,1)S(1)}, u32[]{:S(2)}, u32[]{:S(2)}) async-start(bf16[4,96,1536]{2,1,0:T(8,128)(2,1)} %shard_map.366), calls=%async_computation | async-start | bytes 2359296 | tf_op jit(solution)/shard_map/all_to_all | solution.py:53
  18.1 35.2 %copy-start.42 = (bf16[256,192]{0,1:T(8,128)(2,1)S(1)}, bf16[256,192]{0,1:T(8,128)(2,1)}, u32[]{:S(2)}) copy-start(bf16[256,192]{0,1:T(8,128)(2,1)} %param.41) | copy-start | bytes 294916
  18.1 104.1 %all-gather.9.cloned.1.call-start = ((), (), s32[]{:S(2)}) async-start(), calls=%async_computation.16 | async-start | bytes 10838016 | tf_op jit(solution)/shard_map/all_gather | solution.py:128
  47.3 22.7 %collective-permute-start.1 = (bf16[256,768]{0,1:T(8,128)(2,1)S(1)}, bf16[256,768]{0,1:T(8,128)(2,1)S(1)}, u32[]{:S(2)}, u32[]{:S(2)}) collective-permute-start(bf16[256,768]{0,1:T(8,128)(2,1)S(1)} %bitcast.147), channel_id=1, source_target_pairs={{0,0},{1,4},{2,8},{3,12},{4,1},{5,5},{6,9},{7,13},{8,2},{9,6},{10,... | collective-permute-start | bytes 1179656 | tf_op jit(solution)/shard_map/ppermute | solution.py:64
  51.4 18.6 %collective-permute-start.2 = (bf16[256,768]{0,1:T(8,128)(2,1)S(1)}, bf16[256,768]{0,1:T(8,128)(2,1)S(1)}, u32[]{:S(2)}, u32[]{:S(2)}) collective-permute-start(bf16[256,768]{0,1:T(8,128)(2,1)S(1)} %bitcast.148), channel_id=1, source_target_pairs={{0,0},{1,4},{2,8},{3,12},{4,1},{5,5},{6,9},{7,13},{8,2},{9,6},{10,... | collective-permute-start | bytes 1179656 | tf_op jit(solution)/shard_map/ppermute | solution.py:64
  53.4 16.5 %collective-permute-start = (s32[3,256]{1,0:T(4,128)S(1)}, s32[3,256]{1,0:T(4,128)S(1)}, u32[]{:S(2)}, u32[]{:S(2)}) collective-permute-start(s32[3,256]{1,0:T(4,128)S(1)} %add_add_fusion.4), channel_id=1, source_target_pairs={{0,0},{1,4},{2,8},{3,12},{4,1},{5,5},{6,9},{7,13},{8,2},{9,6},{10,... | collective-permute-start | bytes 9224 | tf_op jit(solution)/shard_map/ppermute | solution.py:64
  69.9 54.1 %copy-start.35 = (bf16[256,768]{0,1:T(8,128)(2,1)}, bf16[256,768]{0,1:T(8,128)(2,1)S(1)}, u32[]{:S(2)}) copy-start(bf16[256,768]{0,1:T(8,128)(2,1)S(1)} %collective-permute-done.2) | copy-start | bytes 1179652
  69.9 45.9 %all-to-all-start.1 = ((bf16[4,96,1600]{2,1,0:T(8,128)(2,1)}), bf16[4,96,1600]{2,1,0:T(8,128)(2,1)S(1)}, u32[]{:S(2)}, u32[]{:S(2)}) async-start(bf16[4,96,1600]{2,1,0:T(8,128)(2,1)} %shard_map.365), calls=%async_computation.1 | async-start | bytes 2555904 | tf_op jit(solution)/shard_map/all_to_all | solution.py:53
  88.5 151.2 %all-gather.11.cloned.1.call-start = ((), (), s32[]{:S(2)}) async-start(), calls=%async_computation.17 | async-start | bytes 11059200 | tf_op jit(solution)/shard_map/all_gather | solution.py:128
  119.4 221.0 %all-gather.13.cloned.1.call-start = ((), (), s32[]{:S(2)}) async-start(), calls=%async_computation.18 | async-start | bytes 7864320 | tf_op jit(solution)/shard_map/all_gather | solution.py:410
  124.0 78.2 %copy-start.44 = (f32[768]{0:T(1024)}, f32[768]{0:T(1024)S(1)}, u32[]{:S(2)}) copy-start(f32[768]{0:T(1024)S(1)} %get-tuple-element.208) | copy-start | bytes 9220
  131.2 40.9 %all-to-all-start.2 = ((bf16[4,960,256]{2,1,0:T(8,128)(2,1)}), bf16[4,960,256]{2,1,0:T(8,128)(2,1)S(1)}, u32[]{:S(2)}, u32[]{:S(2)}) async-start(bf16[4,960,256]{2,1,0:T(8,128)(2,1)} %pad_maximum_fusion.2), calls=%async_computation.2 | async-start | bytes 3932160 | tf_op jit(solution)/shard_map/all_to_all | solution.py:53
  202.2 23.9 %copy-start.55 = (f32[256]{0:T(256)}, f32[256]{0:T(256)S(1)}, u32[]{:S(2)}) copy-start(f32[256]{0:T(256)S(1)} %get-tuple-element.232) | copy-start | bytes 3076
  202.2 34.8 %copy-start.33 = (f32[768,256]{1,0:T(8,128)}, f32[768,256]{1,0:T(8,128)S(1)}, u32[]{:S(2)}) copy-start(f32[768,256]{1,0:T(8,128)S(1)} %get-tuple-element.233) | copy-start | bytes 2359300
  202.2 23.9 %copy-start.53 = (f32[256]{0:T(256)}, f32[256]{0:T(256)S(1)}, u32[]{:S(2)}) copy-start(f32[256]{0:T(256)S(1)} %fusion.91) | copy-start | bytes 3076
  202.2 27.4 %copy-start.30 = (f32[1,256,768]{2,1,0:T(8,128)S(1)}, f32[1,256,768]{2,1,0:T(8,128)}, u32[]{:S(2)}) copy-start(f32[1,256,768]{2,1,0:T(8,128)} %param.27) | copy-start | bytes 2359300
  226.1 10.8 %all-to-all-start.5 = ((bf16[4,192,256]{2,1,0:T(8,128)(2,1)}), bf16[4,192,256]{2,1,0:T(8,128)(2,1)S(1)}, u32[]{:S(2)}, u32[]{:S(2)}) async-start(bf16[4,192,256]{2,1,0:T(8,128)(2,1)} %shard_map.369), calls=%async_computation.5 | async-start | bytes 786432 | tf_op jit(solution)/shard_map/all_to_all | solution.py:53
  229.6 153.7 %all-gather.15.cloned.1.call-start = ((), (), s32[]{:S(2)}) async-start(), calls=%async_computation.19 | async-start | bytes 3538944 | tf_op jit(solution)/shard_map/all_gather | solution.py:468
  230.8 47.3 %collective-permute-start.3 = (f32[256,768]{0,1:T(8,128)}, f32[256,768]{0,1:T(8,128)S(1)}, u32[]{:S(2)}, u32[]{:S(2)}) collective-permute-start(f32[256,768]{0,1:T(8,128)} %bitcast.24), channel_id=1, source_target_pairs={{0,0},{1,4},{2,8},{3,12},{4,1},{5,5},{6,9},{7,13},{8,2},{9,6},{10,... | collective-permute-start | bytes 2359304 | tf_op jit(solution)/shard_map/ppermute | solution.py:64
  248.4 92.0 %copy-start.43 = (s32[8,2,256]{2,1,0:T(2,128)S(1)}, s32[8,2,256]{2,1,0:T(2,128)}, u32[]{:S(2)}) copy-start(s32[8,2,256]{2,1,0:T(2,128)} %all-gather.2) | copy-start | bytes 49156
  249.0 112.5 %copy-start.59 = (f32[256]{0:T(256)}, f32[256]{0:T(256)S(1)}, u32[]{:S(2)}) copy-start(f32[256]{0:T(256)S(1)} %get-tuple-element.238) | copy-start | bytes 3076
  278.1 83.4 %copy-start.11 = (f32[256,768]{0,1:T(8,128)}, f32[256,768]{0,1:T(8,128)S(1)}, u32[]{:S(2)}) copy-start(f32[256,768]{0,1:T(8,128)S(1)} %collective-permute-done.3) | copy-start | bytes 2359300
  340.4 169.1 %reduce-scatter.5.cloned.1.call-start = ((), (), s32[]{:S(2)}) async-start(), calls=%async_computation.20 | async-start | bytes 3538944 | tf_op jit(solution)/shard_map/reduce_scatter | solution.py:487
  463.3 159.2 %reduce-scatter.7.cloned.1.call-start = ((), (), s32[]{:S(2)}) async-start(), calls=%async_computation.21 | async-start | bytes 7864320 | tf_op jit(solution)/shard_map/reduce_scatter | solution.py:499
  464.3 34.1 %collective-permute-start.4 = (bf16[256,768]{0,1:T(8,128)(2,1)S(1)}, bf16[256,768]{0,1:T(8,128)(2,1)S(1)}, u32[]{:S(2)}, u32[]{:S(2)}) collective-permute-start(bf16[256,768]{0,1:T(8,128)(2,1)S(1)} %copy-done.41), channel_id=1, source_target_pairs={{0,0},{1,4},{2,8},{3,12},{4,1},{5,5},{6,9},{7,13},{8,2},{9,6},{10,... | collective-permute-start | bytes 1179656 | tf_op jit(solution)/shard_map/ppermute | solution.py:64
  466.8 31.7 %collective-permute-start.5 = (f32[1,256]{1,0:T(1,128)S(1)}, f32[1,256]{1,0:T(1,128)S(1)}, u32[]{:S(2)}, u32[]{:S(2)}) collective-permute-start(f32[1,256]{1,0:T(1,128)S(1)} %bitcast.165), channel_id=1, source_target_pairs={{0,0},{1,4},{2,8},{3,12},{4,1},{5,5},{6,9},{7,13},{8,2},{9,6},{10,... | collective-permute-start | bytes 3080 | tf_op jit(solution)/shard_map/ppermute | solution.py:64
  509.6 235.5 %reduce-scatter.9.cloned.1.call-start = ((), (), s32[]{:S(2)}) async-start(), calls=%async_computation.22 | async-start | bytes 16367616 | tf_op jit(solution)/shard_map/reduce_scatter | solution.py:537
  558.3 19.6 %copy-start.34 = (f32[768,256]{1,0:T(8,128)S(1)}, f32[768,256]{1,0:T(8,128)}, u32[]{:S(2)}) copy-start(f32[768,256]{1,0:T(8,128)} %copy-done.33) | copy-start | bytes 2359300
  558.3 19.6 %copy-start.45 = (f32[768]{0:T(1024)S(1)}, f32[768]{0:T(1024)}, u32[]{:S(2)}) copy-start(f32[768]{0:T(1024)} %copy-done.44) | copy-start | bytes 9220
  558.3 19.6 %copy-start.54 = (f32[256]{0:T(256)S(1)}, f32[256]{0:T(256)}, u32[]{:S(2)}) copy-start(f32[256]{0:T(256)} %copy-done.53) | copy-start | bytes 3076
  625.9 35.4 %collective-permute-start.6 = (f32[256,768]{1,0:T(8,128)}, f32[256,768]{1,0:T(8,128)S(1)}, u32[]{:S(2)}, u32[]{:S(2)}) collective-permute-start(f32[256,768]{1,0:T(8,128)} %fusion.45), channel_id=1, source_target_pairs={{0,0},{1,4},{2,8},{3,12},{4,1},{5,5},{6,9},{7,13},{8,2},{9,6},{10,... | collective-permute-start | bytes 2359304 | tf_op jit(solution)/shard_map/ppermute | solution.py:64
  641.3 27.5 %copy-start.52 = (bf16[768]{0:T(1024)(128)(2,1)S(1)}, bf16[768]{0:T(1024)(128)(2,1)}, u32[]{:S(2)}) copy-start(bf16[768]{0:T(1024)(128)(2,1)} %get-tuple-element.202) | copy-start | bytes 4612
  641.3 27.5 %copy-start.61 = (bf16[768]{0:T(1024)(128)(2,1)S(1)}, bf16[768]{0:T(1024)(128)(2,1)}, u32[]{:S(2)}) copy-start(bf16[768]{0:T(1024)(128)(2,1)} %get-tuple-element.200) | copy-start | bytes 4612
  641.3 27.5 %copy-start.62 = (bf16[768]{0:T(1024)(128)(2,1)S(1)}, bf16[768]{0:T(1024)(128)(2,1)}, u32[]{:S(2)}) copy-start(bf16[768]{0:T(1024)(128)(2,1)} %get-tuple-element.198) | copy-start | bytes 4612
  641.3 27.6 %copy-start.21 = (bf16[4,192,256]{2,1,0:T(8,128)(2,1)S(1)}, bf16[4,192,256]{2,1,0:T(8,128)(2,1)}, u32[]{:S(2)}) copy-start(bf16[4,192,256]{2,1,0:T(8,128)(2,1)} %copy-done.20) | copy-start | bytes 1179652
  661.2 36.6 %copy-start.47 = (f32[256]{0:T(256)S(1)}, f32[256]{0:T(256)}, u32[]{:S(2)}) copy-start(f32[256]{0:T(256)} %copy-done.46) | copy-start | bytes 3076
  662.2 35.7 %all-to-all-start.9 = ((bf16[4,576,256]{2,1,0:T(8,128)(2,1)}), bf16[4,576,256]{2,1,0:T(8,128)(2,1)S(1)}, u32[]{:S(2)}, u32[]{:S(2)}) async-start(bf16[4,576,256]{2,1,0:T(8,128)(2,1)} %shard_map.373), calls=%async_computation.10 | async-start | bytes 2359296 | tf_op jit(solution)/shard_map/all_to_all | solution.py:53
  668.8 138.6 %reduce-scatter.11.cloned.1.call-start = ((), (), s32[]{:S(2)}) async-start(), calls=%async_computation.23 | async-start | bytes 5529600 | tf_op jit(solution)/shard_map/reduce_scatter | solution.py:559
  748.1 61.4 %all-to-all-start.11 = ((bf16[4,96,2368]{2,1,0:T(8,128)(2,1)}), bf16[4,96,2368]{2,1,0:T(8,128)(2,1)S(1)}, u32[]{:S(2)}, u32[]{:S(2)}) async-start(bf16[4,96,2368]{2,1,0:T(8,128)(2,1)} %shard_map.376), calls=%async_computation.15 | async-start | bytes 3735552 | tf_op jit(solution)/shard_map/all_to_all | solution.py:53
  755.6 36.6 %collective-permute-start.7 = (f32[256,768]{0,1:T(8,128)}, f32[256,768]{0,1:T(8,128)S(1)}, u32[]{:S(2)}, u32[]{:S(2)}) collective-permute-start(f32[256,768]{0,1:T(8,128)} %fusion.80), channel_id=1, source_target_pairs={{0,0},{1,4},{2,8},{3,12},{4,1},{5,5},{6,9},{7,13},{8,2},{9,6},{10,... | collective-permute-start | bytes 2359304 | tf_op jit(solution)/shard_map/ppermute | solution.py:64
  809.5 28.3 %copy-start.3 = (bf16[4,96,2368]{2,1,0:T(8,128)(2,1)}, bf16[4,96,2368]{2,1,0:T(8,128)(2,1)S(1)}, u32[]{:S(2)}) copy-start(bf16[4,96,2368]{2,1,0:T(8,128)(2,1)S(1)} %all-to-all-done.11.terms_ref) | copy-start | bytes 5455876
  809.5 40.5 %all-to-all-start.10 = ((bf16[4,96,896]{2,1,0:T(8,128)(2,1)}), bf16[4,96,896]{2,1,0:T(8,128)(2,1)S(1)}, u32[]{:S(2)}, u32[]{:S(2)}) async-start(bf16[4,96,896]{2,1,0:T(8,128)(2,1)} %shard_map.374), calls=%async_computation.14 | async-start | bytes 1376256 | tf_op jit(solution)/shard_map/all_to_all | solution.py:53
  834.3 20.1 %copy-start.64 = (f32[1,256]{1,0:T(1,128)S(1)}, f32[1,256]{1,0:T(1,128)}, u32[]{:S(2)}) copy-start(f32[1,256]{1,0:T(1,128)} %copy-done.63) | copy-start | bytes 3076
  834.3 20.6 %copy-start.32 = (f32[256,768]{1,0:T(8,128)S(1)}, f32[256,768]{1,0:T(8,128)}, u32[]{:S(2)}) copy-start(f32[256,768]{1,0:T(8,128)} %copy-done.31) | copy-start | bytes 2359300
  (50 other events, 210.1 us)
Sparse Core Ops, SparseCore 0:
  47.2 75.0 all-gather.8
  124.1 76.4 all-gather.10
  202.3 138.0 all-gather.12
  342.1 41.1 all-gather.14
  463.4 46.0 reduce-scatter.4
  511.7 110.7 reduce-scatter.6
  626.1 118.8 reduce-scatter.8
  748.6 58.8 reduce-scatter.10
where the time goes:
time: 872 us; the launch traced here: 863 us
  waiting for transfers between devices  354 us (41%)
  Pallas kernels  138 us (16%)
  matrix products  109 us (12%)
  blocking collectives  90.9 us (10%)
  starting transfers between devices  89.4 us (10%)
  local copies, waits for them, and re-layouts  33.5 us (4%)
  other arithmetic  32.8 us (4%)
  between operations  16.1 us (2%)
    all_to_all x7, waiting for transfers between devices, swap(): return lax.all_to_all(pieces, axis, 0, 0, tiled=True)  111 us
    dot_general x32, matrix products, contract(): lax.dot_general(first_op, second_op, (((first_dim,), (second_dim,)), ((),...  109 us
    ppermute x8, waiting for transfers between devices, relocate(): return lax.ppermute(block, ('group', 'part', 'seq'), pairs)  70.1 us
    all_to_all x5, blocking collectives, swap(): return lax.all_to_all(pieces, axis, 0, 0, tiled=True)  68.8 us
    all_to_all x7, starting transfers between devices, swap(): return lax.all_to_all(pieces, axis, 0, 0, tiled=True)  67.6 us
    all_gather x1, waiting for transfers between devices, per_device(): table = lax.all_gather(shard, 'seq', axis=0, tiled=True)  62.3 us
    pallas_call x1, Pallas kernels, exit_rows(): pl.pallas_call(functools.partial(exit_kernel, rows=rows), grid=(count //...  57.3 us
    reduce_scatter x1, waiting for transfers between devices, per_device(): lax.psum_scatter(rest_terms, dp, scatter_dimension=0, tiled=True)  39.2 us
  transfers between devices with their start and end apart: 23, of which 16 were waited for; matrix products, arithmetic and copies ran while one was open for 16% of the time, Pallas kernels for 9%

commit v1 on v0

--- a/solution.py
+++ b/solution.py
@@ -91,7 +91,7 @@
 every = slice(None)
 
 
-def exchange(shards, after):
+def exchange(shards):
     n_seq = lax.axis_size("seq")
     rows = shards[0].shape[0]
     sizes = [shard.shape[1] for shard in shards]
@@ -102,8 +102,7 @@
         for block in range(n_seq)
     ]
     (copies,) = move(shards, [(n_seq, rows, starts[-1])], moves)
-    copies, after = lax.optimization_barrier((copies, after))
-    return swap(copies, "seq"), after
+    return swap(copies, "seq")
 
 
 def fetch(parts, sizes, extra):
@@ -367,48 +366,42 @@
 
     gains = jnp.stack([self_gain, cross_gain, feed_gain, exit_gain], axis=1)
     gains = jnp.pad(gains, ((0, 0), (0, GAIN_LANES - gains.shape[1])))
-    near_parts, moved = exchange(
+    folded = jnp.pad(feed_down, ((0, folds * own_rows - fold_rows), (0, 0)))
+    parts = exchange(
         [
             jnp.concatenate([self_query, self_key, self_value], axis=1),
             self_output,
             cross_query,
             jnp.concatenate([cross_key, cross_value], axis=1),
             cross_output,
-        ],
-        (),
-    )
-    near_sizes = (3 * own, own, own, 2 * own, own)
+            feed_gate,
+            feed_up,
+        ]
+        + [folded[fold * own_rows : (fold + 1) * own_rows] for fold in range(folds)]
+    )
+    self_sizes = (3 * own, own)
+    rest_sizes = (own, 2 * own, own, own_feed, own_feed) + (own,) * folds
 
     marks = jnp.concatenate(
         [exit_flags, target_ids, jnp.broadcast_to(prefix_len[:, None], exit_flags.shape)], axis=0
     )
-    near_parts, marks, hidden_in, encoder_in = lax.optimization_barrier(
-        (near_parts, marks, hidden_in, encoder_in)
-    )
-    near = fetch(near_parts, near_sizes, gains)
-    self_qkv, self_out, cross_q, cross_kv, cross_out, gain_columns = cut(
-        near, tuple(n_seq * size for size in near_sizes) + (GAIN_LANES,)
-    )
-    moved = (
-        relocate(marks),
-        relocate(hidden_in.reshape(-1, width)),
-        relocate(encoder_in.reshape(-1, width)),
-    )
-    folded = jnp.pad(feed_down, ((0, folds * own_rows - fold_rows), (0, 0)))
-    feed_parts, (marks, hidden, states) = exchange(
-        [feed_gate, feed_up]
-        + [folded[fold * own_rows : (fold + 1) * own_rows] for fold in range(folds)],
-        moved,
-    )
-    feed_sizes = (own_feed, own_feed) + (own,) * folds
+    parts, marks, hidden, states, cotangent = lax.optimization_barrier(
+        (parts, marks, hidden_in, encoder_in, out_cotangent.astype(low))
+    )
+    weights = fetch(parts, self_sizes + rest_sizes, gains)
+    self_qkv, self_out, cross_q, cross_kv, cross_out, gate_full, up_full, *downs = cut(
+        weights, tuple(n_seq * size for size in self_sizes + rest_sizes) + (GAIN_LANES,)
+    )
+    gain_columns = downs.pop()
+    hidden = relocate(hidden.reshape(-1, width))
+    states = relocate(states.reshape(-1, width))
+    marks = relocate(marks)
     prefix_len = marks[2, :1]
     marks = lax.all_gather(marks[:2], dp, axis=0)
     shard = jnp.pad(embedding.T, ((0, 0), (0, vocab_lanes - vocab_rows)))
-    feed_parts, shard, marks = lax.optimization_barrier((feed_parts, shard, marks))
-    feed = fetch(feed_parts, feed_sizes, None)
-    gate_full, up_full, *downs = cut(feed, tuple(n_seq * size for size in feed_sizes))
+    shard, marks, hidden, states = lax.optimization_barrier((shard, marks, hidden, states))
     table = lax.all_gather(shard, "seq", axis=0, tiled=True)
-    cotangent = relocate(out_cotangent.reshape(-1, width))
+    cotangent = relocate(cotangent.reshape(-1, width))
     gain_one, gain_two, gain_three, gain_exit = gain_columns[:, :4].astype(jnp.float32).T
 
     def blocks(rows):
@@ -429,9 +422,9 @@
 
     residual_in = hidden.T.astype(jnp.float32)
     token_count = residual_in.shape[1]
-    residual_in, states, marks = lax.optimization_barrier((residual_in, states.T, marks))
+    residual_in, states, cotangent = lax.optimization_barrier((residual_in, states.T, cotangent.T))
     residual_in, states = rows_first(residual_in), rows_first(states)
-    cotangent = rows_first(cotangent.T)
+    cotangent = rows_first(cotangent)
     normed_one = norm_columns(residual_in, gain_one).astype(low)
     attended = swap(
         jnp.concatenate(
@@ -463,7 +456,7 @@
         after_feed = after_feed + contract(down, hidden, 0, 0)
     block_output = relocate(after_feed.T.astype(low)).reshape(hidden_in.shape)
     normed_exit = rows_first(norm_columns(after_feed, gain_exit).astype(low).T)
-    normed_exit, table, cotangent = lax.optimization_barrier((normed_exit, table, cotangent))
+    normed_exit, table = lax.optimization_barrier((normed_exit, table))
 
     tokens = lax.all_gather(normed_exit, dp, axis=0, tiled=True)
     flag_rows = marks[:, 0].reshape(-1, 1).astype(jnp.float32)
@@ -516,7 +509,7 @@
     cross_grads = swap(cross_grads, "part")
     q_grad = cross_grads[:, :own].reshape(-1, token_count)
     kv_grad = cross_grads[:, own:].reshape(-1, token_count)
-    encoder_grad = relocate(contract(kv_grad, cross_kv, 0, 1)).reshape(encoder_in.shape)
+    encoder_grad = relocate(contract(kv_grad, cross_kv, 0, 1).astype(low)).astype(jnp.float32)
     rest_terms = jnp.concatenate(
         [
             contract(normed_two, q_grad, 1, 1).astype(low),
@@ -542,7 +535,7 @@
     qkv_grad = swap(qkv_grad, "part").reshape(-1, token_count)
     normed_one_grad = contract(self_qkv, qkv_grad, 1, 0)
     input_grad, full_self_gain = norm_back(residual_in, gain_one, normed_one_grad)
-    hidden_grad = relocate((input_grad + self_grad).T).reshape(hidden_in.shape)
+    hidden_grad = relocate((input_grad + self_grad).T.astype(low)).astype(jnp.float32)
     gain_terms = jnp.stack(
         [full_self_gain, full_cross_gain, full_feed_gain, full_exit_gain], axis=1
     ).astype(low)
@@ -566,17 +559,17 @@
         feed_gate_grad,
         feed_up_grad,
         *down_sums,
-    ) = deliver(rest_terms, near_sizes[2:] + feed_sizes, 0, (own,) * 4 + feed_sizes)
+    ) = deliver(rest_terms, rest_sizes, 0, (own,) * 4 + rest_sizes[3:])
     down_grad = jnp.concatenate(down_sums, axis=0)[:fold_rows]
     self_query_grad, self_key_grad, self_value_grad, self_output_grad, gain_sums = deliver(
-        self_terms, near_sizes[:2], GAIN_LANES, (own,) * 4 + (GAIN_LANES,)
+        self_terms, self_sizes, GAIN_LANES, (own,) * 4 + (GAIN_LANES,)
     )
     gain_sums = gain_sums[:, :4].T
     return (
         block_output,
         token_losses,
-        hidden_grad,
-        encoder_grad,
+        hidden_grad.reshape(hidden_in.shape),
+        encoder_grad.reshape(encoder_in.shape),
         gain_sums[0],
         self_query_grad,
         self_key_grad,

time: 872 us -> 824 us (0.945)
  waiting for transfers between devices: 354 us -> 314 us
  starting transfers between devices: 89.4 us -> 52.1 us
  blocking collectives: 90.9 us -> 111 us
  matrix products: 109 us -> 119 us
    all_gather x1, waiting for transfers between devices: 62.3 us -> 0.01 us  [per_device(): table = lax.all_gather(shard, 'seq', axis=0, tiled=True)]
    all_gather x2 -> x1, waiting for transfers between devices: 1.42 us -> 56.4 us  [fetch(): return lax.all_gather(full, dp, axis=0, tiled=True)]
    all_to_all x7 -> x5, starting transfers between devices: 67.6 us -> 29.3 us  [swap(): return lax.all_to_all(pieces, axis, 0, 0, tiled=True)]
    ppermute x8, waiting for transfers between devices: 70.1 us -> 46.2 us  [relocate(): return lax.ppermute(block, ('group', 'part', 'seq'), pairs)]
    all_gather x1, blocking collectives: 12.8 us -> 26.1 us  [per_device(): marks = lax.all_gather(marks[:2], dp, axis=0)]
    dot_general x32, matrix products: 109 us -> 119 us  [contract(): lax.dot_general(first_op, second_op, (((first_dim,), (second_dim,)), ((),...]
    all_to_all x5 -> x6, blocking collectives: 68.8 us -> 75.2 us  [swap(): return lax.all_to_all(pieces, axis, 0, 0, tiled=True)]
    unnamed x158 -> x133, local copies, waits for them, and re-layouts: 20.9 us -> 15.4 us
  transfers between devices with their start and end apart: 23 -> 20, of which waited for: 16 -> 13; matrix products, arithmetic and copies ran while one was open for 16% -> 19% of each run, Pallas kernels for 9% -> 9%
where the time goes in v1:
time: 824 us; the launch traced here: 809 us
  waiting for transfers between devices  314 us (38%)
  Pallas kernels  135 us (16%)
  matrix products  119 us (14%)
  blocking collectives  111 us (13%)
  starting transfers between devices  52.1 us (6%)
  other arithmetic  36 us (4%)
  local copies, waits for them, and re-layouts  26.5 us (3%)
  between operations  15.9 us (2%)
    dot_general x32, matrix products, contract(): lax.dot_general(first_op, second_op, (((first_dim,), (second_dim,)), ((),...  119 us
    all_to_all x5, waiting for transfers between devices, swap(): return lax.all_to_all(pieces, axis, 0, 0, tiled=True)  109 us
    all_to_all x6, blocking collectives, swap(): return lax.all_to_all(pieces, axis, 0, 0, tiled=True)  75.2 us
    pallas_call x1, Pallas kernels, exit_rows(): pl.pallas_call(functools.partial(exit_kernel, rows=rows), grid=(count //...  57.3 us
    all_gather x1, waiting for transfers between devices, fetch(): return lax.all_gather(full, dp, axis=0, tiled=True)  56.4 us
    ppermute x8, waiting for transfers between devices, relocate(): return lax.ppermute(block, ('group', 'part', 'seq'), pairs)  46.2 us
    reduce_scatter x1, waiting for transfers between devices, per_device(): lax.psum_scatter(rest_terms, dp, scatter_dimension=0, tiled=True)  40.7 us
    pallas_call x2, Pallas kernels, attend_back(): pl.pallas_call(functools.partial(attend_back_kernel, places=places, spots...  38.4 us
  transfers between devices with their start and end apart: 20, of which 13 were waited for; matrix products, arithmetic and copies ran while one was open for 19% of the time, Pallas kernels for 9%

profile of v1, /device:TPU:8, one launch (start us, length us, event | category | flops | bytes accessed | tf_op | source)
XLA Modules:
  0.0 808.9 jit_solution(9614412323928238851)
XLA Ops:
  15.0 5.5 all-to-all-start
  22.9 50.1 %all-to-all-done.refs_0_ = bf16[4,96,3136]{2,1,0:T(8,128)(2,1)S(1)} async-done(((bf16[4,96,3136]{2,1,0:T(8,128)(2,1)}), bf16[4,96,3136]{2,1,0:T(8,128)(2,1)S(1)}, u32[]{:S(2)}, u32[]{:S(2)}) %all-to-all-start) | async-done | bytes 2408480 | tf_op jit(solution)/shard_map/all_to_all | solution.py:53
  74.5 3.6 shard_map.366
  78.4 4.0 collective-permute-start.1
  84.5 3.6 collective-permute-start
  89.5 11.6 %collective-permute-done = s32[3,256]{1,0:T(4,128)S(1)} collective-permute-done((s32[3,256]{1,0:T(4,128)S(1)}, s32[3,256]{1,0:T(4,128)S(1)}, u32[]{:S(2)}, u32[]{:S(2)}) %collective-permute-start) | collective-permute-done | bytes 3104 | tf_op jit(solution)/shard_map/ppermute | solution.py:64
  101.1 26.1 %all-gather.2 = s32[8,2,256]{2,1,0:T(2,128)} all-gather(s32[1,2,256]{2,1,0:T(2,128)S(1)} %slice_bitcast_fusion.1), channel_id=2, replica_groups=mesh['group'=2,'part'=4,'seq'=4] {'group','part'}, dimensions={0}, use_global_device_ids=true | all-gather | bytes 18432 | tf_op jit(solution)/shard_map/all_gather | solution.py:400
  127.3 3.4 collective-permute-start.3
  131.8 5.9 collective-permute-done.3
  137.9 56.4 %all-gather.8.cloned.1.call-done = bf16[768,12672]{1,0:T(8,128)(2,1)} async-done(((bf16[96,12672]{1,0:T(8,128)(2,1)}), bf16[768,12672]{1,0:T(8,128)(2,1)}) %all-gather.8.cloned.1.call-update) | async-done | bytes 19464208 | tf_op jit(solution)/shard_map/all_gather | solution.py:127
  198.6 3.3 convolution_convert_fusion.1
  203.3 5.5 all-to-all-start.1
  209.2 24.2 %all-to-all-done.1.refs_0_.refs_1_ = bf16[4,960,256]{2,1,0:T(8,128)(2,1)S(1)} async-done(((bf16[4,960,256]{2,1,0:T(8,128)(2,1)}), bf16[4,960,256]{2,1,0:T(8,128)(2,1)S(1)}, u32[]{:S(2)}, u32[]{:S(2)}) %all-to-all-start.1) | async-done | bytes 1966112 | tf_op jit(solution)/shard_map/all_to_all | solution.py:53
  234.7 11.5 %shard_map.367 = bf16[4,192,256]{2,1,0:T(8,128)(2,1)} custom-call(s32[1]{0:T(128)} %bitcast.14.prefix_ref, bf16[4,960,256]{2,1,0:T(8,128)(2,1)} %copy-done), custom_call_target="tpu_custom_call" | custom-call | tf_op jit(solution)/shard_map/pallas_call | solution.py:302
  246.2 10.8 %all_to_all.55 = bf16[4,192,256]{2,1,0:T(8,128)(2,1)S(1)} all-to-all(bf16[4,192,256]{2,1,0:T(8,128)(2,1)} %shard_map.367), channel_id=1, replica_groups=mesh['group'=2,'part'=4,'seq'=4] {'part'}, dimensions={0} | all-to-all | bytes 786432 | tf_op jit(solution)/shard_map/all_to_all | solution.py:53
  261.9 10.5 %all_to_all.56.refs_0_ = bf16[4,192,256]{2,1,0:T(8,128)(2,1)} all-to-all(bf16[4,192,256]{2,1,0:T(8,128)(2,1)S(1)} %bitcast.151), channel_id=1, replica_groups=mesh['group'=2,'part'=4,'seq'=4] {'part'}, dimensions={0} | all-to-all | bytes 786432 | tf_op jit(solution)/shard_map/all_to_all | solution.py:53
  272.3 11.2 %shard_map.368 = bf16[4,192,256]{2,1,0:T(8,128)(2,1)} custom-call(s32[1]{0:T(128)} %bitcast.14.prefix_ref, bf16[4,192,256]{2,1,0:T(8,128)(2,1)} %all_to_all.56.refs_0_, bf16[4,960,256]{2,1,0:T(8,128)(2,1)} %copy-done), custom_call_target="tpu_custom_call" | custom-call | tf_op jit(solution)/shard_map/pallas_call | solution.py:302
  283.5 11.1 %all_to_all.57 = bf16[4,192,256]{2,1,0:T(8,128)(2,1)S(1)} all-to-all(bf16[4,192,256]{2,1,0:T(8,128)(2,1)} %shard_map.368), channel_id=1, replica_groups=mesh['group'=2,'part'=4,'seq'=4] {'part'}, dimensions={0} | all-to-all | bytes 786432 | tf_op jit(solution)/shard_map/all_to_all | solution.py:53
  300.2 5.4 multiply_convert_fusion
  314.9 19.6 %fusion.23 = bf16[2048,768]{1,0:T(8,128)(2,1)} fusion(bf16[768,4096]{1,0:T(8,128)(2,1)} %all-gather.10.cloned.1.call-done.table_ref, s32[2048]{0:T(1024)S(1)} %bitcast.163, pred[2048]{0:T(1024)(128)(4,1)S(1)} %broadcast_compare_fusion), kind=kOutput, calls=%fused_computation.29 | convolution fusion | flops 12903251968 | bytes 9447424 | tf_op jit(solution)/shard_map/dot_general | solution.py:23
  334.5 13.7 %all-gather.12.cloned.1.call-done.token_ref = bf16[2048,768]{1,0:T(8,128)(2,1)} async-done(((bf16[256,768]{1,0:T(8,128)(2,1)}), bf16[2048,768]{1,0:T(8,128)(2,1)}) %all-gather.12.cloned.1.call-update) | async-done | bytes 3145744 | tf_op jit(solution)/shard_map/all_gather | solution.py:461
  348.2 57.3 %shard_map.369 = (bf16[2048,4096]{1,0:T(8,128)(2,1)}, f32[2048,768]{1,0:T(8,128)}, f32[2048,128]{1,0:T(8,128)}) custom-call(bf16[2048,768]{1,0:T(8,128)(2,1)} %all-gather.12.cloned.1.call-done.token_ref, bf16[768,4096]{1,0:T(8,128)(2,1)} %all-gather.10.cloned.1.call-done.table_ref), custom_call_target="tpu_custom_call" | custom-call | tf_op jit(solution)/shard_map/pallas_call | solution.py:278
  405.5 3.8 fusion.16
  410.3 9.3 %all-gather.3 = f32[8,3,2048]{2,1,0:T(4,128)S(1)} all-gather(f32[1,3,2048]{2,1,0:T(4,128)S(1)} %maximum_bitcast_fusion), channel_id=3, replica_groups=mesh['group'=2,'part'=4,'seq'=4] {'group','part'}, dimensions={0}, use_global_device_ids=true | all-gather | bytes 221184 | tf_op jit(solution)/shard_map/all_gather | solution.py:471
  423.7 4.5 fusion.18
  431.7 3.1 collective-permute-start.5
  434.9 28.5 %fusion.13 = bf16[768,4096]{1,0:T(8,128)(2,1)} fusion(bf16[2048,768]{1,0:T(8,128)(2,1)} %all-gather.12.cloned.1.call-done.token_ref, bf16[2048,4096]{1,0:T(8,128)(2,1)} %get-tuple-element.82, f32[2048]{0:T(1024)S(1)} %bitcast.157, f32[2048]{0:T(1024)S(1)} %multiply_reduce_fusion, s32[2048]{0:T(1024)S(1)} %bitcast.164, ...), kind=kOutput, calls=%fused_computation.16 | convolution fusion | flops 12946767872 | bytes 26241024 | tf_op jit(solution)/shard_map/dot_general | solution.py:23
  463.4 11.1 %reduce-scatter.5.cloned.1.call-done = bf16[256,768]{1,0:T(8,128)(2,1)} async-done(((bf16[2048,768]{1,0:T(8,128)(2,1)}), bf16[256,768]{1,0:T(8,128)(2,1)}) %reduce-scatter.5.cloned.1.call-update) | async-done | bytes 393232 | tf_op jit(solution)/shard_map/reduce_scatter | solution.py:480
  486.8 3.6 fusion.29
  490.5 3.6 multiply_reduce_fusion.1
  497.3 10.5 %all_to_all.58.refs_2_ = bf16[4,192,256]{2,1,0:T(8,128)(2,1)} all-to-all(bf16[4,192,256]{2,1,0:T(8,128)(2,1)S(1)} %bitcast.152), channel_id=1, replica_groups=mesh['group'=2,'part'=4,'seq'=4] {'part'}, dimensions={0} | all-to-all | bytes 786432 | tf_op jit(solution)/shard_map/all_to_all | solution.py:53
  507.8 18.6 %shard_map.370 = bf16[4,576,256]{2,1,0:T(8,128)(2,1)} custom-call(s32[1]{0:T(128)} %bitcast.14.prefix_ref, bf16[4,192,256]{2,1,0:T(8,128)(2,1)} %all_to_all.56.refs_0_, bf16[4,960,256]{2,1,0:T(8,128)(2,1)} %copy-done, bf16[4,192,256]{2,1,0:T(8,128)(2,1)} %all_to_all.58.refs_2_), custom_call_target="tpu_custom_call" | custom-call | tf_op jit(solution)/shard_map/pallas_call | solution.py:314
  526.4 19.6 %all_to_all.59 = bf16[4,576,256]{2,1,0:T(8,128)(2,1)S(1)} all-to-all(bf16[4,576,256]{2,1,0:T(8,128)(2,1)} %shard_map.370), channel_id=1, replica_groups=mesh['group'=2,'part'=4,'seq'=4] {'part'}, dimensions={0} | all-to-all | bytes 2359296 | tf_op jit(solution)/shard_map/all_to_all | solution.py:53
  546.2 3.3 multiply_reduce_fusion.2
  568.5 18.9 %reduce-scatter.7.cloned.1.call-done = bf16[192,4096]{1,0:T(8,128)(2,1)} async-done(((bf16[768,4096]{1,0:T(8,128)(2,1)}), bf16[192,4096]{1,0:T(8,128)(2,1)}) %reduce-scatter.7.cloned.1.call-update) | async-done | bytes 1572880 | tf_op jit(solution)/shard_map/reduce_scatter | solution.py:492
  587.5 3.2 fusion.56
  592.6 12.7 %all_to_all.60.refs_1_ = bf16[4,192,256]{2,1,0:T(8,128)(2,1)} all-to-all(bf16[4,192,256]{2,1,0:T(8,128)(2,1)S(1)} %bitcast.148), channel_id=1, replica_groups=mesh['group'=2,'part'=4,'seq'=4] {'part'}, dimensions={0} | all-to-all | bytes 786432 | tf_op jit(solution)/shard_map/all_to_all | solution.py:53
  605.4 19.8 %shard_map.371 = bf16[4,576,256]{2,1,0:T(8,128)(2,1)} custom-call(s32[1]{0:T(128)} %bitcast.14.prefix_ref, bf16[4,960,256]{2,1,0:T(8,128)(2,1)} %copy-done, bf16[4,192,256]{2,1,0:T(8,128)(2,1)} %all_to_all.60.refs_1_), custom_call_target="tpu_custom_call" | custom-call | tf_op jit(solution)/shard_map/pallas_call | solution.py:314
  626.1 3.9 all-to-all-start.8
  631.8 27.2 %all-to-all-done.8 = bf16[4,576,256]{2,1,0:T(8,128)(2,1)S(1)} async-done(((bf16[4,576,256]{2,1,0:T(8,128)(2,1)}), bf16[4,576,256]{2,1,0:T(8,128)(2,1)S(1)}, u32[]{:S(2)}, u32[]{:S(2)}) %all-to-all-start.8) | async-done | bytes 1179680 | tf_op jit(solution)/shard_map/all_to_all | solution.py:53
  659.0 4.1 multiply_reduce_fusion.3
  667.2 40.7 %reduce-scatter.9.cloned.1.call-done.refs_0_ = bf16[96,9472]{1,0:T(8,128)(2,1)} async-done(((bf16[768,9472]{1,0:T(8,128)(2,1)}), bf16[96,9472]{1,0:T(8,128)(2,1)}) %reduce-scatter.9.cloned.1.call-update) | async-done | bytes 1818640 | tf_op jit(solution)/shard_map/reduce_scatter | solution.py:530
  711.0 5.2 all-to-all-start.10
  722.3 28.6 %collective-permute-done.7 = bf16[256,768]{0,1:T(8,128)(2,1)S(1)} collective-permute-done((bf16[256,768]{0,1:T(8,128)(2,1)}, bf16[256,768]{0,1:T(8,128)(2,1)S(1)}, u32[]{:S(2)}, u32[]{:S(2)}) %collective-permute-start.7) | collective-permute-done | bytes 393248 | tf_op jit(solution)/shard_map/ppermute | solution.py:64
  752.1 18.2 %reduce-scatter.11.cloned.1.call-done.refs_0_ = bf16[96,3200]{1,0:T(8,128)(2,1)} async-done(((bf16[768,3200]{1,0:T(8,128)(2,1)}), bf16[96,3200]{1,0:T(8,128)(2,1)}) %reduce-scatter.11.cloned.1.call-update) | async-done | bytes 614416 | tf_op jit(solution)/shard_map/reduce_scatter | solution.py:552
  772.4 9.3 %all-to-all-start.9 = ((bf16[4,96,896]{2,1,0:T(8,128)(2,1)}), bf16[4,96,896]{2,1,0:T(8,128)(2,1)S(1)}, u32[]{:S(2)}, u32[]{:S(2)}) async-start(bf16[4,96,896]{2,1,0:T(8,128)(2,1)} %shard_map.372), calls=%async_computation.13 | async-start | bytes 1376256 | tf_op jit(solution)/shard_map/all_to_all | solution.py:53
  781.7 3.4 convert_bitcast_fusion
  789.6 7.4 all-to-all-done.9.terms_ref
  (248 shorter events, 116.3 us)
Async XLA Ops:
  14.9 7.1 copy-start.59
  14.9 7.1 copy-start.60
  14.9 7.9 copy-start.57
  15.0 7.9 copy-start.58
  15.0 58.1 %all-to-all-start = ((bf16[4,96,3136]{2,1,0:T(8,128)(2,1)}), bf16[4,96,3136]{2,1,0:T(8,128)(2,1)S(1)}, u32[]{:S(2)}, u32[]{:S(2)}) async-start(bf16[4,96,3136]{2,1,0:T(8,128)(2,1)} %shard_map.365), calls=%async_computation | async-start | bytes 4915200 | tf_op jit(solution)/shard_map/all_to_all | solution.py:53
  20.4 173.9 %all-gather.8.cloned.1.call-start = ((), (), s32[]{:S(2)}) async-start(), calls=%async_computation.15 | async-start | bytes 21897216 | tf_op jit(solution)/shard_map/all_gather | solution.py:127
  22.9 55.2 %copy-start.32 = (bf16[1,256,768]{2,1,0:T(8,128)(2,1)S(1)}, bf16[1,256,768]{2,1,0:T(8,128)(2,1)}, u32[]{:S(2)}) copy-start(bf16[1,256,768]{2,1,0:T(8,128)(2,1)} %param.22) | copy-start | bytes 1179652
  22.9 59.5 %copy-start.33 = (bf16[1,256,768]{2,1,0:T(8,128)(2,1)S(1)}, bf16[1,256,768]{2,1,0:T(8,128)(2,1)}, u32[]{:S(2)}) copy-start(bf16[1,256,768]{2,1,0:T(8,128)(2,1)} %param.23) | copy-start | bytes 1179652
  78.1 10.1 %copy-start.20 = (bf16[4016,192]{0,1:T(8,128)(2,1)S(1)}, bf16[4016,192]{0,1:T(8,128)(2,1)}, u32[]{:S(2)}) copy-start(bf16[4016,192]{0,1:T(8,128)(2,1)} %param.43) | copy-start | bytes 4626436
  78.1 235.3 %all-gather.10.cloned.1.call-start = ((), (), s32[]{:S(2)}) async-start(), calls=%async_computation.16 | async-start | bytes 7864320 | tf_op jit(solution)/shard_map/all_gather | solution.py:403
  78.4 48.9 %collective-permute-start.1 = (bf16[256,768]{0,1:T(8,128)(2,1)S(1)}, bf16[256,768]{0,1:T(8,128)(2,1)}, u32[]{:S(2)}, u32[]{:S(2)}) collective-permute-start(bf16[256,768]{0,1:T(8,128)(2,1)S(1)} %bitcast.146), channel_id=1, source_target_pairs={{0,0},{1,4},{2,8},{3,12},{4,1},{5,5},{6,9},{7,13},{8,2},{9,6},{10,... | collective-permute-start | bytes 1179656 | tf_op jit(solution)/shard_map/ppermute | solution.py:64
  82.6 44.7 %collective-permute-start.2 = (bf16[256,768]{0,1:T(8,128)(2,1)S(1)}, bf16[256,768]{0,1:T(8,128)(2,1)S(1)}, u32[]{:S(2)}, u32[]{:S(2)}) collective-permute-start(bf16[256,768]{0,1:T(8,128)(2,1)S(1)} %bitcast.147), channel_id=1, source_target_pairs={{0,0},{1,4},{2,8},{3,12},{4,1},{5,5},{6,9},{7,13},{8,2},{9,6},{10,... | collective-permute-start | bytes 1179656 | tf_op jit(solution)/shard_map/ppermute | solution.py:64
  84.5 16.6 %collective-permute-start = (s32[3,256]{1,0:T(4,128)S(1)}, s32[3,256]{1,0:T(4,128)S(1)}, u32[]{:S(2)}, u32[]{:S(2)}) collective-permute-start(s32[3,256]{1,0:T(4,128)S(1)} %add_add_fusion.4), channel_id=1, source_target_pairs={{0,0},{1,4},{2,8},{3,12},{4,1},{5,5},{6,9},{7,13},{8,2},{9,6},{10,... | collective-permute-start | bytes 9224 | tf_op jit(solution)/shard_map/ppermute | solution.py:64
  127.3 71.3 %copy-start.30 = (bf16[256,768]{0,1:T(8,128)(2,1)}, bf16[256,768]{0,1:T(8,128)(2,1)S(1)}, u32[]{:S(2)}) copy-start(bf16[256,768]{0,1:T(8,128)(2,1)S(1)} %collective-permute-done.2) | copy-start | bytes 1179652
  127.3 10.4 %collective-permute-start.3 = (bf16[256,768]{0,1:T(8,128)(2,1)}, bf16[256,768]{0,1:T(8,128)(2,1)}, u32[]{:S(2)}, u32[]{:S(2)}) collective-permute-start(bf16[256,768]{0,1:T(8,128)(2,1)} %bitcast.153), channel_id=1, source_target_pairs={{0,0},{1,4},{2,8},{3,12},{4,1},{5,5},{6,9},{7,13},{8,2},{9,6},{10,... | collective-permute-start | bytes 1179656 | tf_op jit(solution)/shard_map/ppermute | solution.py:64
  137.9 60.7 %copy-start.42 = (f32[256]{0:T(256)}, f32[256]{0:T(256)S(1)}, u32[]{:S(2)}) copy-start(f32[256]{0:T(256)S(1)} %multiply_reduce_fusion.10) | copy-start | bytes 3076
  137.9 60.7 %copy-start.40 = (f32[256]{0:T(256)}, f32[256]{0:T(256)S(1)}, u32[]{:S(2)}) copy-start(f32[256]{0:T(256)S(1)} %fusion.94) | copy-start | bytes 3076
  196.1 63.6 %copy-start.38 = (f32[768]{0:T(1024)}, f32[768]{0:T(1024)S(1)}, u32[]{:S(2)}) copy-start(f32[768]{0:T(1024)S(1)} %get-tuple-element.202) | copy-start | bytes 9220
  203.3 30.2 %all-to-all-start.1 = ((bf16[4,960,256]{2,1,0:T(8,128)(2,1)}), bf16[4,960,256]{2,1,0:T(8,128)(2,1)S(1)}, u32[]{:S(2)}, u32[]{:S(2)}) async-start(bf16[4,960,256]{2,1,0:T(8,128)(2,1)} %pad_maximum_fusion.2), calls=%async_computation.1 | async-start | bytes 3932160 | tf_op jit(solution)/shard_map/all_to_all | solution.py:53
  208.7 139.5 %all-gather.12.cloned.1.call-start = ((), (), s32[]{:S(2)}) async-start(), calls=%async_computation.17 | async-start | bytes 3538944 | tf_op jit(solution)/shard_map/all_gather | solution.py:461
  259.6 23.9 %copy-start.49 = (f32[256]{0:T(256)}, f32[256]{0:T(256)S(1)}, u32[]{:S(2)}) copy-start(f32[256]{0:T(256)S(1)} %get-tuple-element.226) | copy-start | bytes 3076
  259.6 34.9 %copy-start.28 = (f32[768,256]{1,0:T(8,128)}, f32[768,256]{1,0:T(8,128)S(1)}, u32[]{:S(2)}) copy-start(f32[768,256]{1,0:T(8,128)S(1)} %get-tuple-element.227) | copy-start | bytes 2359300
  259.7 23.8 %copy-start.47 = (f32[256]{0:T(256)}, f32[256]{0:T(256)S(1)}, u32[]{:S(2)}) copy-start(f32[256]{0:T(256)S(1)} %fusion.95) | copy-start | bytes 3076
  296.5 9.2 %copy-start.10 = (f32[768,256]{1,0:T(8,128)}, f32[768,256]{1,0:T(8,128)S(1)}, u32[]{:S(2)}) copy-start(f32[768,256]{1,0:T(8,128)S(1)} %get-tuple-element.229) | copy-start | bytes 2359300
  313.5 161.0 %reduce-scatter.5.cloned.1.call-start = ((), (), s32[]{:S(2)}) async-start(), calls=%async_computation.18 | async-start | bytes 3538944 | tf_op jit(solution)/shard_map/reduce_scatter | solution.py:480
  428.3 159.2 %reduce-scatter.7.cloned.1.call-start = ((), (), s32[]{:S(2)}) async-start(), calls=%async_computation.19 | async-start | bytes 7864320 | tf_op jit(solution)/shard_map/reduce_scatter | solution.py:492
  429.2 34.1 %collective-permute-start.4 = (bf16[256,768]{0,1:T(8,128)(2,1)S(1)}, bf16[256,768]{0,1:T(8,128)(2,1)S(1)}, u32[]{:S(2)}, u32[]{:S(2)}) collective-permute-start(bf16[256,768]{0,1:T(8,128)(2,1)S(1)} %copy-done.36), channel_id=1, source_target_pairs={{0,0},{1,4},{2,8},{3,12},{4,1},{5,5},{6,9},{7,13},{8,2},{9,6},{10,... | collective-permute-start | bytes 1179656 | tf_op jit(solution)/shard_map/ppermute | solution.py:64
  431.7 31.6 %collective-permute-start.5 = (f32[1,256]{1,0:T(1,128)S(1)}, f32[1,256]{1,0:T(1,128)S(1)}, u32[]{:S(2)}, u32[]{:S(2)}) collective-permute-start(f32[1,256]{1,0:T(1,128)S(1)} %bitcast.165), channel_id=1, source_target_pairs={{0,0},{1,4},{2,8},{3,12},{4,1},{5,5},{6,9},{7,13},{8,2},{9,6},{10,... | collective-permute-start | bytes 3080 | tf_op jit(solution)/shard_map/ppermute | solution.py:64
  463.4 11.1 %copy-start.34 = (bf16[256,768]{0,1:T(8,128)(2,1)}, bf16[256,768]{0,1:T(8,128)(2,1)S(1)}, u32[]{:S(2)}) copy-start(bf16[256,768]{0,1:T(8,128)(2,1)S(1)} %collective-permute-done.4) | copy-start | bytes 1179652
  463.4 11.1 %copy-start.55 = (f32[1,256]{1,0:T(1,128)}, f32[1,256]{1,0:T(1,128)S(1)}, u32[]{:S(2)}) copy-start(f32[1,256]{1,0:T(1,128)S(1)} %collective-permute-done.5) | copy-start | bytes 3076
  474.5 233.4 %reduce-scatter.9.cloned.1.call-start = ((), (), s32[]{:S(2)}) async-start(), calls=%async_computation.20 | async-start | bytes 16367616 | tf_op jit(solution)/shard_map/reduce_scatter | solution.py:530
  526.4 19.8 %copy-start.29 = (f32[768,256]{1,0:T(8,128)S(1)}, f32[768,256]{1,0:T(8,128)}, u32[]{:S(2)}) copy-start(f32[768,256]{1,0:T(8,128)} %copy-done.28) | copy-start | bytes 2359300
  526.4 19.8 %copy-start.39 = (f32[768]{0:T(1024)S(1)}, f32[768]{0:T(1024)}, u32[]{:S(2)}) copy-start(f32[768]{0:T(1024)} %copy-done.38) | copy-start | bytes 9220
  526.4 19.8 %copy-start.48 = (f32[256]{0:T(256)S(1)}, f32[256]{0:T(256)}, u32[]{:S(2)}) copy-start(f32[256]{0:T(256)} %copy-done.47) | copy-start | bytes 3076
  590.7 34.5 %collective-permute-start.6 = (bf16[256,768]{1,0:T(8,128)(2,1)}, bf16[256,768]{1,0:T(8,128)(2,1)S(1)}, u32[]{:S(2)}, u32[]{:S(2)}) collective-permute-start(bf16[256,768]{1,0:T(8,128)(2,1)} %fusion.56), channel_id=1, source_target_pairs={{0,0},{1,4},{2,8},{3,12},{4,1},{5,5},{6,9},{7,13},{8,2},{9,6},{10,... | collective-permute-start | bytes 1179656 | tf_op jit(solution)/shard_map/ppermute | solution.py:64
  605.3 24.8 %copy-start.46 = (bf16[768]{0:T(1024)(128)(2,1)S(1)}, bf16[768]{0:T(1024)(128)(2,1)}, u32[]{:S(2)}) copy-start(bf16[768]{0:T(1024)(128)(2,1)} %get-tuple-element.196) | copy-start | bytes 4612
  605.4 24.9 %copy-start.53 = (bf16[768]{0:T(1024)(128)(2,1)S(1)}, bf16[768]{0:T(1024)(128)(2,1)}, u32[]{:S(2)}) copy-start(bf16[768]{0:T(1024)(128)(2,1)} %get-tuple-element.194) | copy-start | bytes 4612
  605.4 24.9 %copy-start.54 = (bf16[768]{0:T(1024)(128)(2,1)S(1)}, bf16[768]{0:T(1024)(128)(2,1)}, u32[]{:S(2)}) copy-start(bf16[768]{0:T(1024)(128)(2,1)} %get-tuple-element.192) | copy-start | bytes 4612
  605.4 24.9 %copy-start.17 = (bf16[4,192,256]{2,1,0:T(8,128)(2,1)S(1)}, bf16[4,192,256]{2,1,0:T(8,128)(2,1)}, u32[]{:S(2)}) copy-start(bf16[4,192,256]{2,1,0:T(8,128)(2,1)} %copy-done.16) | copy-start | bytes 1179652
  625.2 33.9 %copy-start.41 = (f32[256]{0:T(256)S(1)}, f32[256]{0:T(256)}, u32[]{:S(2)}) copy-start(f32[256]{0:T(256)} %copy-done.40) | copy-start | bytes 3076
  626.1 32.9 %all-to-all-start.8 = ((bf16[4,576,256]{2,1,0:T(8,128)(2,1)}), bf16[4,576,256]{2,1,0:T(8,128)(2,1)S(1)}, u32[]{:S(2)}, u32[]{:S(2)}) async-start(bf16[4,576,256]{2,1,0:T(8,128)(2,1)} %shard_map.371), calls=%async_computation.9 | async-start | bytes 2359296 | tf_op jit(solution)/shard_map/all_to_all | solution.py:53
  630.0 140.3 %reduce-scatter.11.cloned.1.call-start = ((), (), s32[]{:S(2)}) async-start(), calls=%async_computation.21 | async-start | bytes 5529600 | tf_op jit(solution)/shard_map/reduce_scatter | solution.py:552
  708.0 8.2 %copy-start.43 = (f32[256]{0:T(256)S(1)}, f32[256]{0:T(256)}, u32[]{:S(2)}) copy-start(f32[256]{0:T(256)} %copy-done.42) | copy-start | bytes 3076
  711.0 61.3 %all-to-all-start.10 = ((bf16[4,96,2368]{2,1,0:T(8,128)(2,1)}), bf16[4,96,2368]{2,1,0:T(8,128)(2,1)S(1)}, u32[]{:S(2)}, u32[]{:S(2)}) async-start(bf16[4,96,2368]{2,1,0:T(8,128)(2,1)} %shard_map.374), calls=%async_computation.14 | async-start | bytes 3735552 | tf_op jit(solution)/shard_map/all_to_all | solution.py:53
  718.5 32.4 %collective-permute-start.7 = (bf16[256,768]{0,1:T(8,128)(2,1)}, bf16[256,768]{0,1:T(8,128)(2,1)S(1)}, u32[]{:S(2)}, u32[]{:S(2)}) collective-permute-start(bf16[256,768]{0,1:T(8,128)(2,1)} %fusion.85), channel_id=1, source_target_pairs={{0,0},{1,4},{2,8},{3,12},{4,1},{5,5},{6,9},{7,13},{8,2},{9,6},{10,... | collective-permute-start | bytes 1179656 | tf_op jit(solution)/shard_map/ppermute | solution.py:64
  772.4 12.8 %copy-start.4 = (bf16[4,96,2368]{2,1,0:T(8,128)(2,1)}, bf16[4,96,2368]{2,1,0:T(8,128)(2,1)S(1)}, u32[]{:S(2)}) copy-start(bf16[4,96,2368]{2,1,0:T(8,128)(2,1)S(1)} %all-to-all-done.10.terms_ref) | copy-start | bytes 5455876
  772.4 24.5 %all-to-all-start.9 = ((bf16[4,96,896]{2,1,0:T(8,128)(2,1)}), bf16[4,96,896]{2,1,0:T(8,128)(2,1)S(1)}, u32[]{:S(2)}, u32[]{:S(2)}) async-start(bf16[4,96,896]{2,1,0:T(8,128)(2,1)} %shard_map.372), calls=%async_computation.13 | async-start | bytes 1376256 | tf_op jit(solution)/shard_map/all_to_all | solution.py:53
  781.7 19.5 %copy-start.56 = (f32[1,256]{1,0:T(1,128)S(1)}, f32[1,256]{1,0:T(1,128)}, u32[]{:S(2)}) copy-start(f32[1,256]{1,0:T(1,128)} %copy-done.55) | copy-start | bytes 3076
  (35 other events, 120.2 us)
Sparse Core Ops, SparseCore 0:
  78.2 116.0 all-gather.7
  195.9 116.9 all-gather.9
  314.8 33.3 all-gather.11
  428.4 46.0 reduce-scatter.4
  476.6 110.7 reduce-scatter.6
  590.9 116.9 reduce-scatter.8
  711.5 58.7 reduce-scatter.10

commit v2 on v1

--- a/solution.py
+++ b/solution.py
@@ -91,40 +91,27 @@
 every = slice(None)
 
 
-def exchange(shards):
-    n_seq = lax.axis_size("seq")
-    rows = shards[0].shape[0]
-    sizes = [shard.shape[1] for shard in shards]
-    starts = edges(sizes)
-    moves = [
-        (at, (every, every), 0, (block, every, slice(starts[at], starts[at + 1])))
-        for at in range(len(shards))
-        for block in range(n_seq)
-    ]
-    (copies,) = move(shards, [(n_seq, rows, starts[-1])], moves)
-    return swap(copies, "seq")
-
-
-def fetch(parts, sizes, extra):
-    n_seq, rows, unused = parts.shape
-    starts = edges(sizes)
-    moves = [
-        (
-            0,
-            (block, every, slice(starts[at], starts[at + 1])),
-            0,
-            (every, slice(low, low + sizes[at])),
-        )
-        for at in range(len(sizes))
-        for block in range(n_seq)
-        for low in [n_seq * starts[at] + block * sizes[at]]
-    ]
-    width = n_seq * starts[-1]
-    if extra is not None:
-        moves.append((1, (every, every), 0, (every, slice(width, width + extra.shape[1]))))
-        width += extra.shape[1]
-    (full,) = move([parts] if extra is None else [parts, extra], [(rows, width)], moves)
-    return lax.all_gather(full, dp, axis=0, tiled=True)
+def gather_kernel(full_ref, *refs, pieces):
+    for ref, (start, size, copies) in zip(refs, pieces):
+        for block in range(copies):
+            ref[:, block * size : (block + 1) * size] = full_ref[block, :, start : start + size]
+
+
+def matrices(full, lanes, pieces):
+    n_seq, rows, unused = full.shape
+    return pl.pallas_call(
+        functools.partial(gather_kernel, pieces=pieces),
+        grid=(rows // LANES,),
+        in_specs=[pl.BlockSpec((n_seq, LANES, lanes), lambda step: (0, step, 0))],
+        out_specs=[
+            pl.BlockSpec((LANES, size * copies), lambda step: (step, 0))
+            for start, size, copies in pieces
+        ],
+        out_shape=[
+            jax.ShapeDtypeStruct((rows, size * copies), jnp.bfloat16)
+            for start, size, copies in pieces
+        ],
+    )(full)
 
 
 def deliver(terms, sizes, extra, out_sizes):
@@ -365,43 +352,51 @@
     low = jnp.bfloat16
 
     gains = jnp.stack([self_gain, cross_gain, feed_gain, exit_gain], axis=1)
-    gains = jnp.pad(gains, ((0, 0), (0, GAIN_LANES - gains.shape[1])))
+    early = -(-(5 * own + 4) // LANES) * LANES
+    gains = jnp.pad(gains, ((0, 0), (0, early - 5 * own - 4)))
     folded = jnp.pad(feed_down, ((0, folds * own_rows - fold_rows), (0, 0)))
-    parts = exchange(
+    shards = [
+        self_query,
+        self_key,
+        self_value,
+        cross_key,
+        cross_value,
+        gains,
+        self_output,
+        cross_query,
+        cross_output,
+        feed_gate,
+        feed_up,
+    ] + [folded[fold * own_rows : (fold + 1) * own_rows] for fold in range(folds)]
+    starts = edges([shard.shape[1] for shard in shards])
+    (flat,) = move(
+        shards,
+        [(own_rows, starts[-1])],
         [
-            jnp.concatenate([self_query, self_key, self_value], axis=1),
-            self_output,
-            cross_query,
-            jnp.concatenate([cross_key, cross_value], axis=1),
-            cross_output,
-            feed_gate,
-            feed_up,
-        ]
-        + [folded[fold * own_rows : (fold + 1) * own_rows] for fold in range(folds)]
-    )
-    self_sizes = (3 * own, own)
-    rest_sizes = (own, 2 * own, own, own_feed, own_feed) + (own,) * folds
+            (at, (every, every), 0, (every, slice(starts[at], starts[at + 1])))
+            for at in range(len(shards))
+        ],
+    )
+    full = lax.all_gather(flat, ("seq",) + dp, axis=0, tiled=True).reshape(n_seq, width, -1)
+    self_qkv, cross_kv, gain_columns = matrices(
+        full,
+        early,
+        ((0, 3 * own, n_seq), (3 * own, 2 * own, n_seq), (5 * own, early - 5 * own, 1)),
+    )
+    rest_sizes = (own, 2 * own, own, own, own_feed, own_feed) + (own,) * folds
 
     marks = jnp.concatenate(
         [exit_flags, target_ids, jnp.broadcast_to(prefix_len[:, None], exit_flags.shape)], axis=0
     )
-    parts, marks, hidden, states, cotangent = lax.optimization_barrier(
-        (parts, marks, hidden_in, encoder_in, out_cotangent.astype(low))
-    )
-    weights = fetch(parts, self_sizes + rest_sizes, gains)
-    self_qkv, self_out, cross_q, cross_kv, cross_out, gate_full, up_full, *downs = cut(
-        weights, tuple(n_seq * size for size in self_sizes + rest_sizes) + (GAIN_LANES,)
-    )
-    gain_columns = downs.pop()
-    hidden = relocate(hidden.reshape(-1, width))
-    states = relocate(states.reshape(-1, width))
+    hidden = relocate(hidden_in.reshape(-1, width))
+    states = relocate(encoder_in.reshape(-1, width))
     marks = relocate(marks)
     prefix_len = marks[2, :1]
     marks = lax.all_gather(marks[:2], dp, axis=0)
     shard = jnp.pad(embedding.T, ((0, 0), (0, vocab_lanes - vocab_rows)))
     shard, marks, hidden, states = lax.optimization_barrier((shard, marks, hidden, states))
     table = lax.all_gather(shard, "seq", axis=0, tiled=True)
-    cotangent = relocate(cotangent.reshape(-1, width))
+    cotangent = relocate(out_cotangent.reshape(-1, width).astype(low))
     gain_one, gain_two, gain_three, gain_exit = gain_columns[:, :4].astype(jnp.float32).T
 
     def blocks(rows):
@@ -426,16 +421,20 @@
     residual_in, states = rows_first(residual_in), rows_first(states)
     cotangent = rows_first(cotangent)
     normed_one = norm_columns(residual_in, gain_one).astype(low)
-    attended = swap(
-        jnp.concatenate(
-            [
-                blocks(contract(self_qkv, normed_one, 0, 0)),
-                blocks(contract(cross_kv, states, 0, 0)),
-            ],
-            axis=1,
+    attended = jnp.concatenate(
+        [blocks(contract(self_qkv, normed_one, 0, 0)), blocks(contract(cross_kv, states, 0, 0))],
+        axis=1,
+    )
+    attended, full = lax.optimization_barrier((attended, full))
+    attended = swap(attended, "part")
+    self_out, cross_q, cross_out, gate_full, up_full, *downs = matrices(
+        full,
+        starts[-1],
+        tuple(
+            (starts[at], starts[at + 1] - starts[at], n_seq) for at in range(6, len(shards))
         ),
-        "part",
-    )
+    )
+    attended, self_out = lax.optimization_barrier((attended, self_out))
     self_places = ((0, 0), (0, own), (0, 2 * own))
     mixture_one = swap(attend(prefix_len, [attended], self_places, own, True), "part")
     mixture_one = mixture_one.reshape(width, token_count)
@@ -510,20 +509,21 @@
     q_grad = cross_grads[:, :own].reshape(-1, token_count)
     kv_grad = cross_grads[:, own:].reshape(-1, token_count)
     encoder_grad = relocate(contract(kv_grad, cross_kv, 0, 1).astype(low)).astype(jnp.float32)
+    self_grad, full_cross_gain = norm_back(after_self, gain_two, contract(cross_q, q_grad, 1, 0))
+    self_grad = self_grad + cross_grad
+    branch_one = self_grad.astype(low)
     rest_terms = jnp.concatenate(
         [
             contract(normed_two, q_grad, 1, 1).astype(low),
             contract(states, kv_grad, 1, 1).astype(low),
             contract(mixture_two, branch_two, 1, 1).astype(low),
+            contract(mixture_one, branch_one, 1, 1).astype(low),
             contract(normed_three, gate_grad, 1, 1).astype(low),
             contract(normed_three, up_grad, 1, 1).astype(low),
         ]
         + [contract(hidden, branch_three, 1, 1).astype(low) for hidden in hidden_folds],
         axis=1,
     )
-    self_grad, full_cross_gain = norm_back(after_self, gain_two, contract(cross_q, q_grad, 1, 0))
-    self_grad = self_grad + cross_grad
-    branch_one = self_grad.astype(low)
     mixture_one_grad = blocks(contract(self_out, branch_one, 1, 0))
     mixture_one_grad, rest_terms = lax.optimization_barrier((mixture_one_grad, rest_terms))
     rest_terms, table_sums = lax.optimization_barrier((rest_terms, table_sums))
@@ -543,7 +543,6 @@
     self_terms = jnp.concatenate(
         [
             contract(normed_one, qkv_grad, 1, 1).astype(low),
-            contract(mixture_one, branch_one, 1, 1).astype(low),
             gain_terms,
         ],
         axis=1,
@@ -556,13 +555,14 @@
         cross_key_grad,
         cross_value_grad,
         cross_output_grad,
+        self_output_grad,
         feed_gate_grad,
         feed_up_grad,
         *down_sums,
-    ) = deliver(rest_terms, rest_sizes, 0, (own,) * 4 + rest_sizes[3:])
+    ) = deliver(rest_terms, rest_sizes, 0, (own,) * 5 + rest_sizes[4:])
     down_grad = jnp.concatenate(down_sums, axis=0)[:fold_rows]
-    self_query_grad, self_key_grad, self_value_grad, self_output_grad, gain_sums = deliver(
-        self_terms, self_sizes, GAIN_LANES, (own,) * 4 + (GAIN_LANES,)
+    self_query_grad, self_key_grad, self_value_grad, gain_sums = deliver(
+        self_terms, (3 * own,), GAIN_LANES, (own,) * 3 + (GAIN_LANES,)
     )
     gain_sums = gain_sums[:, :4].T
     return (

time: 824 us -> 803 us (0.975)
  waiting for transfers between devices: 314 us -> 283 us
  matrix products: 119 us -> 92.3 us
  Pallas kernels: 135 us -> 151 us
  blocking collectives: 111 us -> 124 us
    all_to_all x5 -> x4, waiting for transfers between devices: 109 us -> 44.6 us  [swap(): return lax.all_to_all(pieces, axis, 0, 0, tiled=True)]
    dot_general x32, matrix products: 119 us -> 92.3 us  [contract(): lax.dot_general(first_op, second_op, (((first_dim,), (second_dim,)), ((),...]
    pallas_call x0 -> x2, Pallas kernels: none -> 20.6 us  [matrices(): pl.pallas_call(functools.partial(gather_kernel, pieces=pieces), grid=(row...]
    all_gather x1, waiting for transfers between devices: 56.4 us -> 74.9 us  [per_device(): lax.all_gather(flat, ('seq',) + dp, axis=0, tiled=True)]
    ppermute x8, waiting for transfers between devices: 46.2 us -> 60.8 us  [relocate(): return lax.ppermute(block, ('group', 'part', 'seq'), pairs)]
    all_gather x1, blocking collectives: 26.1 us -> 39.5 us  [per_device(): marks = lax.all_gather(marks[:2], dp, axis=0)]
    reduce_scatter x1, waiting for transfers between devices: 18.2 us -> 6.11 us  [per_device(): lax.psum_scatter(self_terms, dp, scatter_dimension=0, tiled=True)]
    unnamed x133 -> x181, local copies, waits for them, and re-layouts: 15.4 us -> 19.7 us
  transfers between devices with their start and end apart: 20 -> 19, of which waited for: 13 -> 12; matrix products, arithmetic and copies ran while one was open for 19% -> 16% of each run, Pallas kernels for 9% -> 11%
where the time goes in v2:
time: 803 us; the launch traced here: 789 us
  waiting for transfers between devices  283 us (35%)
  Pallas kernels  151 us (19%)
  blocking collectives  124 us (15%)
  matrix products  92.3 us (11%)
  starting transfers between devices  56.1 us (7%)
  local copies, waits for them, and re-layouts  33.8 us (4%)
  other arithmetic  31.8 us (4%)
  between operations  16.1 us (2%)
    dot_general x32, matrix products, contract(): lax.dot_general(first_op, second_op, (((first_dim,), (second_dim,)), ((),...  92.3 us
    all_to_all x6, blocking collectives, swap(): return lax.all_to_all(pieces, axis, 0, 0, tiled=True)  75.5 us
    all_gather x1, waiting for transfers between devices, per_device(): lax.all_gather(flat, ('seq',) + dp, axis=0, tiled=True)  74.9 us
    ppermute x8, waiting for transfers between devices, relocate(): return lax.ppermute(block, ('group', 'part', 'seq'), pairs)  60.8 us
    pallas_call x1, Pallas kernels, exit_rows(): pl.pallas_call(functools.partial(exit_kernel, rows=rows), grid=(count //...  57.3 us
    reduce_scatter x1, waiting for transfers between devices, per_device(): lax.psum_scatter(rest_terms, dp, scatter_dimension=0, tiled=True)  47.9 us
    all_to_all x4, waiting for transfers between devices, swap(): return lax.all_to_all(pieces, axis, 0, 0, tiled=True)  44.6 us
    all_gather x1, blocking collectives, per_device(): marks = lax.all_gather(marks[:2], dp, axis=0)  39.5 us
  transfers between devices with their start and end apart: 19, of which 12 were waited for; matrix products, arithmetic and copies ran while one was open for 16% of the time, Pallas kernels for 11%

profile of v2, /device:TPU:8, one launch (start us, length us, event | category | flops | bytes accessed | tf_op | source)
XLA Modules:
  0.0 788.8 jit_solution(5706041720277087412)
XLA Ops:
  15.1 3.6 collective-permute-start.2
  22.8 14.5 %collective-permute-done = s32[3,256]{1,0:T(4,128)S(1)} collective-permute-done((s32[3,256]{1,0:T(4,128)S(1)}, s32[3,256]{1,0:T(4,128)S(1)}, u32[]{:S(2)}, u32[]{:S(2)}) %collective-permute-start) | collective-permute-done | bytes 3104 | tf_op jit(solution)/shard_map/ppermute | solution.py:64
  37.3 39.5 %all-gather.2 = s32[8,2,256]{2,1,0:T(2,128)} all-gather(s32[1,2,256]{2,1,0:T(2,128)S(1)} %slice_bitcast_fusion.1), channel_id=2, replica_groups=mesh['group'=2,'part'=4,'seq'=4] {'group','part'}, dimensions={0}, use_global_device_ids=true | all-gather | bytes 18432 | tf_op jit(solution)/shard_map/all_gather | solution.py:395
  77.0 5.6 collective-permute-start.3
  83.6 13.0 %collective-permute-done.3 = bf16[256,768]{0,1:T(8,128)(2,1)} collective-permute-done((bf16[256,768]{0,1:T(8,128)(2,1)S(1)}, bf16[256,768]{0,1:T(8,128)(2,1)}, u32[]{:S(2)}, u32[]{:S(2)}) %collective-permute-start.3) | collective-permute-done | bytes 393248 | tf_op jit(solution)/shard_map/ppermute | solution.py:64
  96.8 74.9 %all-gather.8.cloned.1.call-done = bf16[3072,3200]{1,0:T(8,128)(2,1)} async-done(((bf16[96,3200]{1,0:T(8,128)(2,1)}), bf16[3072,3200]{1,0:T(8,128)(2,1)}) %all-gather.8.cloned.1.call-update) | async-done | bytes 19660816 | tf_op jit(solution)/shard_map/all_gather | solution.py:380
  171.7 7.3 shard_map.366
  180.8 2.9 convolution_convert_fusion.5
  186.8 3.6 all-to-all-start
  191.0 13.3 %shard_map.367 = (bf16[768,768]{1,0:T(8,128)(2,1)}, bf16[768,768]{1,0:T(8,128)(2,1)}, bf16[768,768]{1,0:T(8,128)(2,1)}, bf16[768,2048]{1,0:T(8,128)(2,1)}, bf16[...) custom-call(bf16[4,768,3200]{2,1,0:T(8,128)(2,1)} %bitcast.145), custom_call_target="tpu_custom_call" | custom-call | tf_op jit(solution)/shard_map/pallas_call | solution.py:102
  204.3 10.4 %all-to-all-done.refs_0_.refs_1_ = bf16[4,960,256]{2,1,0:T(8,128)(2,1)S(1)} async-done(((bf16[4,960,256]{2,1,0:T(8,128)(2,1)}), bf16[4,960,256]{2,1,0:T(8,128)(2,1)S(1)}, u32[]{:S(2)}, u32[]{:S(2)}) %all-to-all-start) | async-done | bytes 1966112 | tf_op jit(solution)/shard_map/all_to_all | solution.py:53
  216.0 11.5 %shard_map.368 = bf16[4,192,256]{2,1,0:T(8,128)(2,1)} custom-call(s32[1]{0:T(128)} %bitcast.18.prefix_ref, bf16[4,960,256]{2,1,0:T(8,128)(2,1)} %copy-done), custom_call_target="tpu_custom_call" | custom-call | tf_op jit(solution)/shard_map/pallas_call | solution.py:289
  227.5 11.0 %all_to_all.50 = bf16[4,192,256]{2,1,0:T(8,128)(2,1)S(1)} all-to-all(bf16[4,192,256]{2,1,0:T(8,128)(2,1)} %shard_map.368), channel_id=1, replica_groups=mesh['group'=2,'part'=4,'seq'=4] {'part'}, dimensions={0} | all-to-all | bytes 786432 | tf_op jit(solution)/shard_map/all_to_all | solution.py:53
  241.7 10.6 %all_to_all.51.refs_0_ = bf16[4,192,256]{2,1,0:T(8,128)(2,1)} all-to-all(bf16[4,192,256]{2,1,0:T(8,128)(2,1)S(1)} %bitcast.177), channel_id=1, replica_groups=mesh['group'=2,'part'=4,'seq'=4] {'part'}, dimensions={0} | all-to-all | bytes 786432 | tf_op jit(solution)/shard_map/all_to_all | solution.py:53
  252.3 11.2 %shard_map.369 = bf16[4,192,256]{2,1,0:T(8,128)(2,1)} custom-call(s32[1]{0:T(128)} %bitcast.18.prefix_ref, bf16[4,192,256]{2,1,0:T(8,128)(2,1)} %all_to_all.51.refs_0_, bf16[4,960,256]{2,1,0:T(8,128)(2,1)} %copy-done), custom_call_target="tpu_custom_call" | custom-call | tf_op jit(solution)/shard_map/pallas_call | solution.py:289
  263.4 11.1 %all_to_all.52 = bf16[4,192,256]{2,1,0:T(8,128)(2,1)S(1)} all-to-all(bf16[4,192,256]{2,1,0:T(8,128)(2,1)} %shard_map.369), channel_id=1, replica_groups=mesh['group'=2,'part'=4,'seq'=4] {'part'}, dimensions={0} | all-to-all | bytes 786432 | tf_op jit(solution)/shard_map/all_to_all | solution.py:53
  278.5 2.7 multiply_convert_fusion
  289.8 19.7 %fusion.23 = bf16[2048,768]{1,0:T(8,128)(2,1)} fusion(bf16[768,4096]{1,0:T(8,128)(2,1)} %all-gather.10.cloned.1.call-done.table_ref, s32[2048]{0:T(1024)S(1)} %bitcast.188, pred[2048]{0:T(1024)(128)(4,1)S(1)} %broadcast_compare_fusion), kind=kOutput, calls=%fused_computation.29 | convolution fusion | flops 12903251968 | bytes 9447424 | tf_op jit(solution)/shard_map/dot_general | solution.py:23
  309.5 11.4 %all-gather.12.cloned.1.call-done.token_ref = bf16[2048,768]{1,0:T(8,128)(2,1)} async-done(((bf16[256,768]{1,0:T(8,128)(2,1)}), bf16[2048,768]{1,0:T(8,128)(2,1)}) %all-gather.12.cloned.1.call-update) | async-done | bytes 3145744 | tf_op jit(solution)/shard_map/all_gather | solution.py:460
  320.9 57.3 %shard_map.370 = (bf16[2048,4096]{1,0:T(8,128)(2,1)}, f32[2048,768]{1,0:T(8,128)}, f32[2048,128]{1,0:T(8,128)}) custom-call(bf16[2048,768]{1,0:T(8,128)(2,1)} %all-gather.12.cloned.1.call-done.token_ref, bf16[768,4096]{1,0:T(8,128)(2,1)} %all-gather.10.cloned.1.call-done.table_ref), custom_call_target="tpu_custom_call" | custom-call | tf_op jit(solution)/shard_map/pallas_call | solution.py:265
  378.2 3.8 fusion.16
  382.9 9.3 %all-gather.3 = f32[8,3,2048]{2,1,0:T(4,128)S(1)} all-gather(f32[1,3,2048]{2,1,0:T(4,128)S(1)} %maximum_bitcast_fusion), channel_id=3, replica_groups=mesh['group'=2,'part'=4,'seq'=4] {'group','part'}, dimensions={0}, use_global_device_ids=true | all-gather | bytes 221184 | tf_op jit(solution)/shard_map/all_gather | solution.py:470
  394.4 2.4 multiply_reduce_fusion
  397.3 4.5 fusion.18
  401.9 2.4 collective-permute-start.4
  405.7 3.1 collective-permute-start.5
  408.8 28.4 %fusion.13 = bf16[768,4096]{1,0:T(8,128)(2,1)} fusion(bf16[2048,768]{1,0:T(8,128)(2,1)} %all-gather.12.cloned.1.call-done.token_ref, bf16[2048,4096]{1,0:T(8,128)(2,1)} %get-tuple-element.102, f32[2048]{0:T(1024)S(1)} %bitcast.182, f32[2048]{0:T(1024)} %copy-done.54, s32[2048]{0:T(1024)} %bitcast.189, pred[2048]{0:T(1024)(128)(4,1)} %copy-done.76), kind=kOutput, calls=%fused_computation.16 | convolution fusion | flops 12946767872 | bytes 26241024 | tf_op jit(solution)/shard_map/dot_general | solution.py:23
  437.3 10.8 %reduce-scatter.5.cloned.1.call-done = bf16[256,768]{1,0:T(8,128)(2,1)} async-done(((bf16[2048,768]{1,0:T(8,128)(2,1)}), bf16[256,768]{1,0:T(8,128)(2,1)}) %reduce-scatter.5.cloned.1.call-update) | async-done | bytes 393232 | tf_op jit(solution)/shard_map/reduce_scatter | solution.py:479
  465.5 10.5 %all_to_all.53.refs_2_ = bf16[4,192,256]{2,1,0:T(8,128)(2,1)} all-to-all(bf16[4,192,256]{2,1,0:T(8,128)(2,1)S(1)} %bitcast.167), channel_id=1, replica_groups=mesh['group'=2,'part'=4,'seq'=4] {'part'}, dimensions={0} | all-to-all | bytes 786432 | tf_op jit(solution)/shard_map/all_to_all | solution.py:53
  476.0 18.7 %shard_map.371 = bf16[4,576,256]{2,1,0:T(8,128)(2,1)} custom-call(s32[1]{0:T(128)} %bitcast.18.prefix_ref, bf16[4,192,256]{2,1,0:T(8,128)(2,1)} %all_to_all.51.refs_0_, bf16[4,960,256]{2,1,0:T(8,128)(2,1)} %copy-done, bf16[4,192,256]{2,1,0:T(8,128)(2,1)} %all_to_all.53.refs_2_), custom_call_target="tpu_custom_call" | custom-call | tf_op jit(solution)/shard_map/pallas_call | solution.py:301
  494.6 19.6 %all_to_all.54 = bf16[4,576,256]{2,1,0:T(8,128)(2,1)S(1)} all-to-all(bf16[4,576,256]{2,1,0:T(8,128)(2,1)} %shard_map.371), channel_id=1, replica_groups=mesh['group'=2,'part'=4,'seq'=4] {'part'}, dimensions={0} | all-to-all | bytes 2359296 | tf_op jit(solution)/shard_map/all_to_all | solution.py:53
  522.4 2.7 fusion.21
  525.2 2.7 fusion.20
  534.4 26.6 %reduce-scatter.7.cloned.1.call-done = bf16[192,4096]{1,0:T(8,128)(2,1)} async-done(((bf16[768,4096]{1,0:T(8,128)(2,1)}), bf16[192,4096]{1,0:T(8,128)(2,1)}) %reduce-scatter.7.cloned.1.call-update) | async-done | bytes 1572880 | tf_op jit(solution)/shard_map/reduce_scatter | solution.py:491
  561.1 2.5 convolution_convert_fusion.12
  565.5 12.8 %all_to_all.55.refs_1_ = bf16[4,192,256]{2,1,0:T(8,128)(2,1)} all-to-all(bf16[4,192,256]{2,1,0:T(8,128)(2,1)S(1)} %bitcast.164), channel_id=1, replica_groups=mesh['group'=2,'part'=4,'seq'=4] {'part'}, dimensions={0} | all-to-all | bytes 786432 | tf_op jit(solution)/shard_map/all_to_all | solution.py:53
  578.3 19.8 %shard_map.372 = bf16[4,576,256]{2,1,0:T(8,128)(2,1)} custom-call(s32[1]{0:T(128)} %bitcast.18.prefix_ref, bf16[4,960,256]{2,1,0:T(8,128)(2,1)} %copy-done, bf16[4,192,256]{2,1,0:T(8,128)(2,1)} %all_to_all.55.refs_1_), custom_call_target="tpu_custom_call" | custom-call | tf_op jit(solution)/shard_map/pallas_call | solution.py:301
  599.0 3.9 all-to-all-start.7
  604.9 27.1 %all-to-all-done.7 = bf16[4,576,256]{2,1,0:T(8,128)(2,1)S(1)} async-done(((bf16[4,576,256]{2,1,0:T(8,128)(2,1)}), bf16[4,576,256]{2,1,0:T(8,128)(2,1)S(1)}, u32[]{:S(2)}, u32[]{:S(2)}) %all-to-all-start.7) | async-done | bytes 1179680 | tf_op jit(solution)/shard_map/all_to_all | solution.py:53
  632.0 3.8 multiply_reduce_fusion.3
  639.9 47.9 %reduce-scatter.9.cloned.1.call-done.refs_0_ = bf16[96,10240]{1,0:T(8,128)(2,1)} async-done(((bf16[768,10240]{1,0:T(8,128)(2,1)}), bf16[96,10240]{1,0:T(8,128)(2,1)}) %reduce-scatter.9.cloned.1.call-update) | async-done | bytes 1966096 | tf_op jit(solution)/shard_map/reduce_scatter | solution.py:530
  687.8 3.3 shard_map.375
  691.2 5.3 all-to-all-start.9
  699.6 33.3 %collective-permute-done.7 = bf16[256,768]{0,1:T(8,128)(2,1)S(1)} collective-permute-done((bf16[256,768]{0,1:T(8,128)(2,1)S(1)}, bf16[256,768]{0,1:T(8,128)(2,1)S(1)}, u32[]{:S(2)}, u32[]{:S(2)}) %collective-permute-start.7) | collective-permute-done | bytes 393248 | tf_op jit(solution)/shard_map/ppermute | solution.py:64
  734.1 6.1 reduce-scatter.11.cloned.1.call-done.refs_0_
  742.3 20.5 %all-to-all-start.8 = ((bf16[4,96,704]{2,1,0:T(8,128)(2,1)}), bf16[4,96,704]{2,1,0:T(8,128)(2,1)S(1)}, u32[]{:S(2)}, u32[]{:S(2)}) async-start(bf16[4,96,704]{2,1,0:T(8,128)(2,1)} %shard_map.373), calls=%async_computation.12 | async-start | bytes 1179648 | tf_op jit(solution)/shard_map/all_to_all | solution.py:53
  764.7 2.7 shard_map.376
  769.2 7.1 all-to-all-done.8.terms_ref
  (291 shorter events, 96.2 us)
Async XLA Ops:
  7.2 5.6 copy-start.45
  7.2 7.7 copy-start.46
  7.2 12.3 %copy-start.79 = (s32[1,256]{1,0:T(1,128)S(1)}, s32[1,256]{1,0:T(1,128)}, u32[]{:S(2)}) copy-start(s32[1,256]{1,0:T(1,128)} %param.26) | copy-start | bytes 3076
  7.2 12.3 %copy-start.80 = (s32[1,256]{1,0:T(1,128)S(1)}, s32[1,256]{1,0:T(1,128)}, u32[]{:S(2)}) copy-start(s32[1,256]{1,0:T(1,128)} %param.25) | copy-start | bytes 3076
  7.2 14.3 %copy-start.37 = (bf16[4016,192]{0,1:T(8,128)(2,1)S(1)}, bf16[4016,192]{0,1:T(8,128)(2,1)}, u32[]{:S(2)}) copy-start(bf16[4016,192]{0,1:T(8,128)(2,1)} %param.43) | copy-start | bytes 4626436
  7.2 164.5 %all-gather.8.cloned.1.call-start = ((), (), s32[]{:S(2)}) async-start(), calls=%async_computation.14 | async-start | bytes 20275200 | tf_op jit(solution)/shard_map/all_gather | solution.py:380
  12.8 274.8 %all-gather.10.cloned.1.call-start = ((), (), s32[]{:S(2)}) async-start(), calls=%async_computation.15 | async-start | bytes 7864320 | tf_op jit(solution)/shard_map/all_gather | solution.py:398
  13.0 63.8 %collective-permute-start.1 = (bf16[256,768]{0,1:T(8,128)(2,1)S(1)}, bf16[256,768]{0,1:T(8,128)(2,1)}, u32[]{:S(2)}, u32[]{:S(2)}) collective-permute-start(bf16[256,768]{0,1:T(8,128)(2,1)S(1)} %bitcast.175), channel_id=1, source_target_pairs={{0,0},{1,4},{2,8},{3,12},{4,1},{5,5},{6,9},{7,13},{8,2},{9,6},{10,... | collective-permute-start | bytes 1179656 | tf_op jit(solution)/shard_map/ppermute | solution.py:64
  15.1 61.7 %collective-permute-start.2 = (bf16[256,768]{0,1:T(8,128)(2,1)S(1)}, bf16[256,768]{0,1:T(8,128)(2,1)S(1)}, u32[]{:S(2)}, u32[]{:S(2)}) collective-permute-start(bf16[256,768]{0,1:T(8,128)(2,1)S(1)} %bitcast.176), channel_id=1, source_target_pairs={{0,0},{1,4},{2,8},{3,12},{4,1},{5,5},{6,9},{7,13},{8,2},{9,6},{10,... | collective-permute-start | bytes 1179656 | tf_op jit(solution)/shard_map/ppermute | solution.py:64
  19.6 17.7 %collective-permute-start = (s32[3,256]{1,0:T(4,128)S(1)}, s32[3,256]{1,0:T(4,128)S(1)}, u32[]{:S(2)}, u32[]{:S(2)}) collective-permute-start(s32[3,256]{1,0:T(4,128)S(1)} %add_add_fusion.4), channel_id=1, source_target_pairs={{0,0},{1,4},{2,8},{3,12},{4,1},{5,5},{6,9},{7,13},{8,2},{9,6},{10,... | collective-permute-start | bytes 9224 | tf_op jit(solution)/shard_map/ppermute | solution.py:64
  21.5 55.3 %copy-start.41 = (f32[1,256,768]{2,1,0:T(8,128)S(1)}, f32[1,256,768]{2,1,0:T(8,128)}, u32[]{:S(2)}) copy-start(f32[1,256,768]{2,1,0:T(8,128)} %param.27) | copy-start | bytes 2359300
  76.8 104.0 %copy-start.43 = (bf16[256,768]{0,1:T(8,128)(2,1)}, bf16[256,768]{0,1:T(8,128)(2,1)S(1)}, u32[]{:S(2)}) copy-start(bf16[256,768]{0,1:T(8,128)(2,1)S(1)} %collective-permute-done.2) | copy-start | bytes 1179652
  77.0 19.6 %collective-permute-start.3 = (bf16[256,768]{0,1:T(8,128)(2,1)S(1)}, bf16[256,768]{0,1:T(8,128)(2,1)}, u32[]{:S(2)}, u32[]{:S(2)}) collective-permute-start(bf16[256,768]{0,1:T(8,128)(2,1)S(1)} %bitcast.178), channel_id=1, source_target_pairs={{0,0},{1,4},{2,8},{3,12},{4,1},{5,5},{6,9},{7,13},{8,2},{9,6},{10,... | collective-permute-start | bytes 1179656 | tf_op jit(solution)/shard_map/ppermute | solution.py:64
  96.8 82.2 %copy-start.65 = (f32[256]{0:T(256)}, f32[256]{0:T(256)S(1)}, u32[]{:S(2)}) copy-start(f32[256]{0:T(256)S(1)} %multiply_reduce_fusion.10) | copy-start | bytes 3076
  96.8 87.0 %copy-start.58 = (f32[256]{0:T(256)}, f32[256]{0:T(256)S(1)}, u32[]{:S(2)}) copy-start(f32[256]{0:T(256)S(1)} %fusion.59) | copy-start | bytes 3076
  180.8 59.6 %copy-start.50 = (f32[768]{0:T(1024)}, f32[768]{0:T(1024)S(1)}, u32[]{:S(2)}) copy-start(f32[768]{0:T(1024)S(1)} %get-tuple-element.222) | copy-start | bytes 9220
  180.8 94.5 %copy-start.52 = (f32[768]{0:T(1024)}, f32[768]{0:T(1024)S(1)}, u32[]{:S(2)}) copy-start(f32[768]{0:T(1024)S(1)} %get-tuple-element.221) | copy-start | bytes 9220
  186.8 27.8 %all-to-all-start = ((bf16[4,960,256]{2,1,0:T(8,128)(2,1)}), bf16[4,960,256]{2,1,0:T(8,128)(2,1)S(1)}, u32[]{:S(2)}, u32[]{:S(2)}) async-start(bf16[4,960,256]{2,1,0:T(8,128)(2,1)} %pad_maximum_fusion.2), calls=%async_computation | async-start | bytes 3932160 | tf_op jit(solution)/shard_map/all_to_all | solution.py:53
  190.4 130.5 %all-gather.12.cloned.1.call-start = ((), (), s32[]{:S(2)}) async-start(), calls=%async_computation.16 | async-start | bytes 3538944 | tf_op jit(solution)/shard_map/all_gather | solution.py:460
  227.5 13.5 %copy-start.39 = (bf16[768,768]{1,0:T(8,128)(2,1)S(1)}, bf16[768,768]{1,0:T(8,128)(2,1)}, u32[]{:S(2)}) copy-start(bf16[768,768]{1,0:T(8,128)(2,1)} %get-tuple-element.89) | copy-start | bytes 3538948
  241.6 32.9 %copy-start.11 = (bf16[768,768]{1,0:T(8,128)(2,1)S(1)}, bf16[768,768]{1,0:T(8,128)(2,1)}, u32[]{:S(2)}) copy-start(bf16[768,768]{1,0:T(8,128)(2,1)} %get-tuple-element.88) | copy-start | bytes 3538948
  287.6 160.4 %reduce-scatter.5.cloned.1.call-start = ((), (), s32[]{:S(2)}) async-start(), calls=%async_computation.17 | async-start | bytes 3538944 | tf_op jit(solution)/shard_map/reduce_scatter | solution.py:479
  288.5 21.0 %copy-start.55 = (s32[8,1,256]{2,1,0:T(1,128)}, s32[8,1,256]{2,1,0:T(1,128)S(1)}, u32[]{:S(2)}) copy-start(s32[8,1,256]{2,1,0:T(1,128)S(1)} %get-tuple-element.245) | copy-start | bytes 24580
  289.8 19.7 %copy-start.76 = (pred[2048]{0:T(1024)(128)(4,1)}, pred[2048]{0:T(1024)(128)(4,1)S(1)}, u32[]{:S(2)}) copy-start(pred[2048]{0:T(1024)(128)(4,1)S(1)} %broadcast_compare_fusion) | copy-start | bytes 6148
  393.1 8.8 %copy-start.49 = (f32[2048]{0:T(1024)}, f32[2048]{0:T(1024)S(1)}, u32[]{:S(2)}) copy-start(f32[2048]{0:T(1024)S(1)} %log_add_fusion) | copy-start | bytes 24580
  396.8 5.0 copy-start.54
  401.9 159.2 %reduce-scatter.7.cloned.1.call-start = ((), (), s32[]{:S(2)}) async-start(), calls=%async_computation.18 | async-start | bytes 7864320 | tf_op jit(solution)/shard_map/reduce_scatter | solution.py:491
  401.9 35.3 %collective-permute-start.4 = (bf16[256,768]{0,1:T(8,128)(2,1)}, bf16[256,768]{0,1:T(8,128)(2,1)S(1)}, u32[]{:S(2)}, u32[]{:S(2)}) collective-permute-start(bf16[256,768]{0,1:T(8,128)(2,1)} %get-tuple-element.235), channel_id=1, source_target_pairs={{0,0},{1,4},{2,8},{3,12},{4,1},{5,5},{6,9},{7,13},{8,2},{9,6},{10,... | collective-permute-start | bytes 1179656 | tf_op jit(solution)/shard_map/ppermute | solution.py:64
  405.7 31.6 %collective-permute-start.5 = (f32[1,256]{1,0:T(1,128)}, f32[1,256]{1,0:T(1,128)}, u32[]{:S(2)}, u32[]{:S(2)}) collective-permute-start(f32[1,256]{1,0:T(1,128)} %bitcast.35), channel_id=1, source_target_pairs={{0,0},{1,4},{2,8},{3,12},{4,1},{5,5},{6,9},{7,13},{8,2},{9,6},{10,... | collective-permute-start | bytes 3080 | tf_op jit(solution)/shard_map/ppermute | solution.py:64
  437.2 10.8 %copy-start.47 = (bf16[256,768]{0,1:T(8,128)(2,1)}, bf16[256,768]{0,1:T(8,128)(2,1)S(1)}, u32[]{:S(2)}) copy-start(bf16[256,768]{0,1:T(8,128)(2,1)S(1)} %collective-permute-done.4) | copy-start | bytes 1179652
  448.1 239.7 %reduce-scatter.9.cloned.1.call-start = ((), (), s32[]{:S(2)}) async-start(), calls=%async_computation.19 | async-start | bytes 17694720 | tf_op jit(solution)/shard_map/reduce_scatter | solution.py:530
  494.6 19.8 %copy-start.40 = (bf16[768,768]{1,0:T(8,128)(2,1)S(1)}, bf16[768,768]{1,0:T(8,128)(2,1)}, u32[]{:S(2)}) copy-start(bf16[768,768]{1,0:T(8,128)(2,1)} %get-tuple-element.89) | copy-start | bytes 3538948
  494.6 19.8 %copy-start.51 = (f32[768]{0:T(1024)S(1)}, f32[768]{0:T(1024)}, u32[]{:S(2)}) copy-start(f32[768]{0:T(1024)} %copy-done.50) | copy-start | bytes 9220
  494.6 19.8 %copy-start.64 = (f32[256]{0:T(256)S(1)}, f32[256]{0:T(256)}, u32[]{:S(2)}) copy-start(f32[256]{0:T(256)} %copy-done.63) | copy-start | bytes 3076
  525.2 4.3 copy-start.26
  534.4 26.7 %copy-start.32 = (bf16[4,384,256]{2,1,0:T(8,128)(2,1)S(1)}, bf16[4,384,256]{2,1,0:T(8,128)(2,1)}, u32[]{:S(2)}) copy-start(bf16[4,384,256]{2,1,0:T(8,128)(2,1)} %copy-done.31) | copy-start | bytes 2359300
  563.6 34.4 %collective-permute-start.6 = (bf16[256,768]{1,0:T(8,128)(2,1)S(1)}, bf16[256,768]{1,0:T(8,128)(2,1)S(1)}, u32[]{:S(2)}, u32[]{:S(2)}) collective-permute-start(bf16[256,768]{1,0:T(8,128)(2,1)S(1)} %convolution_convert_fusion.12), channel_id=1, source_target_pairs={{0,0},{1,4},{2,8},{3,12},{4,1},{5,5},{6,9},{7,13},{8,2},{9,6},{10,... | collective-permute-start | bytes 1179656 | tf_op jit(solution)/shard_map/ppermute | solution.py:64
  598.0 5.1 copy-start.75
  598.0 5.7 copy-start.77
  598.0 34.0 %copy-start.59 = (f32[256]{0:T(256)S(1)}, f32[256]{0:T(256)}, u32[]{:S(2)}) copy-start(f32[256]{0:T(256)} %copy-done.58) | copy-start | bytes 3076
  599.0 33.0 %all-to-all-start.7 = ((bf16[4,576,256]{2,1,0:T(8,128)(2,1)}), bf16[4,576,256]{2,1,0:T(8,128)(2,1)S(1)}, u32[]{:S(2)}, u32[]{:S(2)}) async-start(bf16[4,576,256]{2,1,0:T(8,128)(2,1)} %shard_map.372), calls=%async_computation.8 | async-start | bytes 2359296 | tf_op jit(solution)/shard_map/all_to_all | solution.py:53
  602.9 137.3 %reduce-scatter.11.cloned.1.call-start = ((), (), s32[]{:S(2)}) async-start(), calls=%async_computation.20 | async-start | bytes 4202496 | tf_op jit(solution)/shard_map/reduce_scatter | solution.py:551
  691.2 5.3 copy-start.66
  691.2 5.3 copy-start.78
  691.2 51.1 %all-to-all-start.9 = ((bf16[4,96,2560]{2,1,0:T(8,128)(2,1)}), bf16[4,96,2560]{2,1,0:T(8,128)(2,1)}, u32[]{:S(2)}, u32[]{:S(2)}) async-start(bf16[4,96,2560]{2,1,0:T(8,128)(2,1)} %shard_map.375), calls=%async_computation.13 | async-start | bytes 3932160 | tf_op jit(solution)/shard_map/all_to_all | solution.py:53
  696.7 36.2 %collective-permute-start.7 = (bf16[256,768]{0,1:T(8,128)(2,1)S(1)}, bf16[256,768]{0,1:T(8,128)(2,1)S(1)}, u32[]{:S(2)}, u32[]{:S(2)}) collective-permute-start(bf16[256,768]{0,1:T(8,128)(2,1)S(1)} %fusion.50), channel_id=1, source_target_pairs={{0,0},{1,4},{2,8},{3,12},{4,1},{5,5},{6,9},{7,13},{8,2},{9,6},{10,... | collective-permute-start | bytes 1179656 | tf_op jit(solution)/shard_map/ppermute | solution.py:64
  699.6 63.2 %copy-start.38 = (bf16[192,4096]{1,0:T(8,128)(2,1)S(1)}, bf16[192,4096]{1,0:T(8,128)(2,1)}, u32[]{:S(2)}) copy-start(bf16[192,4096]{1,0:T(8,128)(2,1)} %reduce-scatter.7.cloned.1.call-done) | copy-start | bytes 4718596
  742.3 34.0 %all-to-all-start.8 = ((bf16[4,96,704]{2,1,0:T(8,128)(2,1)}), bf16[4,96,704]{2,1,0:T(8,128)(2,1)S(1)}, u32[]{:S(2)}, u32[]{:S(2)}) async-start(bf16[4,96,704]{2,1,0:T(8,128)(2,1)} %shard_map.373), calls=%async_computation.12 | async-start | bytes 1179648 | tf_op jit(solution)/shard_map/all_to_all | solution.py:53
  (57 other events, 115.5 us)
Sparse Core Ops, SparseCore 0:
  12.9 158.7 all-gather.7
  173.3 111.7 all-gather.9
  287.7 33.0 all-gather.11
  402.0 46.0 reduce-scatter.4
  450.2 110.7 reduce-scatter.6
  564.4 123.3 reduce-scatter.8
  691.3 48.8 reduce-scatter.10

commit v3 on v2

--- a/solution.py
+++ b/solution.py
@@ -11,7 +11,6 @@
 
 HD = 64
 GAIN_LANES = 128
-TOKEN_ROWS = 256
 LANES = 128
 
 norm_eps = 1e-06
@@ -233,39 +232,73 @@
         out_ref[:, spots[2] : spots[2] + width, :] = value_sum[...].astype(out_ref.dtype)
 
 
-def exit_kernel(token_ref, table_ref, shifted_ref, product_ref, part_ref, logit_ref, *, rows):
+def exit_kernel(
+    count_ref,
+    token_ref,
+    target_ref,
+    table_ref,
+    shifted_ref,
+    product_ref,
+    part_ref,
+    logit_ref,
+    *,
+    rows,
+):
     lanes = table_ref.shape[1]
     chunk = next(size for size in (1024, 512, 256, 128) if lanes % size == 0)
-    tokens = token_ref[...]
-    row_max = jnp.full((tokens.shape[0], 1), -jnp.inf, jnp.float32)
-    for low in range(0, lanes, chunk):
-        logits = contract(tokens, table_ref[:, low : low + chunk], 1, 0)
-        if low + chunk > rows:
-            lane = low + lax.broadcasted_iota(jnp.int32, (1, chunk), 1)
-            logits = jnp.where(lane < rows, logits, -jnp.inf)
-        logit_ref[:, low : low + chunk] = logits
-        row_max = jnp.maximum(row_max, jnp.max(logits, axis=1, keepdims=True))
-    row_sum = jnp.zeros_like(row_max)
-    product = jnp.zeros(product_ref.shape, jnp.float32)
-    for low in range(0, lanes, chunk):
-        shifted = jnp.exp(logit_ref[:, low : low + chunk] - row_max)
-        row_sum += jnp.sum(shifted, axis=1, keepdims=True)
-        shifted = shifted.astype(shifted_ref.dtype)
-        shifted_ref[:, low : low + chunk] = shifted
-        product += contract(shifted, table_ref[:, low : low + chunk], 1, 1)
-    product_ref[...] = product
-    lane = lax.broadcasted_iota(jnp.int32, part_ref.shape, 1)
-    part_ref[...] = jnp.where(lane == 0, row_max, row_sum)
-
-
-def exit_rows(tokens, table, rows):
+    step_rows = token_ref.shape[0]
+    flagged = count_ref[pl.program_id(0)]
+
+    def part_rows(first, last):
+        here = slice(first, last)
+        tokens = token_ref[here]
+        row_max = jnp.full((last - first, 1), -jnp.inf, jnp.float32)
+        for low in range(0, lanes, chunk):
+            logits = contract(tokens, table_ref[:, low : low + chunk], 1, 0)
+            if low + chunk > rows:
+                lane = low + lax.broadcasted_iota(jnp.int32, (1, chunk), 1)
+                logits = jnp.where(lane < rows, logits, -jnp.inf)
+            logit_ref[here, low : low + chunk] = logits
+            row_max = jnp.maximum(row_max, jnp.max(logits, axis=1, keepdims=True))
+        row_sum = jnp.zeros_like(row_max)
+        product = jnp.zeros((last - first, product_ref.shape[1]), jnp.float32)
+        for low in range(0, lanes, chunk):
+            shifted = jnp.exp(logit_ref[here, low : low + chunk] - row_max)
+            row_sum += jnp.sum(shifted, axis=1, keepdims=True)
+            shifted = shifted.astype(shifted_ref.dtype)
+            shifted_ref[here, low : low + chunk] = shifted
+            product += contract(shifted, table_ref[:, low : low + chunk], 1, 1)
+        product_ref[here] = product
+        picked = tokens.astype(jnp.float32) * target_ref[here].astype(jnp.float32)
+        picked = jnp.sum(picked, axis=1, keepdims=True)
+        lane = lax.broadcasted_iota(jnp.int32, (last - first, part_ref.shape[1]), 1)
+        part_ref[here] = jnp.where(lane == 0, row_max, jnp.where(lane == 1, row_sum, picked))
+
+    split = step_rows * 9 // 16
+    part_rows(0, split)
+
+    @pl.when(flagged > split)
+    def _():
+        part_rows(split, step_rows)
+
+    @pl.when(flagged <= split)
+    def _():
+        here = slice(split, step_rows)
+        shifted_ref[here] = jnp.zeros((step_rows - split, lanes), shifted_ref.dtype)
+        product_ref[here] = jnp.zeros((step_rows - split, product_ref.shape[1]), jnp.float32)
+        lane = lax.broadcasted_iota(jnp.int32, (step_rows - split, part_ref.shape[1]), 1)
+        part_ref[here] = jnp.where(lane == 1, 1.0, 0.0)
+
+
+def exit_rows(counts, tokens, targets, table, rows):
     count, width = tokens.shape
     lanes = table.shape[1]
-    step_rows = min(TOKEN_ROWS, count)
+    step_rows = count // counts.shape[0]
+    block = pl.BlockSpec((step_rows, width), lambda step: (step, 0))
     return pl.pallas_call(
         functools.partial(exit_kernel, rows=rows),
         grid=(count // step_rows,),
-        in_specs=[pl.BlockSpec((step_rows, width), lambda step: (step, 0)), whole(table)],
+        in_specs=[pl.BlockSpec(memory_space=pltpu.SMEM), block, block, whole(table)],
         out_specs=[
             pl.BlockSpec((step_rows, lanes), lambda step: (step, 0)),
             pl.BlockSpec((step_rows, width), lambda step: (step, 0)),
@@ -277,7 +310,7 @@
             jax.ShapeDtypeStruct((count, LANES), jnp.float32),
         ],
         scratch_shapes=[pltpu.VMEM((step_rows, lanes), jnp.float32)],
-    )(tokens, table)
+    )(counts, tokens, targets, table)
 
 
 def whole(array):
@@ -392,11 +425,16 @@
     states = relocate(encoder_in.reshape(-1, width))
     marks = relocate(marks)
     prefix_len = marks[2, :1]
-    marks = lax.all_gather(marks[:2], dp, axis=0)
+    place = jnp.arange(marks.shape[1])
+    key = (1 - marks[0]) * marks.shape[1] + place
+    rank = jnp.sum((key[None, :] < key[:, None]).astype(jnp.int32), axis=1)
+    order = place[:, None] == rank[None, :]
+    marks = jnp.sum(jnp.where(order[None], marks[:2, None, :], 0), axis=2)
+    marks = lax.all_gather(marks, dp, axis=0)
+    order_low = order.astype(low)
     shard = jnp.pad(embedding.T, ((0, 0), (0, vocab_lanes - vocab_rows)))
     shard, marks, hidden, states = lax.optimization_barrier((shard, marks, hidden, states))
     table = lax.all_gather(shard, "seq", axis=0, tiled=True)
-    cotangent = relocate(out_cotangent.reshape(-1, width).astype(low))
     gain_one, gain_two, gain_three, gain_exit = gain_columns[:, :4].astype(jnp.float32).T
 
     def blocks(rows):
@@ -417,9 +455,8 @@
 
     residual_in = hidden.T.astype(jnp.float32)
     token_count = residual_in.shape[1]
-    residual_in, states, cotangent = lax.optimization_barrier((residual_in, states.T, cotangent.T))
+    residual_in, states = lax.optimization_barrier((residual_in, states.T))
     residual_in, states = rows_first(residual_in), rows_first(states)
-    cotangent = rows_first(cotangent)
     normed_one = norm_columns(residual_in, gain_one).astype(low)
     attended = jnp.concatenate(
         [blocks(contract(self_qkv, normed_one, 0, 0)), blocks(contract(cross_kv, states, 0, 0))],
@@ -454,7 +491,8 @@
     for down, hidden in zip(downs, hidden_folds):
         after_feed = after_feed + contract(down, hidden, 0, 0)
     block_output = relocate(after_feed.T.astype(low)).reshape(hidden_in.shape)
-    normed_exit = rows_first(norm_columns(after_feed, gain_exit).astype(low).T)
+    normed_exit = contract(order_low, norm_columns(after_feed, gain_exit).astype(low), 1, 1)
+    normed_exit = rows_first(normed_exit.astype(low))
     normed_exit, table = lax.optimization_barrier((normed_exit, table))
 
     tokens = lax.all_gather(normed_exit, dp, axis=0, tiled=True)
@@ -464,16 +502,19 @@
     hits = hits & (target_rows < vocab_rows)
     target_terms = contract(hits.astype(low), table, 1, 1).astype(low)
     tokens, target_terms = lax.optimization_barrier((tokens, target_terms))
-    shifted, products, parts = exit_rows(tokens, table, vocab_rows)
-    picked = jnp.sum(tokens.astype(jnp.float32) * target_terms.astype(jnp.float32), axis=1)
+    tokens, cotangent = lax.optimization_barrier((tokens, out_cotangent))
+    cotangent = relocate(cotangent.reshape(-1, width).astype(low))
+    counts = jnp.sum(marks[:, 0], axis=1)
+    shifted, products, parts = exit_rows(counts, tokens, target_terms, table, vocab_rows)
     row_max = parts[:, 0]
-    parts = lax.all_gather(jnp.stack([row_max, parts[:, 1], picked]), dp, axis=0)
+    parts = lax.all_gather(parts[:, :3].T, dp, axis=0)
     top = jnp.max(parts[:, 0], axis=0)
     log_total = top + jnp.log(jnp.sum(parts[:, 1] * jnp.exp(parts[:, 0] - top), axis=0))
     all_losses = flag_rows[:, 0] * (log_total - jnp.sum(parts[:, 2], axis=0))
     token_losses = lax.dynamic_slice(
         all_losses, (lax.axis_index(dp) * token_count,), (token_count,)
     )
+    token_losses = jnp.sum(jnp.where(order, token_losses[:, None], 0.0), axis=0)
     token_losses = relocate(token_losses.reshape(exit_flags.shape))
     factor = flag_rows * jnp.exp(row_max - log_total)[:, None]
     exit_in_grad = lax.psum_scatter(
@@ -484,10 +525,11 @@
     )
     logit_grads = jnp.where(hits, factor * shifted - flag_rows, factor * shifted).astype(low)
     table_terms = contract(tokens, logit_grads, 0, 0).astype(low)
-    exit_in_grad, table_terms, block_output, token_losses = lax.optimization_barrier(
-        (rows_first(exit_in_grad), table_terms, block_output, token_losses)
-    )
-    exit_in_grad = rows_first(exit_in_grad.T).astype(jnp.float32)
+    exit_in_grad, table_terms, block_output, token_losses, cotangent = lax.optimization_barrier(
+        (rows_first(exit_in_grad), table_terms, block_output, token_losses, cotangent)
+    )
+    cotangent = rows_first(cotangent.T)
+    exit_in_grad = rows_first(contract(exit_in_grad, order_low, 0, 0))
     table_sums = lax.psum_scatter(table_terms, "seq", scatter_dimension=0, tiled=True)
 
     feed_grad, full_exit_gain = norm_back(after_feed, gain_exit, exit_in_grad)

time: 803 us -> 783 us (0.975)
  waiting for transfers between devices: 283 us -> 317 us
  blocking collectives: 124 us -> 97.9 us
  Pallas kernels: 151 us -> 128 us
    all_gather x1, waiting for transfers between devices: 74.9 us -> 121 us  [per_device(): lax.all_gather(flat, ('seq',) + dp, axis=0, tiled=True)]
    all_gather x2, blocking collectives: 48.7 us -> 22.1 us  [the longest x1 12.9 us: per_device(): marks = lax.all_gather(marks, dp, axis=0)]
    ppermute x8, waiting for transfers between devices: 60.8 us -> 37.7 us  [relocate(): return lax.ppermute(block, ('group', 'part', 'seq'), pairs)]
    pallas_call x1, Pallas kernels: 57.3 us -> 34.4 us  [exit_rows(): pl.pallas_call(functools.partial(exit_kernel, rows=rows), grid=(count //...]
    unnamed x181 -> x185, local copies, waits for them, and re-layouts: 19.7 us -> 24.1 us
    dot_general x32 -> x34, matrix products: 92.3 us -> 94.2 us  [contract(): lax.dot_general(first_op, second_op, (((first_dim,), (second_dim,)), ((),...]
  transfers between devices with their start and end apart: 19 -> 19, of which waited for: 12 -> 11; matrix products, arithmetic and copies ran while one was open for 16% -> 16% of each run, Pallas kernels for 11% -> 12%
where the time goes in v3:
time: 783 us; the launch traced here: 768 us
  waiting for transfers between devices  317 us (40%)
  Pallas kernels  128 us (16%)
  blocking collectives  97.9 us (13%)
  matrix products  94.2 us (12%)
  starting transfers between devices  53.1 us (7%)
  local copies, waits for them, and re-layouts  35.1 us (4%)
  other arithmetic  25.9 us (3%)
  between operations  16.3 us (2%)
    all_gather x1, waiting for transfers between devices, per_device(): lax.all_gather(flat, ('seq',) + dp, axis=0, tiled=True)  121 us
    dot_general x34, matrix products, contract(): lax.dot_general(first_op, second_op, (((first_dim,), (second_dim,)), ((),...  94.2 us
    all_to_all x6, blocking collectives, swap(): return lax.all_to_all(pieces, axis, 0, 0, tiled=True)  75.8 us
    reduce_scatter x1, waiting for transfers between devices, per_device(): lax.psum_scatter(rest_terms, dp, scatter_dimension=0, tiled=True)  47.7 us
    all_to_all x4, waiting for transfers between devices, swap(): return lax.all_to_all(pieces, axis, 0, 0, tiled=True)  44.8 us
    pallas_call x2, Pallas kernels, attend_back(): pl.pallas_call(functools.partial(attend_back_kernel, places=places, spots...  38.4 us
    ppermute x8, waiting for transfers between devices, relocate(): return lax.ppermute(block, ('group', 'part', 'seq'), pairs)  37.7 us
    pallas_call x1, Pallas kernels, exit_rows(): pl.pallas_call(functools.partial(exit_kernel, rows=rows), grid=(count //...  34.4 us
  transfers between devices with their start and end apart: 19, of which 11 were waited for; matrix products, arithmetic and copies ran while one was open for 16% of the time, Pallas kernels for 12%

profile of v3, /device:TPU:8, one launch (start us, length us, event | category | flops | bytes accessed | tf_op | source)
XLA Modules:
  0.0 768.0 jit_solution(15549181014659446104)
XLA Ops:
  10.6 2.2 shard_map.365
  15.7 3.6 collective-permute-start.1
  23.2 12.9 %all-gather.2 = s32[8,2,256]{2,1,0:T(2,128)} all-gather(s32[1,2,256]{2,1,0:T(2,128)S(1)} %bitcast.185), channel_id=2, replica_groups=mesh['group'=2,'part'=4,'seq'=4] {'group','part'}, dimensions={0}, use_global_device_ids=true | all-gather | bytes 18432 | tf_op jit(solution)/shard_map/all_gather | solution.py:433
  36.1 4.4 collective-permute-done.2
  41.9 121.3 %all-gather.8.cloned.1.call-done = bf16[3072,3200]{1,0:T(8,128)(2,1)} async-done(((bf16[96,3200]{1,0:T(8,128)(2,1)}), bf16[3072,3200]{1,0:T(8,128)(2,1)}) %all-gather.8.cloned.1.call-update) | async-done | bytes 19660816 | tf_op jit(solution)/shard_map/all_gather | solution.py:413
  163.2 7.3 shard_map.366
  172.4 2.9 convolution_convert_fusion.5
  178.3 3.6 all-to-all-start
  182.5 13.3 %shard_map.367 = (bf16[768,768]{1,0:T(8,128)(2,1)}, bf16[768,768]{1,0:T(8,128)(2,1)}, bf16[768,768]{1,0:T(8,128)(2,1)}, bf16[768,2048]{1,0:T(8,128)(2,1)}, bf16[...) custom-call(bf16[4,768,3200]{2,1,0:T(8,128)(2,1)} %bitcast.143), custom_call_target="tpu_custom_call" | custom-call | tf_op jit(solution)/shard_map/pallas_call | solution.py:101
  195.8 10.4 %all-to-all-done.refs_0_.refs_1_ = bf16[4,960,256]{2,1,0:T(8,128)(2,1)S(1)} async-done(((bf16[4,960,256]{2,1,0:T(8,128)(2,1)}), bf16[4,960,256]{2,1,0:T(8,128)(2,1)S(1)}, u32[]{:S(2)}, u32[]{:S(2)}) %all-to-all-start) | async-done | bytes 1966112 | tf_op jit(solution)/shard_map/all_to_all | solution.py:52
  207.5 11.5 %shard_map.368 = bf16[4,192,256]{2,1,0:T(8,128)(2,1)} custom-call(s32[1]{0:T(128)} %bitcast.18.prefix_ref, bf16[4,960,256]{2,1,0:T(8,128)(2,1)} %copy-done), custom_call_target="tpu_custom_call" | custom-call | tf_op jit(solution)/shard_map/pallas_call | solution.py:322
  219.0 11.0 %all_to_all.50 = bf16[4,192,256]{2,1,0:T(8,128)(2,1)S(1)} all-to-all(bf16[4,192,256]{2,1,0:T(8,128)(2,1)} %shard_map.368), channel_id=1, replica_groups=mesh['group'=2,'part'=4,'seq'=4] {'part'}, dimensions={0} | all-to-all | bytes 786432 | tf_op jit(solution)/shard_map/all_to_all | solution.py:52
  233.4 10.6 %all_to_all.51.refs_0_ = bf16[4,192,256]{2,1,0:T(8,128)(2,1)} all-to-all(bf16[4,192,256]{2,1,0:T(8,128)(2,1)S(1)} %bitcast.175), channel_id=1, replica_groups=mesh['group'=2,'part'=4,'seq'=4] {'part'}, dimensions={0} | all-to-all | bytes 786432 | tf_op jit(solution)/shard_map/all_to_all | solution.py:52
  244.0 11.2 %shard_map.369 = bf16[4,192,256]{2,1,0:T(8,128)(2,1)} custom-call(s32[1]{0:T(128)} %bitcast.18.prefix_ref, bf16[4,192,256]{2,1,0:T(8,128)(2,1)} %all_to_all.51.refs_0_, bf16[4,960,256]{2,1,0:T(8,128)(2,1)} %copy-done), custom_call_target="tpu_custom_call" | custom-call | tf_op jit(solution)/shard_map/pallas_call | solution.py:322
  255.2 11.0 %all_to_all.52 = bf16[4,192,256]{2,1,0:T(8,128)(2,1)S(1)} all-to-all(bf16[4,192,256]{2,1,0:T(8,128)(2,1)} %shard_map.369), channel_id=1, replica_groups=mesh['group'=2,'part'=4,'seq'=4] {'part'}, dimensions={0} | all-to-all | bytes 786432 | tf_op jit(solution)/shard_map/all_to_all | solution.py:52
  270.1 2.7 multiply_convert_fusion
  280.1 19.6 %fusion.20.target_ref = bf16[2048,768]{1,0:T(8,128)(2,1)} fusion(bf16[768,4096]{1,0:T(8,128)(2,1)} %all-gather.10.cloned.1.call-done.table_ref, s32[2048]{0:T(1024)S(1)} %bitcast.183, pred[2048]{0:T(1024)(128)(4,1)S(1)} %broadcast_compare_fusion), kind=kOutput, calls=%fused_computation.25 | convolution fusion | flops 12903251968 | bytes 9447424 | tf_op jit(solution)/shard_map/dot_general | solution.py:22
  299.7 12.7 %all-gather.12.cloned.1.call-done.token_ref = bf16[2048,768]{1,0:T(8,128)(2,1)} async-done(((bf16[256,768]{1,0:T(8,128)(2,1)}), bf16[2048,768]{1,0:T(8,128)(2,1)}) %all-gather.12.cloned.1.call-update) | async-done | bytes 3145744 | tf_op jit(solution)/shard_map/all_gather | solution.py:498
  312.4 34.4 %shard_map.370 = (bf16[2048,4096]{1,0:T(8,128)(2,1)}, f32[2048,768]{1,0:T(8,128)}, f32[2048,128]{1,0:T(8,128)}) custom-call(s32[8]{0:T(128)} %get-tuple-element.289.count_ref, bf16[2048,768]{1,0:T(8,128)(2,1)} %all-gather.12.cloned.1.call-done.token_ref, bf16[2048,768]{1,0:T(8,128)(2,1)} %fusion.20.target_ref, ...), custom_call_target="tpu_custom_call" | custom-call | tf_op jit(solution)/shard_map/pallas_call | solution.py:298
  346.8 2.3 slice_bitcast_fusion
  350.6 9.2 %all-gather.3 = f32[8,3,2048]{2,1,0:T(4,128)S(1)} all-gather(f32[1,3,2048]{2,1,0:T(4,128)S(1)} %copy.162), channel_id=3, replica_groups=mesh['group'=2,'part'=4,'seq'=4] {'group','part'}, dimensions={0}, use_global_device_ids=true | all-gather | bytes 221184 | tf_op jit(solution)/shard_map/all_gather | solution.py:510
  364.6 4.5 subtract_convert_fusion
  369.2 2.5 collective-permute-start.3
  373.8 3.1 collective-permute-start.4
  377.9 2.8 collective-permute-start.5
  380.7 27.9 %fusion.13 = bf16[768,4096]{1,0:T(8,128)(2,1)} fusion(bf16[2048,768]{1,0:T(8,128)(2,1)} %all-gather.12.cloned.1.call-done.token_ref, bf16[2048,4096]{1,0:T(8,128)(2,1)} %get-tuple-element.105, f32[2048]{0:T(1024)S(1)} %bitcast.180, f32[2048]{0:T(1024)} %copy-done.55, s32[2048]{0:T(1024)} %bitcast.184, pred[2048]{0:T(1024)(128)(4,1)} %copy-done.78), kind=kOutput, calls=%fused_computation.14 | convolution fusion | flops 12946767872 | bytes 26241024 | tf_op jit(solution)/shard_map/dot_general | solution.py:22
  408.7 18.5 %reduce-scatter.5.cloned.1.call-done = bf16[256,768]{1,0:T(8,128)(2,1)} async-done(((bf16[2048,768]{1,0:T(8,128)(2,1)}), bf16[256,768]{1,0:T(8,128)(2,1)}) %reduce-scatter.5.cloned.1.call-update) | async-done | bytes 393232 | tf_op jit(solution)/shard_map/reduce_scatter | solution.py:520
  442.6 10.7 %all_to_all.53.refs_2_ = bf16[4,192,256]{2,1,0:T(8,128)(2,1)} all-to-all(bf16[4,192,256]{2,1,0:T(8,128)(2,1)S(1)} %bitcast.165), channel_id=1, replica_groups=mesh['group'=2,'part'=4,'seq'=4] {'part'}, dimensions={0} | all-to-all | bytes 786432 | tf_op jit(solution)/shard_map/all_to_all | solution.py:52
  453.3 18.6 %shard_map.371 = bf16[4,576,256]{2,1,0:T(8,128)(2,1)} custom-call(s32[1]{0:T(128)} %bitcast.18.prefix_ref, bf16[4,192,256]{2,1,0:T(8,128)(2,1)} %all_to_all.51.refs_0_, bf16[4,960,256]{2,1,0:T(8,128)(2,1)} %copy-done, bf16[4,192,256]{2,1,0:T(8,128)(2,1)} %all_to_all.53.refs_2_), custom_call_target="tpu_custom_call" | custom-call | tf_op jit(solution)/shard_map/pallas_call | solution.py:334
  471.9 19.5 %all_to_all.54 = bf16[4,576,256]{2,1,0:T(8,128)(2,1)S(1)} all-to-all(bf16[4,576,256]{2,1,0:T(8,128)(2,1)} %shard_map.371), channel_id=1, replica_groups=mesh['group'=2,'part'=4,'seq'=4] {'part'}, dimensions={0} | all-to-all | bytes 2359296 | tf_op jit(solution)/shard_map/all_to_all | solution.py:52
  493.9 2.3 fusion.19
  499.6 2.8 fusion.18
  502.4 2.8 fusion.17
  511.8 28.3 %reduce-scatter.7.cloned.1.call-done = bf16[192,4096]{1,0:T(8,128)(2,1)} async-done(((bf16[768,4096]{1,0:T(8,128)(2,1)}), bf16[192,4096]{1,0:T(8,128)(2,1)}) %reduce-scatter.7.cloned.1.call-update) | async-done | bytes 1572880 | tf_op jit(solution)/shard_map/reduce_scatter | solution.py:533
  540.2 2.5 convolution_convert_fusion.12
  544.6 13.0 %all_to_all.55.refs_1_ = bf16[4,192,256]{2,1,0:T(8,128)(2,1)} all-to-all(bf16[4,192,256]{2,1,0:T(8,128)(2,1)S(1)} %bitcast.162), channel_id=1, replica_groups=mesh['group'=2,'part'=4,'seq'=4] {'part'}, dimensions={0} | all-to-all | bytes 786432 | tf_op jit(solution)/shard_map/all_to_all | solution.py:52
  557.6 19.8 %shard_map.372 = bf16[4,576,256]{2,1,0:T(8,128)(2,1)} custom-call(s32[1]{0:T(128)} %bitcast.18.prefix_ref, bf16[4,960,256]{2,1,0:T(8,128)(2,1)} %copy-done, bf16[4,192,256]{2,1,0:T(8,128)(2,1)} %all_to_all.55.refs_1_), custom_call_target="tpu_custom_call" | custom-call | tf_op jit(solution)/shard_map/pallas_call | solution.py:334
  578.4 3.8 all-to-all-start.7
  583.9 27.4 %all-to-all-done.7 = bf16[4,576,256]{2,1,0:T(8,128)(2,1)S(1)} async-done(((bf16[4,576,256]{2,1,0:T(8,128)(2,1)}), bf16[4,576,256]{2,1,0:T(8,128)(2,1)S(1)}, u32[]{:S(2)}, u32[]{:S(2)}) %all-to-all-start.7) | async-done | bytes 1179680 | tf_op jit(solution)/shard_map/all_to_all | solution.py:52
  611.3 3.8 multiply_reduce_fusion.4
  619.2 47.7 %reduce-scatter.9.cloned.1.call-done.refs_0_ = bf16[96,10240]{1,0:T(8,128)(2,1)} async-done(((bf16[768,10240]{1,0:T(8,128)(2,1)}), bf16[96,10240]{1,0:T(8,128)(2,1)}) %reduce-scatter.9.cloned.1.call-update) | async-done | bytes 1966096 | tf_op jit(solution)/shard_map/reduce_scatter | solution.py:572
  666.9 3.3 shard_map.375
  670.3 5.3 all-to-all-start.9
  678.7 33.3 %collective-permute-done.7 = bf16[256,768]{0,1:T(8,128)(2,1)S(1)} collective-permute-done((bf16[256,768]{0,1:T(8,128)(2,1)S(1)}, bf16[256,768]{0,1:T(8,128)(2,1)S(1)}, u32[]{:S(2)}, u32[]{:S(2)}) %collective-permute-start.7) | collective-permute-done | bytes 393248 | tf_op jit(solution)/shard_map/ppermute | solution.py:63
  713.1 6.2 reduce-scatter.11.cloned.1.call-done.refs_0_
  721.3 20.4 %all-to-all-start.8 = ((bf16[4,96,704]{2,1,0:T(8,128)(2,1)}), bf16[4,96,704]{2,1,0:T(8,128)(2,1)S(1)}, u32[]{:S(2)}, u32[]{:S(2)}) async-start(bf16[4,96,704]{2,1,0:T(8,128)(2,1)} %shard_map.373), calls=%async_computation.12 | async-start | bytes 1179648 | tf_op jit(solution)/shard_map/all_to_all | solution.py:52
  743.8 2.7 shard_map.376
  748.2 7.0 all-to-all-done.8.terms_ref
  (299 shorter events, 93.2 us)
Async XLA Ops:
  7.2 6.4 copy-start.82
  7.2 6.4 copy-start.81
  7.2 8.3 %copy-start.45 = (bf16[1,256,768]{2,1,0:T(8,128)(2,1)S(1)}, bf16[1,256,768]{2,1,0:T(8,128)(2,1)}, u32[]{:S(2)}) copy-start(bf16[1,256,768]{2,1,0:T(8,128)(2,1)} %param.22) | copy-start | bytes 1179652
  7.2 12.2 %copy-start.46 = (bf16[1,256,768]{2,1,0:T(8,128)(2,1)S(1)}, bf16[1,256,768]{2,1,0:T(8,128)(2,1)}, u32[]{:S(2)}) copy-start(bf16[1,256,768]{2,1,0:T(8,128)(2,1)} %param.23) | copy-start | bytes 1179652
  7.2 14.3 %copy-start.34 = (bf16[4016,192]{0,1:T(8,128)(2,1)S(1)}, bf16[4016,192]{0,1:T(8,128)(2,1)}, u32[]{:S(2)}) copy-start(bf16[4016,192]{0,1:T(8,128)(2,1)} %param.43) | copy-start | bytes 4626436
  7.2 156.0 %all-gather.8.cloned.1.call-start = ((), (), s32[]{:S(2)}) async-start(), calls=%async_computation.14 | async-start | bytes 20275200 | tf_op jit(solution)/shard_map/all_gather | solution.py:413
  12.8 266.1 %all-gather.10.cloned.1.call-start = ((), (), s32[]{:S(2)}) async-start(), calls=%async_computation.15 | async-start | bytes 7864320 | tf_op jit(solution)/shard_map/all_gather | solution.py:437
  13.6 9.2 %collective-permute-start = (s32[3,256]{1,0:T(4,128)S(1)}, s32[3,256]{1,0:T(4,128)S(1)}, u32[]{:S(2)}, u32[]{:S(2)}) collective-permute-start(s32[3,256]{1,0:T(4,128)S(1)} %add_add_fusion.4), channel_id=1, source_target_pairs={{0,0},{1,4},{2,8},{3,12},{4,1},{5,5},{6,9},{7,13},{8,2},{9,6},{10,... | collective-permute-start | bytes 9224 | tf_op jit(solution)/shard_map/ppermute | solution.py:63
  15.7 20.4 %collective-permute-start.1 = (bf16[256,768]{0,1:T(8,128)(2,1)S(1)}, bf16[256,768]{0,1:T(8,128)(2,1)}, u32[]{:S(2)}, u32[]{:S(2)}) collective-permute-start(bf16[256,768]{0,1:T(8,128)(2,1)S(1)} %bitcast.173), channel_id=1, source_target_pairs={{0,0},{1,4},{2,8},{3,12},{4,1},{5,5},{6,9},{7,13},{8,2},{9,6},{10,... | collective-permute-start | bytes 1179656 | tf_op jit(solution)/shard_map/ppermute | solution.py:63
  19.6 20.9 %collective-permute-start.2 = (bf16[256,768]{0,1:T(8,128)(2,1)S(1)}, bf16[256,768]{0,1:T(8,128)(2,1)S(1)}, u32[]{:S(2)}, u32[]{:S(2)}) collective-permute-start(bf16[256,768]{0,1:T(8,128)(2,1)S(1)} %bitcast.174), channel_id=1, source_target_pairs={{0,0},{1,4},{2,8},{3,12},{4,1},{5,5},{6,9},{7,13},{8,2},{9,6},{10,... | collective-permute-start | bytes 1179656 | tf_op jit(solution)/shard_map/ppermute | solution.py:63
  23.0 254.7 %copy-start.59 = (s32[256]{0:T(256)}, s32[256]{0:T(256)S(1)}, u32[]{:S(2)}) copy-start(s32[256]{0:T(256)S(1)} %convert_reduce_fusion) | copy-start | bytes 3076
  40.5 131.8 %copy-start.42 = (bf16[256,768]{0,1:T(8,128)(2,1)}, bf16[256,768]{0,1:T(8,128)(2,1)S(1)}, u32[]{:S(2)}) copy-start(bf16[256,768]{0,1:T(8,128)(2,1)S(1)} %collective-permute-done.2) | copy-start | bytes 1179652
  41.8 128.7 %copy-start.68 = (f32[256]{0:T(256)}, f32[256]{0:T(256)S(1)}, u32[]{:S(2)}) copy-start(f32[256]{0:T(256)S(1)} %multiply_reduce_fusion.12) | copy-start | bytes 3076
  41.9 133.4 %copy-start.61 = (f32[256]{0:T(256)}, f32[256]{0:T(256)S(1)}, u32[]{:S(2)}) copy-start(f32[256]{0:T(256)S(1)} %fusion.57) | copy-start | bytes 3076
  172.3 59.6 %copy-start.51 = (f32[768]{0:T(1024)}, f32[768]{0:T(1024)S(1)}, u32[]{:S(2)}) copy-start(f32[768]{0:T(1024)S(1)} %get-tuple-element.264) | copy-start | bytes 9220
  172.3 94.6 %copy-start.53 = (f32[768]{0:T(1024)}, f32[768]{0:T(1024)S(1)}, u32[]{:S(2)}) copy-start(f32[768]{0:T(1024)S(1)} %get-tuple-element.263) | copy-start | bytes 9220
  178.3 27.8 %all-to-all-start = ((bf16[4,960,256]{2,1,0:T(8,128)(2,1)}), bf16[4,960,256]{2,1,0:T(8,128)(2,1)S(1)}, u32[]{:S(2)}, u32[]{:S(2)}) async-start(bf16[4,960,256]{2,1,0:T(8,128)(2,1)} %pad_maximum_fusion.2), calls=%async_computation | async-start | bytes 3932160 | tf_op jit(solution)/shard_map/all_to_all | solution.py:52
  181.9 130.5 %all-gather.12.cloned.1.call-start = ((), (), s32[]{:S(2)}) async-start(), calls=%async_computation.16 | async-start | bytes 3538944 | tf_op jit(solution)/shard_map/all_gather | solution.py:498
  219.0 13.8 %copy-start.38 = (bf16[768,768]{1,0:T(8,128)(2,1)S(1)}, bf16[768,768]{1,0:T(8,128)(2,1)}, u32[]{:S(2)}) copy-start(bf16[768,768]{1,0:T(8,128)(2,1)} %get-tuple-element.91) | copy-start | bytes 3538948
  231.9 34.3 %copy-start.2 = (f32[768,256]{1,0:T(8,128)}, f32[768,256]{1,0:T(8,128)S(1)}, u32[]{:S(2)}) copy-start(f32[768,256]{1,0:T(8,128)S(1)} %get-tuple-element.292) | copy-start | bytes 2359300
  233.4 32.8 %copy-start.10 = (bf16[768,768]{1,0:T(8,128)(2,1)S(1)}, bf16[768,768]{1,0:T(8,128)(2,1)}, u32[]{:S(2)}) copy-start(bf16[768,768]{1,0:T(8,128)(2,1)} %get-tuple-element.90) | copy-start | bytes 3538948
  278.9 148.3 %reduce-scatter.5.cloned.1.call-start = ((), (), s32[]{:S(2)}) async-start(), calls=%async_computation.17 | async-start | bytes 3538944 | tf_op jit(solution)/shard_map/reduce_scatter | solution.py:520
  279.7 20.0 %copy-start.56 = (s32[8,1,256]{2,1,0:T(1,128)}, s32[8,1,256]{2,1,0:T(1,128)S(1)}, u32[]{:S(2)}) copy-start(s32[8,1,256]{2,1,0:T(1,128)S(1)} %get-tuple-element.290) | copy-start | bytes 24580
  280.1 19.6 %copy-start.78 = (pred[2048]{0:T(1024)(128)(4,1)}, pred[2048]{0:T(1024)(128)(4,1)S(1)}, u32[]{:S(2)}) copy-start(pred[2048]{0:T(1024)(128)(4,1)S(1)} %broadcast_compare_fusion) | copy-start | bytes 6148
  360.7 8.4 %copy-start.50 = (f32[2048]{0:T(1024)}, f32[2048]{0:T(1024)S(1)}, u32[]{:S(2)}) copy-start(f32[2048]{0:T(1024)S(1)} %log_add_fusion) | copy-start | bytes 24580
  369.1 7.9 %copy-start.40 = (f32[1,256,768]{2,1,0:T(8,128)S(1)}, f32[1,256,768]{2,1,0:T(8,128)}, u32[]{:S(2)}) copy-start(f32[1,256,768]{2,1,0:T(8,128)} %param.27) | copy-start | bytes 2359300
  369.1 171.0 %reduce-scatter.7.cloned.1.call-start = ((), (), s32[]{:S(2)}) async-start(), calls=%async_computation.18 | async-start | bytes 7864320 | tf_op jit(solution)/shard_map/reduce_scatter | solution.py:533
  369.2 39.5 %collective-permute-start.3 = (bf16[256,768]{0,1:T(8,128)(2,1)}, bf16[256,768]{0,1:T(8,128)(2,1)S(1)}, u32[]{:S(2)}, u32[]{:S(2)}) collective-permute-start(bf16[256,768]{0,1:T(8,128)(2,1)} %get-tuple-element.279), channel_id=1, source_target_pairs={{0,0},{1,4},{2,8},{3,12},{4,1},{5,5},{6,9},{7,13},{8,2},{9,6},{10,... | collective-permute-start | bytes 1179656 | tf_op jit(solution)/shard_map/ppermute | solution.py:63
  373.8 34.8 %collective-permute-start.4 = (f32[1,256]{1,0:T(1,128)}, f32[1,256]{1,0:T(1,128)}, u32[]{:S(2)}, u32[]{:S(2)}) collective-permute-start(f32[1,256]{1,0:T(1,128)} %bitcast.35), channel_id=1, source_target_pairs={{0,0},{1,4},{2,8},{3,12},{4,1},{5,5},{6,9},{7,13},{8,2},{9,6},{10,... | collective-permute-start | bytes 3080 | tf_op jit(solution)/shard_map/ppermute | solution.py:63
  377.9 30.7 %collective-permute-start.5 = (bf16[256,768]{0,1:T(8,128)(2,1)}, bf16[256,768]{0,1:T(8,128)(2,1)S(1)}, u32[]{:S(2)}, u32[]{:S(2)}) collective-permute-start(bf16[256,768]{0,1:T(8,128)(2,1)} %bitcast.176), channel_id=1, source_target_pairs={{0,0},{1,4},{2,8},{3,12},{4,1},{5,5},{6,9},{7,13},{8,2},{9,6},{10,... | collective-permute-start | bytes 1179656 | tf_op jit(solution)/shard_map/ppermute | solution.py:63
  408.6 18.6 %copy-start.47 = (bf16[256,768]{0,1:T(8,128)(2,1)}, bf16[256,768]{0,1:T(8,128)(2,1)S(1)}, u32[]{:S(2)}) copy-start(bf16[256,768]{0,1:T(8,128)(2,1)S(1)} %collective-permute-done.3) | copy-start | bytes 1179652
  408.6 21.3 %copy-start.36 = (bf16[256,768]{0,1:T(8,128)(2,1)}, bf16[256,768]{0,1:T(8,128)(2,1)S(1)}, u32[]{:S(2)}) copy-start(bf16[256,768]{0,1:T(8,128)(2,1)S(1)} %collective-permute-done.5) | copy-start | bytes 1179652
  427.2 239.7 %reduce-scatter.9.cloned.1.call-start = ((), (), s32[]{:S(2)}) async-start(), calls=%async_computation.19 | async-start | bytes 17694720 | tf_op jit(solution)/shard_map/reduce_scatter | solution.py:572
  471.9 19.6 %copy-start.3 = (f32[768,256]{1,0:T(8,128)S(1)}, f32[768,256]{1,0:T(8,128)}, u32[]{:S(2)}) copy-start(f32[768,256]{1,0:T(8,128)} %copy-done.2) | copy-start | bytes 2359300
  471.9 19.6 %copy-start.39 = (bf16[768,768]{1,0:T(8,128)(2,1)S(1)}, bf16[768,768]{1,0:T(8,128)(2,1)}, u32[]{:S(2)}) copy-start(bf16[768,768]{1,0:T(8,128)(2,1)} %get-tuple-element.91) | copy-start | bytes 3538948
  471.9 19.6 %copy-start.52 = (f32[768]{0:T(1024)S(1)}, f32[768]{0:T(1024)}, u32[]{:S(2)}) copy-start(f32[768]{0:T(1024)} %copy-done.51) | copy-start | bytes 9220
  471.9 19.6 %copy-start.67 = (f32[256]{0:T(256)S(1)}, f32[256]{0:T(256)}, u32[]{:S(2)}) copy-start(f32[256]{0:T(256)} %copy-done.66) | copy-start | bytes 3076
  511.8 28.4 %copy-start.29 = (bf16[4,384,256]{2,1,0:T(8,128)(2,1)S(1)}, bf16[4,384,256]{2,1,0:T(8,128)(2,1)}, u32[]{:S(2)}) copy-start(bf16[4,384,256]{2,1,0:T(8,128)(2,1)} %copy-done.28) | copy-start | bytes 2359300
  542.6 34.8 %collective-permute-start.6 = (bf16[256,768]{1,0:T(8,128)(2,1)S(1)}, bf16[256,768]{1,0:T(8,128)(2,1)S(1)}, u32[]{:S(2)}, u32[]{:S(2)}) collective-permute-start(bf16[256,768]{1,0:T(8,128)(2,1)S(1)} %convolution_convert_fusion.12), channel_id=1, source_target_pairs={{0,0},{1,4},{2,8},{3,12},{4,1},{5,5},{6,9},{7,13},{8,2},{9,6},{10,... | collective-permute-start | bytes 1179656 | tf_op jit(solution)/shard_map/ppermute | solution.py:63
  577.4 5.3 copy-start.77
  577.4 33.8 %copy-start.62 = (f32[256]{0:T(256)S(1)}, f32[256]{0:T(256)}, u32[]{:S(2)}) copy-start(f32[256]{0:T(256)} %copy-done.61) | copy-start | bytes 3076
  578.4 32.9 %all-to-all-start.7 = ((bf16[4,576,256]{2,1,0:T(8,128)(2,1)}), bf16[4,576,256]{2,1,0:T(8,128)(2,1)S(1)}, u32[]{:S(2)}, u32[]{:S(2)}) async-start(bf16[4,576,256]{2,1,0:T(8,128)(2,1)} %shard_map.372), calls=%async_computation.8 | async-start | bytes 2359296 | tf_op jit(solution)/shard_map/all_to_all | solution.py:52
  582.2 137.1 %reduce-scatter.11.cloned.1.call-start = ((), (), s32[]{:S(2)}) async-start(), calls=%async_computation.20 | async-start | bytes 4202496 | tf_op jit(solution)/shard_map/reduce_scatter | solution.py:593
  670.3 5.3 copy-start.80
  670.3 51.1 %all-to-all-start.9 = ((bf16[4,96,2560]{2,1,0:T(8,128)(2,1)}), bf16[4,96,2560]{2,1,0:T(8,128)(2,1)}, u32[]{:S(2)}, u32[]{:S(2)}) async-start(bf16[4,96,2560]{2,1,0:T(8,128)(2,1)} %shard_map.375), calls=%async_computation.13 | async-start | bytes 3932160 | tf_op jit(solution)/shard_map/all_to_all | solution.py:52
  675.8 36.1 %collective-permute-start.7 = (bf16[256,768]{0,1:T(8,128)(2,1)S(1)}, bf16[256,768]{0,1:T(8,128)(2,1)S(1)}, u32[]{:S(2)}, u32[]{:S(2)}) collective-permute-start(bf16[256,768]{0,1:T(8,128)(2,1)S(1)} %fusion.42), channel_id=1, source_target_pairs={{0,0},{1,4},{2,8},{3,12},{4,1},{5,5},{6,9},{7,13},{8,2},{9,6},{10,... | collective-permute-start | bytes 1179656 | tf_op jit(solution)/shard_map/ppermute | solution.py:63
  678.7 63.1 %copy-start.35 = (bf16[192,4096]{1,0:T(8,128)(2,1)S(1)}, bf16[192,4096]{1,0:T(8,128)(2,1)}, u32[]{:S(2)}) copy-start(bf16[192,4096]{1,0:T(8,128)(2,1)} %reduce-scatter.7.cloned.1.call-done) | copy-start | bytes 4718596
  721.3 33.9 %all-to-all-start.8 = ((bf16[4,96,704]{2,1,0:T(8,128)(2,1)}), bf16[4,96,704]{2,1,0:T(8,128)(2,1)S(1)}, u32[]{:S(2)}, u32[]{:S(2)}) async-start(bf16[4,96,704]{2,1,0:T(8,128)(2,1)} %shard_map.373), calls=%async_computation.12 | async-start | bytes 1179648 | tf_op jit(solution)/shard_map/all_to_all | solution.py:52
  (59 other events, 128.1 us)
Sparse Core Ops, SparseCore 0:
  12.9 150.2 all-gather.7
  164.8 111.7 all-gather.9
  279.0 33.3 all-gather.11
  369.2 57.8 reduce-scatter.4
  429.3 110.7 reduce-scatter.6
  543.5 123.3 reduce-scatter.8
  670.4 48.8 reduce-scatter.10

commit v4 on v3

--- a/solution.py
+++ b/solution.py
@@ -490,7 +490,7 @@
     after_feed = after_cross
     for down, hidden in zip(downs, hidden_folds):
         after_feed = after_feed + contract(down, hidden, 0, 0)
-    block_output = relocate(after_feed.T.astype(low)).reshape(hidden_in.shape)
+    block_output = after_feed.T.astype(low)
     normed_exit = contract(order_low, norm_columns(after_feed, gain_exit).astype(low), 1, 1)
     normed_exit = rows_first(normed_exit.astype(low))
     normed_exit, table = lax.optimization_barrier((normed_exit, table))
@@ -502,10 +502,15 @@
     hits = hits & (target_rows < vocab_rows)
     target_terms = contract(hits.astype(low), table, 1, 1).astype(low)
     tokens, target_terms = lax.optimization_barrier((tokens, target_terms))
-    tokens, cotangent = lax.optimization_barrier((tokens, out_cotangent))
+    tokens, cotangent, block_output = lax.optimization_barrier(
+        (tokens, out_cotangent, block_output)
+    )
     cotangent = relocate(cotangent.reshape(-1, width).astype(low))
+    block_output = relocate(block_output)
     counts = jnp.sum(marks[:, 0], axis=1)
     shifted, products, parts = exit_rows(counts, tokens, target_terms, table, vocab_rows)
+    parts, cotangent, block_output = lax.optimization_barrier((parts, cotangent, block_output))
+    block_output = block_output.reshape(hidden_in.shape)
     row_max = parts[:, 0]
     parts = lax.all_gather(parts[:, :3].T, dp, axis=0)
     top = jnp.max(parts[:, 0], axis=0)
@@ -525,8 +530,8 @@
     )
     logit_grads = jnp.where(hits, factor * shifted - flag_rows, factor * shifted).astype(low)
     table_terms = contract(tokens, logit_grads, 0, 0).astype(low)
-    exit_in_grad, table_terms, block_output, token_losses, cotangent = lax.optimization_barrier(
-        (rows_first(exit_in_grad), table_terms, block_output, token_losses, cotangent)
+    exit_in_grad, table_terms, token_losses = lax.optimization_barrier(
+        (rows_first(exit_in_grad), table_terms, token_losses)
     )
     cotangent = rows_first(cotangent.T)
     exit_in_grad = rows_first(contract(exit_in_grad, order_low, 0, 0))
@@ -589,7 +594,9 @@
         ],
         axis=1,
     )
-    self_terms, rest_terms = lax.optimization_barrier((self_terms, rest_terms))
+    self_terms, rest_terms, hidden_grad = lax.optimization_barrier(
+        (self_terms, rest_terms, hidden_grad)
+    )
     self_terms = lax.psum_scatter(self_terms, dp, scatter_dimension=0, tiled=True)
     embedding_grad = table_sums[:, :vocab_rows].astype(jnp.float32).T
     (

time: 783 us -> 772 us (0.986)
  starting transfers between devices: 53.1 us -> 44.7 us
    reduce_scatter x1, waiting for transfers between devices: 6.15 us -> 41.9 us  [per_device(): lax.psum_scatter(self_terms, dp, scatter_dimension=0, tiled=True)]
    ppermute x8, waiting for transfers between devices: 37.7 us -> 10.8 us  [relocate(): return lax.ppermute(block, ('group', 'part', 'seq'), pairs)]
    all_to_all x4, starting transfers between devices: 33.1 us -> 17.7 us  [swap(): return lax.all_to_all(pieces, axis, 0, 0, tiled=True)]
    unnamed x185 -> x151, local copies, waits for them, and re-layouts: 24.1 us -> 23.3 us
  transfers between devices with their start and end apart: 19 -> 19, of which waited for: 11 -> 11; matrix products, arithmetic and copies ran while one was open for 16% -> 16% of each run, Pallas kernels for 12% -> 16%
where the time goes in v4:
time: 772 us; the launch traced here: 757 us
  waiting for transfers between devices  317 us (41%)
  Pallas kernels  128 us (17%)
  blocking collectives  99.7 us (13%)
  matrix products  93.9 us (12%)
  starting transfers between devices  44.7 us (6%)
  local copies, waits for them, and re-layouts  32 us (4%)
  other arithmetic  26.4 us (3%)
  between operations  16.2 us (2%)
    all_gather x1, waiting for transfers between devices, per_device(): lax.all_gather(flat, ('seq',) + dp, axis=0, tiled=True)  121 us
    dot_general x34, matrix products, contract(): lax.dot_general(first_op, second_op, (((first_dim,), (second_dim,)), ((),...  93.9 us
    all_to_all x6, blocking collectives, swap(): return lax.all_to_all(pieces, axis, 0, 0, tiled=True)  75.8 us
    reduce_scatter x1, waiting for transfers between devices, per_device(): lax.psum_scatter(rest_terms, dp, scatter_dimension=0, tiled=True)  46.2 us
    all_to_all x4, waiting for transfers between devices, swap(): return lax.all_to_all(pieces, axis, 0, 0, tiled=True)  42.9 us
    reduce_scatter x1, waiting for transfers between devices, per_device(): lax.psum_scatter(self_terms, dp, scatter_dimension=0, tiled=True)  41.9 us
    pallas_call x2, Pallas kernels, attend_back(): pl.pallas_call(functools.partial(attend_back_kernel, places=places, spots...  38.4 us
    pallas_call x1, Pallas kernels, exit_rows(): pl.pallas_call(functools.partial(exit_kernel, rows=rows), grid=(count //...  34.2 us
  transfers between devices with their start and end apart: 19, of which 11 were waited for; matrix products, arithmetic and copies ran while one was open for 16% of the time, Pallas kernels for 16%

profile of v4, /device:TPU:8, one launch (start us, length us, event | category | flops | bytes accessed | tf_op | source)
XLA Modules:
  0.0 757.3 jit_solution(10098292539097643827)
XLA Ops:
  15.7 3.6 collective-permute-start.1
  23.2 12.7 %all-gather.2 = s32[8,2,256]{2,1,0:T(2,128)} all-gather(s32[1,2,256]{2,1,0:T(2,128)S(1)} %bitcast.182), channel_id=2, replica_groups=mesh['group'=2,'part'=4,'seq'=4] {'group','part'}, dimensions={0}, use_global_device_ids=true | all-gather | bytes 18432 | tf_op jit(solution)/shard_map/all_gather | solution.py:433
  35.9 4.6 collective-permute-done.2
  41.9 121.3 %all-gather.8.cloned.1.call-done = bf16[3072,3200]{1,0:T(8,128)(2,1)} async-done(((bf16[96,3200]{1,0:T(8,128)(2,1)}), bf16[3072,3200]{1,0:T(8,128)(2,1)}) %all-gather.8.cloned.1.call-update) | async-done | bytes 19660816 | tf_op jit(solution)/shard_map/all_gather | solution.py:413
  163.2 7.3 shard_map.366
  172.3 2.9 convolution_convert_fusion.5
  178.3 3.6 all-to-all-start
  182.4 13.3 %shard_map.367 = (bf16[768,768]{1,0:T(8,128)(2,1)}, bf16[768,768]{1,0:T(8,128)(2,1)}, bf16[768,768]{1,0:T(8,128)(2,1)}, bf16[768,2048]{1,0:T(8,128)(2,1)}, bf16[...) custom-call(bf16[4,768,3200]{2,1,0:T(8,128)(2,1)} %bitcast.141), custom_call_target="tpu_custom_call" | custom-call | tf_op jit(solution)/shard_map/pallas_call | solution.py:101
  195.7 10.4 %all-to-all-done.refs_0_.refs_1_ = bf16[4,960,256]{2,1,0:T(8,128)(2,1)S(1)} async-done(((bf16[4,960,256]{2,1,0:T(8,128)(2,1)}), bf16[4,960,256]{2,1,0:T(8,128)(2,1)S(1)}, u32[]{:S(2)}, u32[]{:S(2)}) %all-to-all-start) | async-done | bytes 1966112 | tf_op jit(solution)/shard_map/all_to_all | solution.py:52
  207.4 11.5 %shard_map.368 = bf16[4,192,256]{2,1,0:T(8,128)(2,1)} custom-call(s32[1]{0:T(128)} %bitcast.17.prefix_ref, bf16[4,960,256]{2,1,0:T(8,128)(2,1)} %copy-done), custom_call_target="tpu_custom_call" | custom-call | tf_op jit(solution)/shard_map/pallas_call | solution.py:322
  218.9 11.0 %all_to_all.50 = bf16[4,192,256]{2,1,0:T(8,128)(2,1)S(1)} all-to-all(bf16[4,192,256]{2,1,0:T(8,128)(2,1)} %shard_map.368), channel_id=1, replica_groups=mesh['group'=2,'part'=4,'seq'=4] {'part'}, dimensions={0} | all-to-all | bytes 786432 | tf_op jit(solution)/shard_map/all_to_all | solution.py:52
  233.1 10.6 %all_to_all.51.refs_0_ = bf16[4,192,256]{2,1,0:T(8,128)(2,1)} all-to-all(bf16[4,192,256]{2,1,0:T(8,128)(2,1)S(1)} %bitcast.173), channel_id=1, replica_groups=mesh['group'=2,'part'=4,'seq'=4] {'part'}, dimensions={0} | all-to-all | bytes 786432 | tf_op jit(solution)/shard_map/all_to_all | solution.py:52
  243.8 11.2 %shard_map.369 = bf16[4,192,256]{2,1,0:T(8,128)(2,1)} custom-call(s32[1]{0:T(128)} %bitcast.17.prefix_ref, bf16[4,192,256]{2,1,0:T(8,128)(2,1)} %all_to_all.51.refs_0_, bf16[4,960,256]{2,1,0:T(8,128)(2,1)} %copy-done), custom_call_target="tpu_custom_call" | custom-call | tf_op jit(solution)/shard_map/pallas_call | solution.py:322
  254.9 11.0 %all_to_all.52 = bf16[4,192,256]{2,1,0:T(8,128)(2,1)S(1)} all-to-all(bf16[4,192,256]{2,1,0:T(8,128)(2,1)} %shard_map.369), channel_id=1, replica_groups=mesh['group'=2,'part'=4,'seq'=4] {'part'}, dimensions={0} | all-to-all | bytes 786432 | tf_op jit(solution)/shard_map/all_to_all | solution.py:52
  269.9 2.7 multiply_convert_fusion
  279.4 19.7 %fusion.20.target_ref = bf16[2048,768]{1,0:T(8,128)(2,1)} fusion(bf16[768,4096]{1,0:T(8,128)(2,1)} %all-gather.10.cloned.1.call-done.table_ref, s32[2048]{0:T(1024)S(1)} %bitcast.180, pred[2048]{0:T(1024)(128)(4,1)S(1)} %broadcast_compare_fusion), kind=kOutput, calls=%fused_computation.25 | convolution fusion | flops 12903251968 | bytes 9447424 | tf_op jit(solution)/shard_map/dot_general | solution.py:22
  299.1 13.3 %all-gather.12.cloned.1.call-done.token_ref = bf16[2048,768]{1,0:T(8,128)(2,1)} async-done(((bf16[256,768]{1,0:T(8,128)(2,1)}), bf16[2048,768]{1,0:T(8,128)(2,1)}) %all-gather.12.cloned.1.call-update) | async-done | bytes 3145744 | tf_op jit(solution)/shard_map/all_gather | solution.py:498
  313.3 2.3 collective-permute-start.3
  315.6 3.5 collective-permute-start.4
  319.5 34.2 %shard_map.370 = (bf16[2048,4096]{1,0:T(8,128)(2,1)}, f32[2048,768]{1,0:T(8,128)}, f32[2048,128]{1,0:T(8,128)}) custom-call(s32[8]{0:T(128)} %get-tuple-element.296.count_ref, bf16[2048,768]{1,0:T(8,128)(2,1)} %all-gather.12.cloned.1.call-done.token_ref, bf16[2048,768]{1,0:T(8,128)(2,1)} %fusion.20.target_ref, ...), custom_call_target="tpu_custom_call" | custom-call | tf_op jit(solution)/shard_map/pallas_call | solution.py:298
  357.5 11.3 %all-gather.3 = f32[8,3,2048]{2,1,0:T(4,128)S(1)} all-gather(f32[1,3,2048]{2,1,0:T(4,128)S(1)} %copy.163), channel_id=3, replica_groups=mesh['group'=2,'part'=4,'seq'=4] {'group','part'}, dimensions={0}, use_global_device_ids=true | all-gather | bytes 221184 | tf_op jit(solution)/shard_map/all_gather | solution.py:515
  373.0 4.5 subtract_convert_fusion
  377.8 7.2 collective-permute-start.5
  385.0 28.3 %fusion.13 = bf16[768,4096]{1,0:T(8,128)(2,1)} fusion(bf16[2048,768]{1,0:T(8,128)(2,1)} %all-gather.12.cloned.1.call-done.token_ref, bf16[2048,4096]{1,0:T(8,128)(2,1)} %get-tuple-element.112, f32[2048]{0:T(1024)S(1)} %bitcast.177, f32[2048]{0:T(1024)S(1)} %multiply_reduce_fusion, s32[2048]{0:T(1024)S(1)} %bitcast.181, ...), kind=kOutput, calls=%fused_computation.14 | convolution fusion | flops 12946767872 | bytes 26241024 | tf_op jit(solution)/shard_map/dot_general | solution.py:22
  413.3 12.0 %reduce-scatter.5.cloned.1.call-done = bf16[256,768]{1,0:T(8,128)(2,1)} async-done(((bf16[2048,768]{1,0:T(8,128)(2,1)}), bf16[256,768]{1,0:T(8,128)(2,1)}) %reduce-scatter.5.cloned.1.call-update) | async-done | bytes 393232 | tf_op jit(solution)/shard_map/reduce_scatter | solution.py:525
  441.3 10.7 %all_to_all.53.refs_2_ = bf16[4,192,256]{2,1,0:T(8,128)(2,1)} all-to-all(bf16[4,192,256]{2,1,0:T(8,128)(2,1)S(1)} %bitcast.164), channel_id=1, replica_groups=mesh['group'=2,'part'=4,'seq'=4] {'part'}, dimensions={0} | all-to-all | bytes 786432 | tf_op jit(solution)/shard_map/all_to_all | solution.py:52
  452.0 18.6 %shard_map.371 = bf16[4,576,256]{2,1,0:T(8,128)(2,1)} custom-call(s32[1]{0:T(128)} %bitcast.17.prefix_ref, bf16[4,192,256]{2,1,0:T(8,128)(2,1)} %all_to_all.51.refs_0_, bf16[4,960,256]{2,1,0:T(8,128)(2,1)} %copy-done, bf16[4,192,256]{2,1,0:T(8,128)(2,1)} %all_to_all.53.refs_2_), custom_call_target="tpu_custom_call" | custom-call | tf_op jit(solution)/shard_map/pallas_call | solution.py:334
  470.6 19.5 %all_to_all.54 = bf16[4,576,256]{2,1,0:T(8,128)(2,1)S(1)} all-to-all(bf16[4,576,256]{2,1,0:T(8,128)(2,1)} %shard_map.371), channel_id=1, replica_groups=mesh['group'=2,'part'=4,'seq'=4] {'part'}, dimensions={0} | all-to-all | bytes 2359296 | tf_op jit(solution)/shard_map/all_to_all | solution.py:52
  492.5 2.3 fusion.19
  498.3 2.7 fusion.18
  501.0 2.7 fusion.17
  510.3 28.1 %reduce-scatter.7.cloned.1.call-done = bf16[192,4096]{1,0:T(8,128)(2,1)} async-done(((bf16[768,4096]{1,0:T(8,128)(2,1)}), bf16[192,4096]{1,0:T(8,128)(2,1)}) %reduce-scatter.7.cloned.1.call-update) | async-done | bytes 1572880 | tf_op jit(solution)/shard_map/reduce_scatter | solution.py:538
  538.4 2.5 convolution_convert_fusion.12
  542.8 13.0 %all_to_all.55.refs_1_ = bf16[4,192,256]{2,1,0:T(8,128)(2,1)} all-to-all(bf16[4,192,256]{2,1,0:T(8,128)(2,1)S(1)} %bitcast.161), channel_id=1, replica_groups=mesh['group'=2,'part'=4,'seq'=4] {'part'}, dimensions={0} | all-to-all | bytes 786432 | tf_op jit(solution)/shard_map/all_to_all | solution.py:52
  555.8 19.8 %shard_map.372 = bf16[4,576,256]{2,1,0:T(8,128)(2,1)} custom-call(s32[1]{0:T(128)} %bitcast.17.prefix_ref, bf16[4,960,256]{2,1,0:T(8,128)(2,1)} %copy-done, bf16[4,192,256]{2,1,0:T(8,128)(2,1)} %all_to_all.55.refs_1_), custom_call_target="tpu_custom_call" | custom-call | tf_op jit(solution)/shard_map/pallas_call | solution.py:334
  576.5 3.9 all-to-all-start.7
  580.4 29.1 %all-to-all-done.7 = bf16[4,576,256]{2,1,0:T(8,128)(2,1)S(1)} async-done(((bf16[4,576,256]{2,1,0:T(8,128)(2,1)}), bf16[4,576,256]{2,1,0:T(8,128)(2,1)S(1)}, u32[]{:S(2)}, u32[]{:S(2)}) %all-to-all-start.7) | async-done | bytes 1179680 | tf_op jit(solution)/shard_map/all_to_all | solution.py:52
  609.5 3.2 multiply_reduce_fusion.1
  613.0 4.4 collective-permute-start.7
  620.8 6.2 collective-permute-done.7
  627.0 46.2 %reduce-scatter.9.cloned.1.call-done.refs_0_ = bf16[96,10240]{1,0:T(8,128)(2,1)} async-done(((bf16[768,10240]{1,0:T(8,128)(2,1)}), bf16[96,10240]{1,0:T(8,128)(2,1)}) %reduce-scatter.9.cloned.1.call-update) | async-done | bytes 1966096 | tf_op jit(solution)/shard_map/reduce_scatter | solution.py:577
  673.2 3.3 shard_map.375
  676.6 5.1 all-to-all-start.9
  683.7 41.9 %reduce-scatter.11.cloned.1.call-done.refs_0_ = bf16[96,2432]{1,0:T(8,128)(2,1)} async-done(((bf16[768,2432]{1,0:T(8,128)(2,1)}), bf16[96,2432]{1,0:T(8,128)(2,1)}) %reduce-scatter.11.cloned.1.call-update) | async-done | bytes 466960 | tf_op jit(solution)/shard_map/reduce_scatter | solution.py:600
  727.7 5.1 all-to-all-start.8
  732.8 3.4 convert_bitcast_fusion
  737.4 2.7 shard_map.376
  741.8 3.4 all-to-all-done.8.terms_ref
  (265 shorter events, 89.4 us)
Async XLA Ops:
  7.2 6.4 copy-start.65
  7.2 6.4 copy-start.64
  7.2 8.3 %copy-start.42 = (bf16[1,256,768]{2,1,0:T(8,128)(2,1)S(1)}, bf16[1,256,768]{2,1,0:T(8,128)(2,1)}, u32[]{:S(2)}) copy-start(bf16[1,256,768]{2,1,0:T(8,128)(2,1)} %param.22) | copy-start | bytes 1179652
  7.2 12.2 %copy-start.43 = (bf16[1,256,768]{2,1,0:T(8,128)(2,1)S(1)}, bf16[1,256,768]{2,1,0:T(8,128)(2,1)}, u32[]{:S(2)}) copy-start(bf16[1,256,768]{2,1,0:T(8,128)(2,1)} %param.23) | copy-start | bytes 1179652
  7.2 14.3 %copy-start.35 = (bf16[4016,192]{0,1:T(8,128)(2,1)S(1)}, bf16[4016,192]{0,1:T(8,128)(2,1)}, u32[]{:S(2)}) copy-start(bf16[4016,192]{0,1:T(8,128)(2,1)} %param.43) | copy-start | bytes 4626436
  7.2 156.0 %all-gather.8.cloned.1.call-start = ((), (), s32[]{:S(2)}) async-start(), calls=%async_computation.14 | async-start | bytes 20275200 | tf_op jit(solution)/shard_map/all_gather | solution.py:413
  12.8 265.8 %all-gather.10.cloned.1.call-start = ((), (), s32[]{:S(2)}) async-start(), calls=%async_computation.15 | async-start | bytes 7864320 | tf_op jit(solution)/shard_map/all_gather | solution.py:437
  13.6 9.2 %collective-permute-start = (s32[3,256]{1,0:T(4,128)S(1)}, s32[3,256]{1,0:T(4,128)S(1)}, u32[]{:S(2)}, u32[]{:S(2)}) collective-permute-start(s32[3,256]{1,0:T(4,128)S(1)} %add_add_fusion.4), channel_id=1, source_target_pairs={{0,0},{1,4},{2,8},{3,12},{4,1},{5,5},{6,9},{7,13},{8,2},{9,6},{10,... | collective-permute-start | bytes 9224 | tf_op jit(solution)/shard_map/ppermute | solution.py:63
  15.7 20.2 %collective-permute-start.1 = (bf16[256,768]{0,1:T(8,128)(2,1)S(1)}, bf16[256,768]{0,1:T(8,128)(2,1)}, u32[]{:S(2)}, u32[]{:S(2)}) collective-permute-start(bf16[256,768]{0,1:T(8,128)(2,1)S(1)} %bitcast.171), channel_id=1, source_target_pairs={{0,0},{1,4},{2,8},{3,12},{4,1},{5,5},{6,9},{7,13},{8,2},{9,6},{10,... | collective-permute-start | bytes 1179656 | tf_op jit(solution)/shard_map/ppermute | solution.py:63
  19.6 20.9 %collective-permute-start.2 = (bf16[256,768]{0,1:T(8,128)(2,1)S(1)}, bf16[256,768]{0,1:T(8,128)(2,1)S(1)}, u32[]{:S(2)}, u32[]{:S(2)}) collective-permute-start(bf16[256,768]{0,1:T(8,128)(2,1)S(1)} %bitcast.172), channel_id=1, source_target_pairs={{0,0},{1,4},{2,8},{3,12},{4,1},{5,5},{6,9},{7,13},{8,2},{9,6},{10,... | collective-permute-start | bytes 1179656 | tf_op jit(solution)/shard_map/ppermute | solution.py:63
  23.0 147.5 %copy-start.47 = (s32[256]{0:T(256)}, s32[256]{0:T(256)S(1)}, u32[]{:S(2)}) copy-start(s32[256]{0:T(256)S(1)} %convert_reduce_fusion) | copy-start | bytes 3076
  40.5 131.8 %copy-start.39 = (bf16[256,768]{0,1:T(8,128)(2,1)}, bf16[256,768]{0,1:T(8,128)(2,1)S(1)}, u32[]{:S(2)}) copy-start(bf16[256,768]{0,1:T(8,128)(2,1)S(1)} %collective-permute-done.2) | copy-start | bytes 1179652
  41.8 128.7 %copy-start.53 = (f32[256]{0:T(256)}, f32[256]{0:T(256)S(1)}, u32[]{:S(2)}) copy-start(f32[256]{0:T(256)S(1)} %multiply_reduce_fusion.12) | copy-start | bytes 3076
  41.9 133.4 %copy-start.49 = (f32[256]{0:T(256)}, f32[256]{0:T(256)S(1)}, u32[]{:S(2)}) copy-start(f32[256]{0:T(256)S(1)} %fusion.57) | copy-start | bytes 3076
  172.3 3.2 copy-start.66
  178.3 27.8 %all-to-all-start = ((bf16[4,960,256]{2,1,0:T(8,128)(2,1)}), bf16[4,960,256]{2,1,0:T(8,128)(2,1)S(1)}, u32[]{:S(2)}, u32[]{:S(2)}) async-start(bf16[4,960,256]{2,1,0:T(8,128)(2,1)} %pad_maximum_fusion.2), calls=%async_computation | async-start | bytes 3932160 | tf_op jit(solution)/shard_map/all_to_all | solution.py:52
  181.9 130.5 %all-gather.12.cloned.1.call-start = ((), (), s32[]{:S(2)}) async-start(), calls=%async_computation.16 | async-start | bytes 3538944 | tf_op jit(solution)/shard_map/all_gather | solution.py:498
  218.9 13.6 %copy-start.36 = (bf16[768,768]{1,0:T(8,128)(2,1)S(1)}, bf16[768,768]{1,0:T(8,128)(2,1)}, u32[]{:S(2)}) copy-start(bf16[768,768]{1,0:T(8,128)(2,1)} %get-tuple-element.94) | copy-start | bytes 3538948
  229.9 3.2 copy-start.19
  231.8 34.1 %copy-start.2 = (f32[768,256]{1,0:T(8,128)}, f32[768,256]{1,0:T(8,128)S(1)}, u32[]{:S(2)}) copy-start(f32[768,256]{1,0:T(8,128)S(1)} %get-tuple-element.298) | copy-start | bytes 2359300
  233.1 32.8 %copy-start.11 = (bf16[768,768]{1,0:T(8,128)(2,1)S(1)}, bf16[768,768]{1,0:T(8,128)(2,1)}, u32[]{:S(2)}) copy-start(bf16[768,768]{1,0:T(8,128)(2,1)} %get-tuple-element.93) | copy-start | bytes 3538948
  266.5 170.2 %copy-start.59 = (f32[256]{0:T(256)}, f32[256]{0:T(256)S(1)}, u32[]{:S(2)}) copy-start(f32[256]{0:T(256)S(1)} %fusion.59) | copy-start | bytes 3076
  269.0 3.6 copy-start.32
  277.4 150.0 %copy-start.45 = (f32[256]{0:T(256)}, f32[256]{0:T(256)S(1)}, u32[]{:S(2)}) copy-start(f32[256]{0:T(256)S(1)} %fusion.60) | copy-start | bytes 3076
  278.6 146.8 %reduce-scatter.5.cloned.1.call-start = ((), (), s32[]{:S(2)}) async-start(), calls=%async_computation.17 | async-start | bytes 3538944 | tf_op jit(solution)/shard_map/reduce_scatter | solution.py:525
  279.4 33.0 %copy-start.38 = (f32[1,256,768]{2,1,0:T(8,128)S(1)}, f32[1,256,768]{2,1,0:T(8,128)}, u32[]{:S(2)}) copy-start(f32[1,256,768]{2,1,0:T(8,128)} %param.27) | copy-start | bytes 2359300
  313.3 40.4 %collective-permute-start.3 = (bf16[256,768]{0,1:T(8,128)(2,1)}, bf16[256,768]{0,1:T(8,128)(2,1)}, u32[]{:S(2)}, u32[]{:S(2)}) collective-permute-start(bf16[256,768]{0,1:T(8,128)(2,1)} %bitcast.84), channel_id=1, source_target_pairs={{0,0},{1,4},{2,8},{3,12},{4,1},{5,5},{6,9},{7,13},{8,2},{9,6},{10,... | collective-permute-start | bytes 1179656 | tf_op jit(solution)/shard_map/ppermute | solution.py:63
  315.6 38.1 %collective-permute-start.4 = (bf16[256,768]{0,1:T(8,128)(2,1)}, bf16[256,768]{0,1:T(8,128)(2,1)}, u32[]{:S(2)}, u32[]{:S(2)}) collective-permute-start(bf16[256,768]{0,1:T(8,128)(2,1)} %get-tuple-element.108), channel_id=1, source_target_pairs={{0,0},{1,4},{2,8},{3,12},{4,1},{5,5},{6,9},{7,13},{8,2},{9,6},{10,... | collective-permute-start | bytes 1179656 | tf_op jit(solution)/shard_map/ppermute | solution.py:63
  377.6 160.7 %reduce-scatter.7.cloned.1.call-start = ((), (), s32[]{:S(2)}) async-start(), calls=%async_computation.18 | async-start | bytes 7864320 | tf_op jit(solution)/shard_map/reduce_scatter | solution.py:538
  377.8 35.5 %collective-permute-start.5 = (f32[1,256]{1,0:T(1,128)S(1)}, f32[1,256]{1,0:T(1,128)S(1)}, u32[]{:S(2)}, u32[]{:S(2)}) collective-permute-start(f32[1,256]{1,0:T(1,128)S(1)} %bitcast.185), channel_id=1, source_target_pairs={{0,0},{1,4},{2,8},{3,12},{4,1},{5,5},{6,9},{7,13},{8,2},{9,6},{10,... | collective-permute-start | bytes 3080 | tf_op jit(solution)/shard_map/ppermute | solution.py:63
  413.3 12.0 %copy-start.62 = (f32[1,256]{1,0:T(1,128)}, f32[1,256]{1,0:T(1,128)S(1)}, u32[]{:S(2)}) copy-start(f32[1,256]{1,0:T(1,128)S(1)} %collective-permute-done.5) | copy-start | bytes 3076
  425.4 247.8 %reduce-scatter.9.cloned.1.call-start = ((), (), s32[]{:S(2)}) async-start(), calls=%async_computation.19 | async-start | bytes 17694720 | tf_op jit(solution)/shard_map/reduce_scatter | solution.py:577
  470.6 19.6 %copy-start.3 = (f32[768,256]{1,0:T(8,128)S(1)}, f32[768,256]{1,0:T(8,128)}, u32[]{:S(2)}) copy-start(f32[768,256]{1,0:T(8,128)} %copy-done.2) | copy-start | bytes 2359300
  470.6 19.6 %copy-start.37 = (bf16[768,768]{1,0:T(8,128)(2,1)S(1)}, bf16[768,768]{1,0:T(8,128)(2,1)}, u32[]{:S(2)}) copy-start(bf16[768,768]{1,0:T(8,128)(2,1)} %get-tuple-element.94) | copy-start | bytes 3538948
  470.6 19.6 %copy-start.52 = (f32[256]{0:T(256)S(1)}, f32[256]{0:T(256)}, u32[]{:S(2)}) copy-start(f32[256]{0:T(256)} %copy-done.51) | copy-start | bytes 3076
  501.0 4.3 copy-start.26
  510.2 28.1 %copy-start.30 = (bf16[4,384,256]{2,1,0:T(8,128)(2,1)S(1)}, bf16[4,384,256]{2,1,0:T(8,128)(2,1)}, u32[]{:S(2)}) copy-start(bf16[4,384,256]{2,1,0:T(8,128)(2,1)} %copy-done.29) | copy-start | bytes 2359300
  540.8 34.7 %collective-permute-start.6 = (bf16[256,768]{1,0:T(8,128)(2,1)S(1)}, bf16[256,768]{1,0:T(8,128)(2,1)S(1)}, u32[]{:S(2)}, u32[]{:S(2)}) collective-permute-start(bf16[256,768]{1,0:T(8,128)(2,1)S(1)} %convolution_convert_fusion.12), channel_id=1, source_target_pairs={{0,0},{1,4},{2,8},{3,12},{4,1},{5,5},{6,9},{7,13},{8,2},{9,6},{10,... | collective-permute-start | bytes 1179656 | tf_op jit(solution)/shard_map/ppermute | solution.py:63
  575.6 4.8 copy-start.61
  575.6 4.8 copy-start.60
  575.6 33.9 %copy-start.50 = (f32[256]{0:T(256)S(1)}, f32[256]{0:T(256)}, u32[]{:S(2)}) copy-start(f32[256]{0:T(256)} %copy-done.49) | copy-start | bytes 3076
  576.5 33.0 %all-to-all-start.7 = ((bf16[4,576,256]{2,1,0:T(8,128)(2,1)}), bf16[4,576,256]{2,1,0:T(8,128)(2,1)S(1)}, u32[]{:S(2)}, u32[]{:S(2)}) async-start(bf16[4,576,256]{2,1,0:T(8,128)(2,1)} %shard_map.372), calls=%async_computation.8 | async-start | bytes 2359296 | tf_op jit(solution)/shard_map/all_to_all | solution.py:52
  580.4 145.2 %reduce-scatter.11.cloned.1.call-start = ((), (), s32[]{:S(2)}) async-start(), calls=%async_computation.20 | async-start | bytes 4202496 | tf_op jit(solution)/shard_map/reduce_scatter | solution.py:600
  613.0 14.0 %collective-permute-start.7 = (bf16[256,768]{0,1:T(8,128)(2,1)S(1)}, bf16[256,768]{0,1:T(8,128)(2,1)S(1)}, u32[]{:S(2)}, u32[]{:S(2)}) collective-permute-start(bf16[256,768]{0,1:T(8,128)(2,1)S(1)} %fusion.42), channel_id=1, source_target_pairs={{0,0},{1,4},{2,8},{3,12},{4,1},{5,5},{6,9},{7,13},{8,2},{9,6},{10,... | collective-permute-start | bytes 1179656 | tf_op jit(solution)/shard_map/ppermute | solution.py:63
  676.6 51.1 %all-to-all-start.9 = ((bf16[4,96,2560]{2,1,0:T(8,128)(2,1)}), bf16[4,96,2560]{2,1,0:T(8,128)(2,1)S(1)}, u32[]{:S(2)}, u32[]{:S(2)}) async-start(bf16[4,96,2560]{2,1,0:T(8,128)(2,1)} %shard_map.375), calls=%async_computation.13 | async-start | bytes 3932160 | tf_op jit(solution)/shard_map/all_to_all | solution.py:52
  727.7 8.6 %copy-start.4 = (bf16[4,96,2560]{2,1,0:T(8,128)(2,1)}, bf16[4,96,2560]{2,1,0:T(8,128)(2,1)S(1)}, u32[]{:S(2)}) copy-start(bf16[4,96,2560]{2,1,0:T(8,128)(2,1)S(1)} %all-to-all-done.9.terms_ref) | copy-start | bytes 5898244
  727.7 17.6 %all-to-all-start.8 = ((bf16[4,96,704]{2,1,0:T(8,128)(2,1)}), bf16[4,96,704]{2,1,0:T(8,128)(2,1)S(1)}, u32[]{:S(2)}, u32[]{:S(2)}) async-start(bf16[4,96,704]{2,1,0:T(8,128)(2,1)} %shard_map.373), calls=%async_computation.12 | async-start | bytes 1179648 | tf_op jit(solution)/shard_map/all_to_all | solution.py:52
  736.2 13.2 %copy-start.63 = (f32[1,256]{1,0:T(1,128)S(1)}, f32[1,256]{1,0:T(1,128)}, u32[]{:S(2)}) copy-start(f32[1,256]{1,0:T(1,128)} %copy-done.62) | copy-start | bytes 3076
  (42 other events, 80.4 us)
Sparse Core Ops, SparseCore 0:
  12.9 150.2 all-gather.7
  164.8 111.7 all-gather.9
  279.0 33.3 all-gather.11
  377.7 47.6 reduce-scatter.4
  427.5 110.7 reduce-scatter.6
  541.7 131.5 reduce-scatter.8
  676.7 48.8 reduce-scatter.10

commit v5 on v4

--- a/solution.py
+++ b/solution.py
@@ -493,7 +493,9 @@
     block_output = after_feed.T.astype(low)
     normed_exit = contract(order_low, norm_columns(after_feed, gain_exit).astype(low), 1, 1)
     normed_exit = rows_first(normed_exit.astype(low))
-    normed_exit, table = lax.optimization_barrier((normed_exit, table))
+    normed_exit, table, cotangent, block_output = lax.optimization_barrier(
+        (normed_exit, table, out_cotangent, block_output)
+    )
 
     tokens = lax.all_gather(normed_exit, dp, axis=0, tiled=True)
     flag_rows = marks[:, 0].reshape(-1, 1).astype(jnp.float32)
@@ -502,14 +504,11 @@
     hits = hits & (target_rows < vocab_rows)
     target_terms = contract(hits.astype(low), table, 1, 1).astype(low)
     tokens, target_terms = lax.optimization_barrier((tokens, target_terms))
-    tokens, cotangent, block_output = lax.optimization_barrier(
-        (tokens, out_cotangent, block_output)
-    )
     cotangent = relocate(cotangent.reshape(-1, width).astype(low))
     block_output = relocate(block_output)
+    tokens, cotangent, block_output = lax.optimization_barrier((tokens, cotangent, block_output))
     counts = jnp.sum(marks[:, 0], axis=1)
     shifted, products, parts = exit_rows(counts, tokens, target_terms, table, vocab_rows)
-    parts, cotangent, block_output = lax.optimization_barrier((parts, cotangent, block_output))
     block_output = block_output.reshape(hidden_in.shape)
     row_max = parts[:, 0]
     parts = lax.all_gather(parts[:, :3].T, dp, axis=0)

time: 772 us -> 776 us (level)
  transfers between devices with their start and end apart: 19 -> 19, of which waited for: 11 -> 11; matrix products, arithmetic and copies ran while one was open for 16% -> 16% of each run, Pallas kernels for 16% -> 12%
where the time goes in v5:
time: 776 us; the launch traced here: 762 us
  waiting for transfers between devices  321 us (41%)
  Pallas kernels  131 us (17%)
  blocking collectives  100 us (13%)
  matrix products  93.4 us (12%)
  starting transfers between devices  40.2 us (5%)
  local copies, waits for them, and re-layouts  34.4 us (4%)
  other arithmetic  25.3 us (3%)
  between operations  16.2 us (2%)
    all_gather x1, waiting for transfers between devices, per_device(): lax.all_gather(flat, ('seq',) + dp, axis=0, tiled=True)  122 us
    dot_general x34, matrix products, contract(): lax.dot_general(first_op, second_op, (((first_dim,), (second_dim,)), ((),...  93.4 us
    all_to_all x6, blocking collectives, swap(): return lax.all_to_all(pieces, axis, 0, 0, tiled=True)  75.7 us
    reduce_scatter x1, waiting for transfers between devices, per_device(): lax.psum_scatter(rest_terms, dp, scatter_dimension=0, tiled=True)  46 us
    all_to_all x4, waiting for transfers between devices, swap(): return lax.all_to_all(pieces, axis, 0, 0, tiled=True)  42.2 us
    reduce_scatter x1, waiting for transfers between devices, per_device(): lax.psum_scatter(self_terms, dp, scatter_dimension=0, tiled=True)  41.9 us
    pallas_call x2, Pallas kernels, attend_back(): pl.pallas_call(functools.partial(attend_back_kernel, places=places, spots...  38.4 us
    pallas_call x1, Pallas kernels, exit_rows(): pl.pallas_call(functools.partial(exit_kernel, rows=rows), grid=(count //...  37.7 us
  transfers between devices with their start and end apart: 19, of which 11 were waited for; matrix products, arithmetic and copies ran while one was open for 16% of the time, Pallas kernels for 12%

profile of v5, /device:TPU:8, one launch (start us, length us, event | category | flops | bytes accessed | tf_op | source)
XLA Modules:
  0.0 761.6 jit_solution(1576238634702216124)
XLA Ops:
  15.7 3.6 collective-permute-start.1
  23.3 12.7 %all-gather.2 = s32[8,2,256]{2,1,0:T(2,128)} all-gather(s32[1,2,256]{2,1,0:T(2,128)S(1)} %bitcast.183), channel_id=2, replica_groups=mesh['group'=2,'part'=4,'seq'=4] {'group','part'}, dimensions={0}, use_global_device_ids=true | all-gather | bytes 18432 | tf_op jit(solution)/shard_map/all_gather | solution.py:433
  35.9 4.6 collective-permute-done.2
  41.3 121.9 %all-gather.8.cloned.1.call-done = bf16[3072,3200]{1,0:T(8,128)(2,1)} async-done(((bf16[96,3200]{1,0:T(8,128)(2,1)}), bf16[3072,3200]{1,0:T(8,128)(2,1)}) %all-gather.8.cloned.1.call-update) | async-done | bytes 19660816 | tf_op jit(solution)/shard_map/all_gather | solution.py:413
  163.2 7.3 shard_map.366
  172.3 2.9 convolution_convert_fusion.5
  178.3 3.6 all-to-all-start
  183.1 13.3 %shard_map.367 = (bf16[768,768]{1,0:T(8,128)(2,1)}, bf16[768,768]{1,0:T(8,128)(2,1)}, bf16[768,768]{1,0:T(8,128)(2,1)}, bf16[768,2048]{1,0:T(8,128)(2,1)}, bf16[...) custom-call(bf16[4,768,3200]{2,1,0:T(8,128)(2,1)} %bitcast.141), custom_call_target="tpu_custom_call" | custom-call | tf_op jit(solution)/shard_map/pallas_call | solution.py:101
  196.4 9.7 %all-to-all-done.refs_0_.refs_1_ = bf16[4,960,256]{2,1,0:T(8,128)(2,1)S(1)} async-done(((bf16[4,960,256]{2,1,0:T(8,128)(2,1)}), bf16[4,960,256]{2,1,0:T(8,128)(2,1)S(1)}, u32[]{:S(2)}, u32[]{:S(2)}) %all-to-all-start) | async-done | bytes 1966112 | tf_op jit(solution)/shard_map/all_to_all | solution.py:52
  207.4 11.5 %shard_map.368 = bf16[4,192,256]{2,1,0:T(8,128)(2,1)} custom-call(s32[1]{0:T(128)} %bitcast.17.prefix_ref, bf16[4,960,256]{2,1,0:T(8,128)(2,1)} %copy-done), custom_call_target="tpu_custom_call" | custom-call | tf_op jit(solution)/shard_map/pallas_call | solution.py:322
  218.9 11.0 %all_to_all.50 = bf16[4,192,256]{2,1,0:T(8,128)(2,1)S(1)} all-to-all(bf16[4,192,256]{2,1,0:T(8,128)(2,1)} %shard_map.368), channel_id=1, replica_groups=mesh['group'=2,'part'=4,'seq'=4] {'part'}, dimensions={0} | all-to-all | bytes 786432 | tf_op jit(solution)/shard_map/all_to_all | solution.py:52
  233.2 10.6 %all_to_all.51.refs_0_ = bf16[4,192,256]{2,1,0:T(8,128)(2,1)} all-to-all(bf16[4,192,256]{2,1,0:T(8,128)(2,1)S(1)} %bitcast.173), channel_id=1, replica_groups=mesh['group'=2,'part'=4,'seq'=4] {'part'}, dimensions={0} | all-to-all | bytes 786432 | tf_op jit(solution)/shard_map/all_to_all | solution.py:52
  243.8 11.2 %shard_map.369 = bf16[4,192,256]{2,1,0:T(8,128)(2,1)} custom-call(s32[1]{0:T(128)} %bitcast.17.prefix_ref, bf16[4,192,256]{2,1,0:T(8,128)(2,1)} %all_to_all.51.refs_0_, bf16[4,960,256]{2,1,0:T(8,128)(2,1)} %copy-done), custom_call_target="tpu_custom_call" | custom-call | tf_op jit(solution)/shard_map/pallas_call | solution.py:322
  255.0 11.0 %all_to_all.52 = bf16[4,192,256]{2,1,0:T(8,128)(2,1)S(1)} all-to-all(bf16[4,192,256]{2,1,0:T(8,128)(2,1)} %shard_map.369), channel_id=1, replica_groups=mesh['group'=2,'part'=4,'seq'=4] {'part'}, dimensions={0} | all-to-all | bytes 786432 | tf_op jit(solution)/shard_map/all_to_all | solution.py:52
  269.9 2.7 multiply_convert_fusion
  281.9 3.0 collective-permute-start.3
  284.9 2.8 collective-permute-start.4
  287.6 19.8 %fusion.20.target_ref = bf16[2048,768]{1,0:T(8,128)(2,1)} fusion(bf16[768,4096]{1,0:T(8,128)(2,1)} %all-gather.10.cloned.1.call-done.table_ref, s32[2048]{0:T(1024)S(1)} %bitcast.181, pred[2048]{0:T(1024)(128)(4,1)S(1)} %broadcast_compare_fusion), kind=kOutput, calls=%fused_computation.25 | convolution fusion | flops 12903251968 | bytes 9447424 | tf_op jit(solution)/shard_map/dot_general | solution.py:22
  307.5 12.8 %all-gather.12.cloned.1.call-done.token_ref = bf16[2048,768]{1,0:T(8,128)(2,1)} async-done(((bf16[256,768]{1,0:T(8,128)(2,1)}), bf16[2048,768]{1,0:T(8,128)(2,1)}) %all-gather.12.cloned.1.call-update) | async-done | bytes 3145744 | tf_op jit(solution)/shard_map/all_gather | solution.py:500
  320.2 37.7 %shard_map.370 = (bf16[2048,4096]{1,0:T(8,128)(2,1)}, f32[2048,768]{1,0:T(8,128)}, f32[2048,128]{1,0:T(8,128)}) custom-call(s32[8]{0:T(128)} %get-tuple-element.293.count_ref, bf16[2048,768]{1,0:T(8,128)(2,1)} %all-gather.12.cloned.1.call-done.token_ref, bf16[2048,768]{1,0:T(8,128)(2,1)} %fusion.20.target_ref, ...), custom_call_target="tpu_custom_call" | custom-call | tf_op jit(solution)/shard_map/pallas_call | solution.py:298
  361.8 11.7 %all-gather.3 = f32[8,3,2048]{2,1,0:T(4,128)S(1)} all-gather(f32[1,3,2048]{2,1,0:T(4,128)S(1)} %copy.163), channel_id=3, replica_groups=mesh['group'=2,'part'=4,'seq'=4] {'group','part'}, dimensions={0}, use_global_device_ids=true | all-gather | bytes 221184 | tf_op jit(solution)/shard_map/all_gather | solution.py:514
  377.6 4.5 subtract_convert_fusion
  382.4 2.4 collective-permute-start.5
  384.8 27.7 %fusion.13 = bf16[768,4096]{1,0:T(8,128)(2,1)} fusion(bf16[2048,768]{1,0:T(8,128)(2,1)} %all-gather.12.cloned.1.call-done.token_ref, bf16[2048,4096]{1,0:T(8,128)(2,1)} %get-tuple-element.110, f32[2048]{0:T(1024)S(1)} %bitcast.178, f32[2048]{0:T(1024)S(1)} %multiply_reduce_fusion, s32[2048]{0:T(1024)S(1)} %bitcast.182, ...), kind=kOutput, calls=%fused_computation.14 | convolution fusion | flops 12946767872 | bytes 26241024 | tf_op jit(solution)/shard_map/dot_general | solution.py:22
  412.5 16.9 %reduce-scatter.5.cloned.1.call-done = bf16[256,768]{1,0:T(8,128)(2,1)} async-done(((bf16[2048,768]{1,0:T(8,128)(2,1)}), bf16[256,768]{1,0:T(8,128)(2,1)}) %reduce-scatter.5.cloned.1.call-update) | async-done | bytes 393232 | tf_op jit(solution)/shard_map/reduce_scatter | solution.py:524
  445.3 10.7 %all_to_all.53.refs_2_ = bf16[4,192,256]{2,1,0:T(8,128)(2,1)} all-to-all(bf16[4,192,256]{2,1,0:T(8,128)(2,1)S(1)} %bitcast.164), channel_id=1, replica_groups=mesh['group'=2,'part'=4,'seq'=4] {'part'}, dimensions={0} | all-to-all | bytes 786432 | tf_op jit(solution)/shard_map/all_to_all | solution.py:52
  456.0 18.6 %shard_map.371 = bf16[4,576,256]{2,1,0:T(8,128)(2,1)} custom-call(s32[1]{0:T(128)} %bitcast.17.prefix_ref, bf16[4,192,256]{2,1,0:T(8,128)(2,1)} %all_to_all.51.refs_0_, bf16[4,960,256]{2,1,0:T(8,128)(2,1)} %copy-done, bf16[4,192,256]{2,1,0:T(8,128)(2,1)} %all_to_all.53.refs_2_), custom_call_target="tpu_custom_call" | custom-call | tf_op jit(solution)/shard_map/pallas_call | solution.py:334
  474.6 19.5 %all_to_all.54 = bf16[4,576,256]{2,1,0:T(8,128)(2,1)S(1)} all-to-all(bf16[4,576,256]{2,1,0:T(8,128)(2,1)} %shard_map.371), channel_id=1, replica_groups=mesh['group'=2,'part'=4,'seq'=4] {'part'}, dimensions={0} | all-to-all | bytes 2359296 | tf_op jit(solution)/shard_map/all_to_all | solution.py:52
  496.4 2.3 fusion.19
  502.3 2.7 fusion.18
  505.0 2.7 fusion.17
  514.2 28.1 %reduce-scatter.7.cloned.1.call-done = bf16[192,4096]{1,0:T(8,128)(2,1)} async-done(((bf16[768,4096]{1,0:T(8,128)(2,1)}), bf16[192,4096]{1,0:T(8,128)(2,1)}) %reduce-scatter.7.cloned.1.call-update) | async-done | bytes 1572880 | tf_op jit(solution)/shard_map/reduce_scatter | solution.py:537
  542.3 2.5 convolution_convert_fusion.12
  546.8 13.0 %all_to_all.55.refs_1_ = bf16[4,192,256]{2,1,0:T(8,128)(2,1)} all-to-all(bf16[4,192,256]{2,1,0:T(8,128)(2,1)S(1)} %bitcast.161), channel_id=1, replica_groups=mesh['group'=2,'part'=4,'seq'=4] {'part'}, dimensions={0} | all-to-all | bytes 786432 | tf_op jit(solution)/shard_map/all_to_all | solution.py:52
  559.8 19.8 %shard_map.372 = bf16[4,576,256]{2,1,0:T(8,128)(2,1)} custom-call(s32[1]{0:T(128)} %bitcast.17.prefix_ref, bf16[4,960,256]{2,1,0:T(8,128)(2,1)} %copy-done, bf16[4,192,256]{2,1,0:T(8,128)(2,1)} %all_to_all.55.refs_1_), custom_call_target="tpu_custom_call" | custom-call | tf_op jit(solution)/shard_map/pallas_call | solution.py:334
  580.5 3.8 all-to-all-start.7
  584.4 29.1 %all-to-all-done.7 = bf16[4,576,256]{2,1,0:T(8,128)(2,1)S(1)} async-done(((bf16[4,576,256]{2,1,0:T(8,128)(2,1)}), bf16[4,576,256]{2,1,0:T(8,128)(2,1)S(1)}, u32[]{:S(2)}, u32[]{:S(2)}) %all-to-all-start.7) | async-done | bytes 1179680 | tf_op jit(solution)/shard_map/all_to_all | solution.py:52
  613.5 3.2 multiply_reduce_fusion.1
  617.0 4.7 collective-permute-start.7
  625.1 6.4 collective-permute-done.7
  631.5 46.0 %reduce-scatter.9.cloned.1.call-done.refs_0_ = bf16[96,10240]{1,0:T(8,128)(2,1)} async-done(((bf16[768,10240]{1,0:T(8,128)(2,1)}), bf16[96,10240]{1,0:T(8,128)(2,1)}) %reduce-scatter.9.cloned.1.call-update) | async-done | bytes 1966096 | tf_op jit(solution)/shard_map/reduce_scatter | solution.py:576
  677.5 3.3 shard_map.375
  680.9 5.1 all-to-all-start.9
  688.0 41.9 %reduce-scatter.11.cloned.1.call-done.refs_0_ = bf16[96,2432]{1,0:T(8,128)(2,1)} async-done(((bf16[768,2432]{1,0:T(8,128)(2,1)}), bf16[96,2432]{1,0:T(8,128)(2,1)}) %reduce-scatter.11.cloned.1.call-update) | async-done | bytes 466960 | tf_op jit(solution)/shard_map/reduce_scatter | solution.py:599
  731.9 5.2 all-to-all-start.8
  737.1 3.4 convert_bitcast_fusion
  741.7 2.7 shard_map.376
  746.1 3.4 all-to-all-done.8.terms_ref
  (265 shorter events, 90.7 us)
Async XLA Ops:
  7.2 6.4 copy-start.65
  7.2 6.4 copy-start.64
  7.2 8.3 %copy-start.41 = (bf16[1,256,768]{2,1,0:T(8,128)(2,1)S(1)}, bf16[1,256,768]{2,1,0:T(8,128)(2,1)}, u32[]{:S(2)}) copy-start(bf16[1,256,768]{2,1,0:T(8,128)(2,1)} %param.22) | copy-start | bytes 1179652
  7.2 12.2 %copy-start.42 = (bf16[1,256,768]{2,1,0:T(8,128)(2,1)S(1)}, bf16[1,256,768]{2,1,0:T(8,128)(2,1)}, u32[]{:S(2)}) copy-start(bf16[1,256,768]{2,1,0:T(8,128)(2,1)} %param.23) | copy-start | bytes 1179652
  7.2 14.3 %copy-start.35 = (bf16[4016,192]{0,1:T(8,128)(2,1)S(1)}, bf16[4016,192]{0,1:T(8,128)(2,1)}, u32[]{:S(2)}) copy-start(bf16[4016,192]{0,1:T(8,128)(2,1)} %param.43) | copy-start | bytes 4626436
  7.2 156.0 %all-gather.8.cloned.1.call-start = ((), (), s32[]{:S(2)}) async-start(), calls=%async_computation.14 | async-start | bytes 20275200 | tf_op jit(solution)/shard_map/all_gather | solution.py:413
  12.8 265.8 %all-gather.10.cloned.1.call-start = ((), (), s32[]{:S(2)}) async-start(), calls=%async_computation.15 | async-start | bytes 7864320 | tf_op jit(solution)/shard_map/all_gather | solution.py:437
  13.6 9.2 %collective-permute-start = (s32[3,256]{1,0:T(4,128)S(1)}, s32[3,256]{1,0:T(4,128)S(1)}, u32[]{:S(2)}, u32[]{:S(2)}) collective-permute-start(s32[3,256]{1,0:T(4,128)S(1)} %add_add_fusion.4), channel_id=1, source_target_pairs={{0,0},{1,4},{2,8},{3,12},{4,1},{5,5},{6,9},{7,13},{8,2},{9,6},{10,... | collective-permute-start | bytes 9224 | tf_op jit(solution)/shard_map/ppermute | solution.py:63
  15.7 20.2 %collective-permute-start.1 = (bf16[256,768]{0,1:T(8,128)(2,1)S(1)}, bf16[256,768]{0,1:T(8,128)(2,1)S(1)}, u32[]{:S(2)}, u32[]{:S(2)}) collective-permute-start(bf16[256,768]{0,1:T(8,128)(2,1)S(1)} %bitcast.171), channel_id=1, source_target_pairs={{0,0},{1,4},{2,8},{3,12},{4,1},{5,5},{6,9},{7,13},{8,2},{9,6},{10,... | collective-permute-start | bytes 1179656 | tf_op jit(solution)/shard_map/ppermute | solution.py:63
  19.6 20.9 %collective-permute-start.2 = (bf16[256,768]{0,1:T(8,128)(2,1)S(1)}, bf16[256,768]{0,1:T(8,128)(2,1)S(1)}, u32[]{:S(2)}, u32[]{:S(2)}) collective-permute-start(bf16[256,768]{0,1:T(8,128)(2,1)S(1)} %bitcast.172), channel_id=1, source_target_pairs={{0,0},{1,4},{2,8},{3,12},{4,1},{5,5},{6,9},{7,13},{8,2},{9,6},{10,... | collective-permute-start | bytes 1179656 | tf_op jit(solution)/shard_map/ppermute | solution.py:63
  22.8 17.7 %copy-start.60 = (s32[3,256]{1,0:T(4,128)}, s32[3,256]{1,0:T(4,128)S(1)}, u32[]{:S(2)}) copy-start(s32[3,256]{1,0:T(4,128)S(1)} %collective-permute-done) | copy-start | bytes 9220
  23.0 17.5 %copy-start.46 = (s32[256]{0:T(256)}, s32[256]{0:T(256)S(1)}, u32[]{:S(2)}) copy-start(s32[256]{0:T(256)S(1)} %convert_reduce_fusion) | copy-start | bytes 3076
  40.5 131.8 %copy-start.38 = (bf16[256,768]{0,1:T(8,128)(2,1)}, bf16[256,768]{0,1:T(8,128)(2,1)S(1)}, u32[]{:S(2)}) copy-start(bf16[256,768]{0,1:T(8,128)(2,1)S(1)} %collective-permute-done.2) | copy-start | bytes 1179652
  41.3 134.0 %copy-start.48 = (f32[256]{0:T(256)}, f32[256]{0:T(256)S(1)}, u32[]{:S(2)}) copy-start(f32[256]{0:T(256)S(1)} %fusion.57) | copy-start | bytes 3076
  172.3 3.3 copy-start.66
  178.3 27.8 %all-to-all-start = ((bf16[4,960,256]{2,1,0:T(8,128)(2,1)}), bf16[4,960,256]{2,1,0:T(8,128)(2,1)S(1)}, u32[]{:S(2)}, u32[]{:S(2)}) async-start(bf16[4,960,256]{2,1,0:T(8,128)(2,1)} %pad_maximum_fusion.2), calls=%async_computation | async-start | bytes 3932160 | tf_op jit(solution)/shard_map/all_to_all | solution.py:52
  181.9 138.3 %all-gather.12.cloned.1.call-start = ((), (), s32[]{:S(2)}) async-start(), calls=%async_computation.16 | async-start | bytes 3538944 | tf_op jit(solution)/shard_map/all_gather | solution.py:500
  218.9 13.6 %copy-start.36 = (bf16[768,768]{1,0:T(8,128)(2,1)S(1)}, bf16[768,768]{1,0:T(8,128)(2,1)}, u32[]{:S(2)}) copy-start(bf16[768,768]{1,0:T(8,128)(2,1)} %get-tuple-element.92) | copy-start | bytes 3538948
  229.9 3.2 copy-start.19
  231.8 34.1 %copy-start.2 = (f32[768,256]{1,0:T(8,128)}, f32[768,256]{1,0:T(8,128)S(1)}, u32[]{:S(2)}) copy-start(f32[768,256]{1,0:T(8,128)S(1)} %get-tuple-element.296) | copy-start | bytes 2359300
  233.1 32.8 %copy-start.11 = (bf16[768,768]{1,0:T(8,128)(2,1)S(1)}, bf16[768,768]{1,0:T(8,128)(2,1)}, u32[]{:S(2)}) copy-start(bf16[768,768]{1,0:T(8,128)(2,1)} %get-tuple-element.91) | copy-start | bytes 3538948
  266.5 174.2 %copy-start.58 = (f32[256]{0:T(256)}, f32[256]{0:T(256)S(1)}, u32[]{:S(2)}) copy-start(f32[256]{0:T(256)S(1)} %fusion.59) | copy-start | bytes 3076
  269.0 3.6 copy-start.32
  277.4 154.0 %copy-start.44 = (f32[256]{0:T(256)}, f32[256]{0:T(256)S(1)}, u32[]{:S(2)}) copy-start(f32[256]{0:T(256)S(1)} %fusion.60) | copy-start | bytes 3076
  278.6 150.7 %reduce-scatter.5.cloned.1.call-start = ((), (), s32[]{:S(2)}) async-start(), calls=%async_computation.17 | async-start | bytes 3538944 | tf_op jit(solution)/shard_map/reduce_scatter | solution.py:524
  281.9 38.3 %collective-permute-start.3 = (bf16[256,768]{0,1:T(8,128)(2,1)}, bf16[256,768]{0,1:T(8,128)(2,1)}, u32[]{:S(2)}, u32[]{:S(2)}) collective-permute-start(bf16[256,768]{0,1:T(8,128)(2,1)} %bitcast.174), channel_id=1, source_target_pairs={{0,0},{1,4},{2,8},{3,12},{4,1},{5,5},{6,9},{7,13},{8,2},{9,6},{10,... | collective-permute-start | bytes 1179656 | tf_op jit(solution)/shard_map/ppermute | solution.py:63
  284.9 35.4 %collective-permute-start.4 = (bf16[256,768]{0,1:T(8,128)(2,1)}, bf16[256,768]{0,1:T(8,128)(2,1)}, u32[]{:S(2)}, u32[]{:S(2)}) collective-permute-start(bf16[256,768]{0,1:T(8,128)(2,1)} %get-tuple-element.104), channel_id=1, source_target_pairs={{0,0},{1,4},{2,8},{3,12},{4,1},{5,5},{6,9},{7,13},{8,2},{9,6},{10,... | collective-permute-start | bytes 1179656 | tf_op jit(solution)/shard_map/ppermute | solution.py:63
  382.1 160.2 %reduce-scatter.7.cloned.1.call-start = ((), (), s32[]{:S(2)}) async-start(), calls=%async_computation.18 | async-start | bytes 7864320 | tf_op jit(solution)/shard_map/reduce_scatter | solution.py:537
  382.4 30.1 %collective-permute-start.5 = (f32[1,256]{1,0:T(1,128)S(1)}, f32[1,256]{1,0:T(1,128)S(1)}, u32[]{:S(2)}, u32[]{:S(2)}) collective-permute-start(f32[1,256]{1,0:T(1,128)S(1)} %bitcast.186), channel_id=1, source_target_pairs={{0,0},{1,4},{2,8},{3,12},{4,1},{5,5},{6,9},{7,13},{8,2},{9,6},{10,... | collective-permute-start | bytes 3080 | tf_op jit(solution)/shard_map/ppermute | solution.py:63
  412.5 16.9 %copy-start.62 = (f32[1,256]{1,0:T(1,128)}, f32[1,256]{1,0:T(1,128)S(1)}, u32[]{:S(2)}) copy-start(f32[1,256]{1,0:T(1,128)S(1)} %collective-permute-done.5) | copy-start | bytes 3076
  429.4 248.1 %reduce-scatter.9.cloned.1.call-start = ((), (), s32[]{:S(2)}) async-start(), calls=%async_computation.19 | async-start | bytes 17694720 | tf_op jit(solution)/shard_map/reduce_scatter | solution.py:576
  474.6 19.6 %copy-start.3 = (f32[768,256]{1,0:T(8,128)S(1)}, f32[768,256]{1,0:T(8,128)}, u32[]{:S(2)}) copy-start(f32[768,256]{1,0:T(8,128)} %copy-done.2) | copy-start | bytes 2359300
  474.6 19.6 %copy-start.37 = (bf16[768,768]{1,0:T(8,128)(2,1)S(1)}, bf16[768,768]{1,0:T(8,128)(2,1)}, u32[]{:S(2)}) copy-start(bf16[768,768]{1,0:T(8,128)(2,1)} %get-tuple-element.92) | copy-start | bytes 3538948
  474.6 19.6 %copy-start.51 = (f32[256]{0:T(256)S(1)}, f32[256]{0:T(256)}, u32[]{:S(2)}) copy-start(f32[256]{0:T(256)} %copy-done.50) | copy-start | bytes 3076
  505.0 4.3 copy-start.26
  514.2 28.1 %copy-start.30 = (bf16[4,384,256]{2,1,0:T(8,128)(2,1)S(1)}, bf16[4,384,256]{2,1,0:T(8,128)(2,1)}, u32[]{:S(2)}) copy-start(bf16[4,384,256]{2,1,0:T(8,128)(2,1)} %copy-done.29) | copy-start | bytes 2359300
  544.8 34.7 %collective-permute-start.6 = (bf16[256,768]{1,0:T(8,128)(2,1)S(1)}, bf16[256,768]{1,0:T(8,128)(2,1)S(1)}, u32[]{:S(2)}, u32[]{:S(2)}) collective-permute-start(bf16[256,768]{1,0:T(8,128)(2,1)S(1)} %convolution_convert_fusion.12), channel_id=1, source_target_pairs={{0,0},{1,4},{2,8},{3,12},{4,1},{5,5},{6,9},{7,13},{8,2},{9,6},{10,... | collective-permute-start | bytes 1179656 | tf_op jit(solution)/shard_map/ppermute | solution.py:63
  579.6 4.8 copy-start.61
  579.6 4.8 copy-start.59
  579.6 33.9 %copy-start.49 = (f32[256]{0:T(256)S(1)}, f32[256]{0:T(256)}, u32[]{:S(2)}) copy-start(f32[256]{0:T(256)} %copy-done.48) | copy-start | bytes 3076
  580.5 32.9 %all-to-all-start.7 = ((bf16[4,576,256]{2,1,0:T(8,128)(2,1)}), bf16[4,576,256]{2,1,0:T(8,128)(2,1)S(1)}, u32[]{:S(2)}, u32[]{:S(2)}) async-start(bf16[4,576,256]{2,1,0:T(8,128)(2,1)} %shard_map.372), calls=%async_computation.8 | async-start | bytes 2359296 | tf_op jit(solution)/shard_map/all_to_all | solution.py:52
  584.3 145.6 %reduce-scatter.11.cloned.1.call-start = ((), (), s32[]{:S(2)}) async-start(), calls=%async_computation.20 | async-start | bytes 4202496 | tf_op jit(solution)/shard_map/reduce_scatter | solution.py:599
  613.5 3.2 copy-start.53
  617.0 14.5 %collective-permute-start.7 = (bf16[256,768]{0,1:T(8,128)(2,1)S(1)}, bf16[256,768]{0,1:T(8,128)(2,1)S(1)}, u32[]{:S(2)}, u32[]{:S(2)}) collective-permute-start(bf16[256,768]{0,1:T(8,128)(2,1)S(1)} %fusion.42), channel_id=1, source_target_pairs={{0,0},{1,4},{2,8},{3,12},{4,1},{5,5},{6,9},{7,13},{8,2},{9,6},{10,... | collective-permute-start | bytes 1179656 | tf_op jit(solution)/shard_map/ppermute | solution.py:63
  680.9 51.1 %all-to-all-start.9 = ((bf16[4,96,2560]{2,1,0:T(8,128)(2,1)}), bf16[4,96,2560]{2,1,0:T(8,128)(2,1)S(1)}, u32[]{:S(2)}, u32[]{:S(2)}) async-start(bf16[4,96,2560]{2,1,0:T(8,128)(2,1)} %shard_map.375), calls=%async_computation.13 | async-start | bytes 3932160 | tf_op jit(solution)/shard_map/all_to_all | solution.py:52
  731.9 8.6 %copy-start.4 = (bf16[4,96,2560]{2,1,0:T(8,128)(2,1)}, bf16[4,96,2560]{2,1,0:T(8,128)(2,1)S(1)}, u32[]{:S(2)}) copy-start(bf16[4,96,2560]{2,1,0:T(8,128)(2,1)S(1)} %all-to-all-done.9.terms_ref) | copy-start | bytes 5898244
  731.9 17.6 %all-to-all-start.8 = ((bf16[4,96,704]{2,1,0:T(8,128)(2,1)}), bf16[4,96,704]{2,1,0:T(8,128)(2,1)S(1)}, u32[]{:S(2)}, u32[]{:S(2)}) async-start(bf16[4,96,704]{2,1,0:T(8,128)(2,1)} %shard_map.373), calls=%async_computation.12 | async-start | bytes 1179648 | tf_op jit(solution)/shard_map/all_to_all | solution.py:52
  740.5 13.2 %copy-start.63 = (f32[1,256]{1,0:T(1,128)S(1)}, f32[1,256]{1,0:T(1,128)}, u32[]{:S(2)}) copy-start(f32[1,256]{1,0:T(1,128)} %copy-done.62) | copy-start | bytes 3076
  (42 other events, 77.8 us)
Sparse Core Ops, SparseCore 0:
  12.9 150.2 all-gather.7
  164.8 111.7 all-gather.9
  279.0 41.1 all-gather.11
  382.3 47.0 reduce-scatter.4
  431.5 110.7 reduce-scatter.6
  545.7 131.7 reduce-scatter.8
  681.0 48.8 reduce-scatter.10
